TPU v7x, 256 devices: a whole 4x4x8 slice. The times are simulated.
256 devices in a mesh: row: 16 (over y_lo, x, core), col: 16 (over z, y_hi).
Axes of the slice: x: 4, y: 4 (y_hi: 2, y_lo: 2; y = y_hi * 2 + y_lo), z: 8, core: 2. Of those that a mesh axis runs over, the one named last changes fastest.
Arguments:
- counts: int32 [16, 16, 6, 8, 128, 128], P('row', 'col'), may hold values from 0 to 5
- block_coords: int32 [3, 16, 16, 6], P(None, 'row', 'col'), may hold values from 0 to 127, as said below
- block_count: int32 [16, 16], P('row', 'col'), may hold values from 1 to 6, as said below
- factor_a: float32 [32768, 128], P(('row', 'col')), may hold values from -0.6 to 0.6
- factor_b: float32 [32768, 128], P(('col', 'row')), may hold values from -0.6 to 0.6
- factor_c: float32 [1024, 128], replicated, may hold values from -0.6 to 0.6
Outputs:
- updated_a: float32 [32768, 128], P(('row', 'col'))
- updated_b: float32 [32768, 128], P(('col', 'row'))
Inputs may be any that keep to these rules, and one draw needn't show every extreme that they name: `block_coords`: the slots of one cell name distinct blocks; the first index is below 16, the second below 16, the third below 128. `block_count`: at least one cell has all 6 slots live in every draw.
All inputs are finite; a program needn't handle non-finite values.
Results may differ from a plain program's by a relative error of at most 0.0003.
Values sent between devices are 32-bit elements; how exact they have to be, the bound alone decides.
No kernel may reach another device: no remote copies, remote signals or barrier semaphores. Data moves between devices by JAX's collectives and lax.ppermute only.
A program may use at most 64 MiB of HBM per device.

v0:
```python
import jax
import jax.numpy as jnp
from jax import lax
from jax.sharding import PartitionSpec as P

STEPS = 2


step_rate = 0.004
highest = lax.Precision.HIGHEST


def block_gradient(piece_a, piece_b, piece_c, observed, valid_flag):
    depth = piece_c.shape[0]
    side = piece_a.shape[0]
    rank = piece_a.shape[1]
    scaled_a = (piece_c[:, None, :] * piece_a[None, :, :]).reshape(depth * side, rank)
    model = jnp.dot(scaled_a, piece_b.T, precision=highest, preferred_element_type=jnp.float32)
    residual = (
        jnp.exp(model) - observed.reshape(depth * side, side).astype(jnp.float32)
    ) * valid_flag
    scaled_b = piece_c[:, None, :] * piece_b[None, :, :]
    grad_a = jnp.einsum(
        "kab,kbr->ar", residual.reshape(depth, side, side), scaled_b, precision=highest
    )
    grad_b = jnp.dot(residual.T, scaled_a, precision=highest, preferred_element_type=jnp.float32)
    return (grad_a, grad_b)


def local_gradients(band_a, band_b, factor_c, counts, block_coords, block_count):
    slot_total = counts.shape[2]
    depth = counts.shape[3]
    side = counts.shape[4]
    limit = block_count[0, 0]

    def visit_slot(partial_value, slot_index):
        grad_a, grad_b = partial_value
        start_a = block_coords[0, 0, 0, slot_index] * side
        start_b = block_coords[1, 0, 0, slot_index] * side
        start_c = block_coords[2, 0, 0, slot_index] * depth
        valid_flag = (slot_index < limit).astype(jnp.float32)
        piece_a = lax.dynamic_slice_in_dim(band_a, start_a, side, 0)
        piece_b = lax.dynamic_slice_in_dim(band_b, start_b, side, 0)
        piece_c = lax.dynamic_slice_in_dim(factor_c, start_c, depth, 0)
        observed = counts[0, 0, slot_index]
        block_a, block_b = block_gradient(piece_a, piece_b, piece_c, observed, valid_flag)
        old_a = lax.dynamic_slice_in_dim(grad_a, start_a, side, 0)
        old_b = lax.dynamic_slice_in_dim(grad_b, start_b, side, 0)
        grad_a = lax.dynamic_update_slice_in_dim(grad_a, old_a + block_a, start_a, 0)
        grad_b = lax.dynamic_update_slice_in_dim(grad_b, old_b + block_b, start_b, 0)
        return ((grad_a, grad_b), None)

    start = (jnp.zeros_like(band_a), jnp.zeros_like(band_b))
    result, unused = lax.scan(visit_slot, start, jnp.arange(slot_total, dtype=jnp.int32))
    return result


def local(counts, block_coords, block_count, factor_a, factor_b, factor_c):
    for step_index in range(STEPS):
        band_a = lax.all_gather(factor_a, "col", axis=0, tiled=True)
        band_b = lax.all_gather(factor_b, "row", axis=0, tiled=True)
        grad_a, grad_b = local_gradients(
            band_a, band_b, factor_c, counts, block_coords, block_count
        )
        share_a = lax.psum_scatter(grad_a, "col", scatter_dimension=0, tiled=True)
        share_b = lax.psum_scatter(grad_b, "row", scatter_dimension=0, tiled=True)
        factor_a = factor_a - step_rate * share_a
        factor_b = factor_b - step_rate * share_b
    return (factor_a, factor_b)


def solution(mesh):
    return jax.shard_map(
        local,
        mesh=mesh,
        in_specs=(
            P("row", "col", None, None, None, None),
            P(None, "row", "col", None),
            P("row", "col"),
            P(("row", "col"), None),
            P(("col", "row"), None),
            P(),
        ),
        out_specs=(P(("row", "col"), None), P(("col", "row"), None)),
        check_vma=False,
    )
```

profile of v0, /device:TPU:1, one launch (start us, length us, event | category | flops | bytes accessed | tf_op | source)
XLA Modules:
  0.0 928.2 jit_solution(7172400108618782772)
XLA Ops:
  8.7 80.0 %all-gather.5.cloned.1.call-done = f32[2048,128]{1,0:T(8,128)} async-done(((f32[128,128]{1,0:T(8,128)}), f32[2048,128]{1,0:T(8,128)}) %all-gather.5.cloned.1.call-update) | async-done | bytes 1048592 | tf_op jit(solution)/shard_map/all_gather | solution.py:60
  88.7 37.8 %all-gather.7.cloned.1.call-done = f32[2048,128]{1,0:T(8,128)} async-done(((f32[128,128]{1,0:T(8,128)}), f32[2048,128]{1,0:T(8,128)}) %all-gather.7.cloned.1.call-update) | async-done | bytes 1048592 | tf_op jit(solution)/shard_map/all_gather | solution.py:61
  126.7 71.9 %while.24 = (s32[]{:T(128)}, f32[2048,128]{1,0:T(8,128)S(1)}, f32[2048,128]{1,0:T(8,128)S(1)}, s32[6]{0:T(128)S(1)}, s32[3,1,1,6]{3,2,1,0:T(1,128)}, /*index=5*/...) while((s32[]{:T(128)}, f32[2048,128]{1,0:T(8,128)S(1)}, ...), condition=%wide.region_1.2_spmd, body=%wide.region_0.1_spmd.sunk | while | flops 604667904 | bytes 5456283 | solution.py:54
  129.3 1.3 constant_dynamic-slice_fusion.18
  134.0 1.1 dynamic-slice_convert_fusion.4
  141.3 1.3 constant_dynamic-slice_fusion.18
  146.0 1.1 dynamic-slice_convert_fusion.4
  153.3 1.3 constant_dynamic-slice_fusion.18
  158.0 1.1 dynamic-slice_convert_fusion.4
  165.3 1.3 constant_dynamic-slice_fusion.18
  170.0 1.1 dynamic-slice_convert_fusion.4
  177.2 1.3 constant_dynamic-slice_fusion.18
  182.0 1.1 dynamic-slice_convert_fusion.4
  189.2 1.3 constant_dynamic-slice_fusion.18
  194.0 1.1 dynamic-slice_convert_fusion.4
  200.4 60.6 %reduce-scatter.7.cloned.1.call-done = f32[128,128]{1,0:T(8,128)} async-done(((f32[2048,128]{1,0:T(8,128)}), f32[128,128]{1,0:T(8,128)}) %reduce-scatter.7.cloned.1.call-update) | async-done | bytes 65552 | tf_op jit(solution)/shard_map/reduce_scatter | solution.py:66
  261.0 1.5 multiply_subtract_fusion.2
  262.5 203.1 %reduce-scatter.5.cloned.1.call-done = f32[128,128]{1,0:T(8,128)} async-done(((f32[2048,128]{1,0:T(8,128)}), f32[128,128]{1,0:T(8,128)}) %reduce-scatter.5.cloned.1.call-update) | async-done | bytes 65552 | tf_op jit(solution)/shard_map/reduce_scatter | solution.py:65
  465.7 1.5 multiply_subtract_fusion.3
  467.2 38.8 %all-gather.11.cloned.1.call-done = f32[2048,128]{1,0:T(8,128)} async-done(((f32[128,128]{1,0:T(8,128)}), f32[2048,128]{1,0:T(8,128)}) %all-gather.11.cloned.1.call-update) | async-done | bytes 1048592 | tf_op jit(solution)/shard_map/all_gather | solution.py:61
  506.1 76.9 %all-gather.9.cloned.1.call-done = f32[2048,128]{1,0:T(8,128)} async-done(((f32[128,128]{1,0:T(8,128)}), f32[2048,128]{1,0:T(8,128)}) %all-gather.9.cloned.1.call-update) | async-done | bytes 1048592 | tf_op jit(solution)/shard_map/all_gather | solution.py:60
  583.2 68.0 %while.25 = (s32[]{:T(128)}, f32[2048,128]{1,0:T(8,128)S(1)}, f32[2048,128]{1,0:T(8,128)S(1)}, s32[6]{0:T(128)S(1)}, s32[3,1,1,6]{3,2,1,0:T(1,128)S(1)}, /*index...) while((s32[]{:T(128)}, f32[2048,128]{1,0:T(8,128)S(1)}, ...), condition=%wide.region_5.6_spmd, body=%wide.region_4.5_spmd.sunk | while | flops 604667904 | bytes 5456283 | solution.py:54
  589.9 1.1 dynamic-slice_convert_fusion.5
  601.2 1.1 dynamic-slice_convert_fusion.5
  612.5 1.1 dynamic-slice_convert_fusion.5
  623.9 1.1 dynamic-slice_convert_fusion.5
  635.2 1.1 dynamic-slice_convert_fusion.5
  646.5 1.1 dynamic-slice_convert_fusion.5
  652.9 61.8 %reduce-scatter.11.cloned.1.call-done = f32[128,128]{1,0:T(8,128)} async-done(((f32[2048,128]{1,0:T(8,128)}), f32[128,128]{1,0:T(8,128)}) %reduce-scatter.11.cloned.1.call-update) | async-done | bytes 65552 | tf_op jit(solution)/shard_map/reduce_scatter | solution.py:66
  714.7 1.5 multiply_subtract_fusion
  716.2 203.7 %reduce-scatter.9.cloned.1.call-done = f32[128,128]{1,0:T(8,128)} async-done(((f32[2048,128]{1,0:T(8,128)}), f32[128,128]{1,0:T(8,128)}) %reduce-scatter.9.cloned.1.call-update) | async-done | bytes 65552 | tf_op jit(solution)/shard_map/reduce_scatter | solution.py:65
  919.9 1.5 multiply_subtract_fusion.1
  (130 shorter events, 63.3 us)
Async XLA Ops:
  7.2 81.6 %all-gather.5.cloned.1.call-start = ((), (), s32[]{:S(2)}) async-start(), calls=%async_computation.4 | async-start | bytes 1114112 | tf_op jit(solution)/shard_map/all_gather | solution.py:60
  7.9 118.7 %all-gather.7.cloned.1.call-start = ((), (), s32[]{:S(2)}) async-start(), calls=%async_computation.5 | async-start | bytes 1114112 | tf_op jit(solution)/shard_map/all_gather | solution.py:61
  8.6 252.3 %reduce-scatter.7.cloned.1.call-start = ((), (), s32[]{:S(2)}) async-start(), calls=%async_computation.8 | async-start | bytes 1114112 | tf_op jit(solution)/shard_map/reduce_scatter | solution.py:66
  126.7 134.3 %copy-start.6 = (f32[128,128]{1,0:T(8,128)S(1)}, f32[128,128]{1,0:T(8,128)}, u32[]{:S(2)}) copy-start(f32[128,128]{1,0:T(8,128)} %param.14) | copy-start | bytes 196612
  126.7 338.9 %copy-start.7 = (f32[128,128]{1,0:T(8,128)S(1)}, f32[128,128]{1,0:T(8,128)}, u32[]{:S(2)}) copy-start(f32[128,128]{1,0:T(8,128)} %param.13) | copy-start | bytes 196612
  198.7 1.0 copy-start.3
  198.7 1.3 copy-start.2
  198.7 384.4 %copy-start.8 = (s32[3,1,1,6]{3,2,1,0:T(1,128)S(1)}, s32[3,1,1,6]{3,2,1,0:T(1,128)}, u32[]{:S(2)}) copy-start(s32[3,1,1,6]{3,2,1,0:T(1,128)} %get-tuple-element.431) | copy-start | bytes 220
  199.7 265.9 %reduce-scatter.5.cloned.1.call-start = ((), (), s32[]{:S(2)}) async-start(), calls=%async_computation.6 | async-start | bytes 1114112 | tf_op jit(solution)/shard_map/reduce_scatter | solution.py:65
  200.3 305.8 %all-gather.11.cloned.1.call-start = ((), (), s32[]{:S(2)}) async-start(), calls=%async_computation.9 | async-start | bytes 1114112 | tf_op jit(solution)/shard_map/all_gather | solution.py:61
  262.5 320.5 %all-gather.9.cloned.1.call-start = ((), (), s32[]{:S(2)}) async-start(), calls=%async_computation.7 | async-start | bytes 1114112 | tf_op jit(solution)/shard_map/all_gather | solution.py:60
  467.2 247.6 %reduce-scatter.11.cloned.1.call-start = ((), (), s32[]{:S(2)}) async-start(), calls=%async_computation.11 | async-start | bytes 1114112 | tf_op jit(solution)/shard_map/reduce_scatter | solution.py:66
  583.2 131.6 %copy-start.4 = (f32[128,128]{1,0:T(8,128)S(1)}, f32[128,128]{1,0:T(8,128)}, u32[]{:S(2)}) copy-start(f32[128,128]{1,0:T(8,128)} %multiply_subtract_fusion.2) | copy-start | bytes 196612
  583.2 336.7 %copy-start.5 = (f32[128,128]{1,0:T(8,128)S(1)}, f32[128,128]{1,0:T(8,128)}, u32[]{:S(2)}) copy-start(f32[128,128]{1,0:T(8,128)} %multiply_subtract_fusion.3) | copy-start | bytes 196612
  651.2 0.9 copy-start.1
  651.2 1.3 copy-start
  652.2 267.7 %reduce-scatter.9.cloned.1.call-start = ((), (), s32[]{:S(2)}) async-start(), calls=%async_computation.10 | async-start | bytes 1114112 | tf_op jit(solution)/shard_map/reduce_scatter | solution.py:65
Sparse Core Ops, SparseCore 0:
  10.6 78.1 all-gather.4
  90.6 35.9 all-gather.6
  199.9 61.0 reduce-scatter.6
  264.7 200.9 reduce-scatter.4
  467.9 38.0 all-gather.10
  509.1 73.8 all-gather.8
  652.3 62.3 reduce-scatter.10
  718.5 201.3 reduce-scatter.8
where the time goes:
time: 935 us; the launch traced here: 928 us
  waiting for transfers between devices  765 us (82%)
  loops' own time  61 us (7%)
  local copies, waits for them, and re-layouts  40.9 us (4%)
  matrix products  27.4 us (3%)
  other arithmetic  19.4 us (2%)
  between operations  14.3 us (2%)
    reduce_scatter x2, waiting for transfers between devices, local(): share_a = lax.psum_scatter(grad_a, 'col', scatter_dimension=0, tiled=True)  407 us
    all_gather x2, waiting for transfers between devices, local(): band_a = lax.all_gather(factor_a, 'col', axis=0, tiled=True)  157 us
    reduce_scatter x2, waiting for transfers between devices, local(): share_b = lax.psum_scatter(grad_b, 'row', scatter_dimension=0, tiled=True)  122 us
    all_gather x2, waiting for transfers between devices, local(): band_b = lax.all_gather(factor_b, 'row', axis=0, tiled=True)  76.7 us
    another operation x2, loops' own time, local_gradients(): lax.scan(visit_slot, start, jnp.arange(slot_total, dtype=jnp.int32))  61 us
  transfers between devices with their start and end apart: 8, of which 8 were waited for; matrix products, arithmetic and copies ran while one was open for 0% of the time, Pallas kernels for 0%

commit v1 on v0

v1 whole, which is shorter than its diff:
```python
import functools

import jax
import jax.numpy as jnp
from jax import lax
from jax.experimental import pallas as pl
from jax.experimental.pallas import tpu as pltpu
from jax.sharding import PartitionSpec as P

STEPS = 2
step_rate = 0.004


def split(value):
    high = value.astype(jnp.bfloat16)
    low = (value - high.astype(jnp.float32)).astype(jnp.bfloat16)
    return high, low


def two_halves(value):
    high, low = split(value)
    return jnp.concatenate([high, low], axis=1)


def pair_table(value):
    high, low = split(value)
    row = jnp.concatenate([high, low], axis=1)
    return jnp.concatenate([row, row], axis=0)


def fold(product):
    return product[:, :128] + product[:, 128:]


def gradient_kernel(where_ref, live_ref, a_ref, b_ref, c_ref, counts_ref, ga_ref, gb_ref, seen, sems):
    slots, depth, side, rank = counts_ref.shape
    pieces = a_ref.shape[0]
    live = live_ref[0]

    def fetch(slot):
        return pltpu.make_async_copy(counts_ref.at[slot], seen.at[slot], sems.at[slot])

    for slot in range(slots):

        @pl.when(slot < live)
        def _():
            fetch(slot).start()

    def visit(slot, carry):
        start_c = pl.multiple_of(where_ref[2 * slots + slot] * depth, depth)
        piece_a = a_ref[:, slot].reshape(side, rank)
        piece_b = b_ref[:, slot].reshape(side, rank)
        piece_c = c_ref[pl.ds(start_c, depth), :]
        scaled_a = (piece_c[:, None, :] * piece_a[None, :, :]).reshape(depth * side, rank)
        b_high, b_low = split(piece_b)
        b_rows = jnp.concatenate(
            [jnp.concatenate([b_high, b_high], axis=1), jnp.concatenate([b_low, b_low], axis=1)], axis=0
        )
        model = fold(
            lax.dot_general(
                two_halves(scaled_a), b_rows, (((1,), (1,)), ((), ())), preferred_element_type=jnp.float32
            )
        )
        fetch(slot).wait()
        observed = seen[slot].reshape(depth * side, side)
        residual = jnp.exp(model) - observed.astype(jnp.float32)
        along_b = fold(jnp.dot(two_halves(residual), pair_table(piece_b), preferred_element_type=jnp.float32))
        turned = jnp.swapaxes(residual.reshape(depth, side, side), 1, 2).reshape(depth * side, side)
        along_a = fold(jnp.dot(two_halves(turned), pair_table(piece_a), preferred_element_type=jnp.float32))
        grad_a = (along_b.reshape(depth, side, rank) * piece_c[:, None, :]).sum(0)
        grad_b = (along_a.reshape(depth, side, rank) * piece_c[:, None, :]).sum(0)
        ga_ref[:, slot] = grad_a.reshape(pieces, side // pieces, rank)
        gb_ref[:, slot] = grad_b.reshape(pieces, side // pieces, rank)
        return carry

    lax.fori_loop(0, live, visit, 0)

    def clear(slot, carry):
        ga_ref[:, slot] = jnp.zeros((pieces, side // pieces, rank), jnp.float32)
        gb_ref[:, slot] = jnp.zeros((pieces, side // pieces, rank), jnp.float32)
        return carry

    lax.fori_loop(live, slots, clear, 0)


def block_gradients(where, live, a, b, c, counts):
    slots = counts.shape[0]
    vmem = pl.BlockSpec(memory_space=pltpu.VMEM)
    smem = pl.BlockSpec(memory_space=pltpu.SMEM)
    return pl.pallas_call(
        gradient_kernel,
        out_shape=(jax.ShapeDtypeStruct(a.shape, jnp.float32), jax.ShapeDtypeStruct(b.shape, jnp.float32)),
        in_specs=[smem, smem, vmem, vmem, vmem, pl.BlockSpec(memory_space=pl.ANY)],
        out_specs=(vmem, vmem),
        scratch_shapes=[pltpu.VMEM(counts.shape, jnp.int32), pltpu.SemaphoreType.DMA((slots,))],
        cost_estimate=pl.CostEstimate(flops=1 << 30, bytes_accessed=6 << 20, transcendentals=1 << 20),
    )(where, live, a, b, c, counts)


def deal_kernel(wanted_ref, piece_ref, out_ref):
    members, slots = out_ref.shape[:2]
    for member in range(members):
        for slot in range(slots):
            block = jnp.minimum(wanted_ref[member * slots + slot], members - 1)
            out_ref[member, slot] = piece_ref[block]


def deal(wanted, pieces, slots):
    members, rows, rank = pieces.shape
    vmem = pl.BlockSpec(memory_space=pltpu.VMEM)
    return pl.pallas_call(
        deal_kernel,
        out_shape=jax.ShapeDtypeStruct((members, slots, rows, rank), jnp.float32),
        in_specs=[pl.BlockSpec(memory_space=pltpu.SMEM), vmem],
        out_specs=vmem,
        cost_estimate=pl.CostEstimate(flops=1 << 20, bytes_accessed=1 << 20, transcendentals=0),
    )(wanted, pieces)


def update_kernel(again, wanted_ref, piece_ref, grad_ref, *rest):
    new_ref, total = rest[0], rest[-1]
    members, slots = grad_ref.shape[:2]
    total[...] = jnp.zeros_like(total)
    for member in range(members):
        for slot in range(slots):
            block = wanted_ref[member * slots + slot]
            total[block] = total[block] + grad_ref[member, slot]
    new_ref[...] = piece_ref[...] - step_rate * total[:members]
    if again:
        deal_kernel(wanted_ref, new_ref, rest[1])


def update(wanted, pieces, grads, again):
    members, rows, rank = pieces.shape
    vmem = pl.BlockSpec(memory_space=pltpu.VMEM)
    shapes = [jax.ShapeDtypeStruct(pieces.shape, jnp.float32)]
    if again:
        shapes.append(jax.ShapeDtypeStruct(grads.shape, jnp.float32))
    return pl.pallas_call(
        functools.partial(update_kernel, again),
        out_shape=shapes,
        in_specs=[pl.BlockSpec(memory_space=pltpu.SMEM), vmem, vmem],
        out_specs=[vmem] * len(shapes),
        scratch_shapes=[pltpu.VMEM((members + 1, rows, rank), jnp.float32)],
        cost_estimate=pl.CostEstimate(flops=1 << 20, bytes_accessed=1 << 20, transcendentals=0),
    )(wanted, pieces, grads)


def swap(value, axis):
    return lax.all_to_all(value, axis, 0, 0, tiled=True)


def spread(factor, named, axis, members):
    slots = named.shape[0]
    rows, rank = factor.shape
    note = jnp.zeros((rank,), jnp.float32).at[:slots].set(named.astype(jnp.float32))
    pieces = factor.reshape(members, rows // members, rank)
    sent = jnp.concatenate([pieces, jnp.broadcast_to(note, pieces.shape)], axis=1)
    got = swap(sent, axis)
    wanted = got[:, rows // members, :slots].astype(jnp.int32).reshape(members * slots)
    return got[:, : rows // members], wanted


def local(counts, block_coords, block_count, factor_a, factor_b, factor_c):
    slots = counts.shape[2]
    members_a, members_b = lax.axis_size("col"), lax.axis_size("row")
    where = block_coords.reshape(3 * slots)
    live = block_count.reshape(1)
    counts = counts.reshape(counts.shape[2:])
    alive = jnp.arange(slots, dtype=jnp.int32) < live
    pieces_b, wanted_b = spread(factor_b, jnp.where(alive, where[slots : 2 * slots], members_b), "row", members_b)
    pieces_a, wanted_a = spread(factor_a, jnp.where(alive, where[:slots], members_a), "col", members_a)
    dealt_b = deal(wanted_b, pieces_b, slots)
    dealt_a = deal(wanted_a, pieces_a, slots)
    for step_index in range(STEPS):
        held_b = swap(dealt_b, "row")
        held_a = swap(dealt_a, "col")
        grad_a, grad_b = block_gradients(where, live, held_a, held_b, factor_c, counts)
        back_b = swap(grad_b, "row")
        back_a = swap(grad_a, "col")
        again = step_index + 1 < STEPS
        pieces_b, *dealt_b = update(wanted_b, pieces_b, back_b, again)
        pieces_a, *dealt_a = update(wanted_a, pieces_a, back_a, again)
        if again:
            dealt_a, dealt_b = dealt_a[0], dealt_b[0]
    new_b = swap(pieces_b, "row").reshape(factor_b.shape)
    new_a = swap(pieces_a, "col").reshape(factor_a.shape)
    return (new_a, new_b)


def solution(mesh):
    return jax.shard_map(
        local,
        mesh=mesh,
        in_specs=(
            P("row", "col", None, None, None, None),
            P(None, "row", "col", None),
            P("row", "col"),
            P(("row", "col"), None),
            P(("col", "row"), None),
            P(),
        ),
        out_specs=(P(("row", "col"), None), P(("col", "row"), None)),
        check_vma=False,
    )
```

time: 935 us -> 212 us (0.23)
  waiting for transfers between devices: 765 us -> 73.6 us
  loops' own time: 61 us -> 0 us
  starting transfers between devices: 0.32 us -> 50.4 us
  blocking collectives: 0 us -> 45.6 us
  local copies, waits for them, and re-layouts: 40.9 us -> 5.26 us
  Pallas kernels: 0 us -> 28.7 us
  matrix products: 27.4 us -> 0 us
  other arithmetic: 19.4 us -> 3.78 us
  between operations: 14.3 us -> 1.41 us
    reduce_scatter x4 -> x0, waiting for transfers between devices: 529 us -> none  [the longest x2 407 us: local(): share_a = lax.psum_scatter(grad_a, 'col', scatter_dimension=0, tiled=True)]
    all_gather x4 -> x0, waiting for transfers between devices: 234 us -> none  [the longest x2 157 us: local(): band_a = lax.all_gather(factor_a, 'col', axis=0, tiled=True)]
    all_to_all x0 -> x9, waiting for transfers between devices: none -> 73.6 us  [swap(): return lax.all_to_all(value, axis, 0, 0, tiled=True)]
    another operation x2 -> x0, loops' own time: 61 us -> none  [local_gradients(): lax.scan(visit_slot, start, jnp.arange(slot_total, dtype=jnp.int32))]
    all_to_all x0 -> x9, starting transfers between devices: none -> 50.4 us  [swap(): return lax.all_to_all(value, axis, 0, 0, tiled=True)]
    all_to_all x0 -> x3, blocking collectives: none -> 45.6 us  [swap(): return lax.all_to_all(value, axis, 0, 0, tiled=True)]
    dynamic_slice x48 -> x0, local copies, waits for them, and re-layouts: 38.1 us -> none  [the longest x12 11.9 us: visit_slot(): start_b = block_coords[1, 0, 0, slot_index] * side]
    pallas_call x0 -> x8, Pallas kernels: none -> 28.7 us  [the longest x2 16.3 us: block_gradients(): pl.pallas_call(gradient_kernel, out_shape=(jax.ShapeDtypeStruct(a.shape,...]
  transfers between devices with their start and end apart: 8 -> 9, of which waited for: 8 -> 9; matrix products, arithmetic and copies ran while one was open for 0% -> 2% of each run, Pallas kernels for 0% -> 6%
where the time goes in v1:
time: 212 us; the launch traced here: 209 us
  waiting for transfers between devices  73.6 us (35%)
  starting transfers between devices  50.4 us (24%)
  blocking collectives  45.6 us (22%)
  Pallas kernels  28.7 us (14%)
  local copies, waits for them, and re-layouts  5.26 us (2%)
  other arithmetic  3.78 us (2%)
    all_to_all x9, waiting for transfers between devices, swap(): return lax.all_to_all(value, axis, 0, 0, tiled=True)  73.6 us
    all_to_all x9, starting transfers between devices, swap(): return lax.all_to_all(value, axis, 0, 0, tiled=True)  50.4 us
    all_to_all x3, blocking collectives, swap(): return lax.all_to_all(value, axis, 0, 0, tiled=True)  45.6 us
    pallas_call x2, Pallas kernels, block_gradients(): pl.pallas_call(gradient_kernel, out_shape=(jax.ShapeDtypeStruct(a.shape,...  16.3 us
    pallas_call x4, Pallas kernels, update(): pl.pallas_call(functools.partial(update_kernel, again), out_shape=shapes,...  9.01 us
  transfers between devices with their start and end apart: 9, of which 9 were waited for; matrix products, arithmetic and copies ran while one was open for 2% of the time, Pallas kernels for 6%

profile of v1, /device:TPU:1, one launch (start us, length us, event | category | flops | bytes accessed | tf_op | source)
XLA Modules:
  0.0 208.8 jit_solution(284428365873688064)
XLA Ops:
  2.0 1.5 pad_maximum_fusion.1
  3.5 6.8 %all-to-all-start.2 = ((f32[16,16,128]{2,1,0:T(8,128)}), f32[16,16,128]{2,1,0:T(8,128)S(1)}, u32[]{:S(2)}, u32[]{:S(2)}) async-start(f32[16,16,128]{2,1,0:T(8,128)} %pad_maximum_fusion.1), calls=%async_computation.2 | async-start | bytes 262144 | tf_op jit(solution)/shard_map/all_to_all | solution.py:150
  10.3 1.5 pad_maximum_fusion
  11.9 4.5 %all-to-all-done.2 = f32[16,16,128]{2,1,0:T(8,128)S(1)} async-done(((f32[16,16,128]{2,1,0:T(8,128)}), f32[16,16,128]{2,1,0:T(8,128)S(1)}, u32[]{:S(2)}, u32[]{:S(2)}) %all-to-all-start.2) | async-done | bytes 131104 | tf_op jit(solution)/shard_map/all_to_all | solution.py:150
  16.4 10.6 %all-to-all-start = ((f32[16,16,128]{2,1,0:T(8,128)}), f32[16,16,128]{2,1,0:T(8,128)S(1)}, u32[]{:S(2)}, u32[]{:S(2)}) async-start(f32[16,16,128]{2,1,0:T(8,128)} %pad_maximum_fusion), calls=%async_computation | async-start | bytes 262144 | tf_op jit(solution)/shard_map/all_to_all | solution.py:150
  28.3 1.7 shard_map.78
  30.0 6.9 %all-to-all-done = f32[16,16,128]{2,1,0:T(8,128)S(1)} async-done(((f32[16,16,128]{2,1,0:T(8,128)}), f32[16,16,128]{2,1,0:T(8,128)S(1)}, u32[]{:S(2)}, u32[]{:S(2)}) %all-to-all-start) | async-done | bytes 131104 | tf_op jit(solution)/shard_map/all_to_all | solution.py:150
  37.0 5.4 %all-to-all-start.3 = ((f32[16,6,8,128]{3,2,1,0:T(8,128)}), f32[16,6,8,128]{3,2,1,0:T(8,128)S(1)}, u32[]{:S(2)}, u32[]{:S(2)}) async-start(f32[16,6,8,128]{3,2,1,0:T(8,128)} %shard_map.78), calls=%async_computation.3 | async-start | bytes 786432 | tf_op jit(solution)/shard_map/all_to_all | solution.py:150
  43.8 1.7 shard_map.77
  45.5 5.2 %all-to-all-done.3.b_ref = f32[16,6,8,128]{3,2,1,0:T(8,128)S(1)} async-done(((f32[16,6,8,128]{3,2,1,0:T(8,128)}), f32[16,6,8,128]{3,2,1,0:T(8,128)S(1)}, u32[]{:S(2)}, u32[]{:S(2)}) %all-to-all-start.3) | async-done | bytes 393248 | tf_op jit(solution)/shard_map/all_to_all | solution.py:150
  50.7 3.6 %all-to-all-start.1 = ((f32[16,6,8,128]{3,2,1,0:T(8,128)}), f32[16,6,8,128]{3,2,1,0:T(8,128)S(1)}, u32[]{:S(2)}, u32[]{:S(2)}) async-start(f32[16,6,8,128]{3,2,1,0:T(8,128)} %shard_map.77), calls=%async_computation.1 | async-start | bytes 786432 | tf_op jit(solution)/shard_map/all_to_all | solution.py:150
  55.0 13.9 %all-to-all-done.1.a_ref = f32[16,6,8,128]{3,2,1,0:T(8,128)S(1)} async-done(((f32[16,6,8,128]{3,2,1,0:T(8,128)}), f32[16,6,8,128]{3,2,1,0:T(8,128)S(1)}, u32[]{:S(2)}, u32[]{:S(2)}) %all-to-all-start.1) | async-done | bytes 393248 | tf_op jit(solution)/shard_map/all_to_all | solution.py:150
  68.8 0.7 copy-done.4
  69.6 8.1 %shard_map.79 = (f32[16,6,8,128]{3,2,1,0:T(8,128)}, f32[16,6,8,128]{3,2,1,0:T(8,128)}) custom-call(s32[18]{0:T(128)} %reshape.75.where_ref, s32[1]{0:T(128)} %bitcast.12.live_ref, f32[16,6,8,128]{3,2,1,0:T(8,128)} %copy-done.4, f32[16,6,8,128]{3,2,1,0:T(8,128)} %copy-done, f32[1024,128]{1,0:T(8,128)} %c_ref.3, s32[6,8,128,128]{3,2,1,0:T(8,128)} %bitcast.14), custom_call_target="tpu_custom_call" | custom-call | flops 1073741824 | bytes 6291456 | tf_op jit(solution)/shard_map/pallas_call | solution.py:90
  77.7 13.4 %all_to_all.60.grad_ref = f32[16,6,8,128]{3,2,1,0:T(8,128)} all-to-all(f32[16,6,8,128]{3,2,1,0:T(8,128)} %get-tuple-element.37), channel_id=1, replica_groups=mesh['row'=16,'col'=16] {'row'}, dimensions={0} | all-to-all | bytes 786432 | tf_op jit(solution)/shard_map/all_to_all | solution.py:150
  91.1 3.8 %all-to-all-start.4 = ((f32[16,6,8,128]{3,2,1,0:T(8,128)}), f32[16,6,8,128]{3,2,1,0:T(8,128)S(1)}, u32[]{:S(2)}, u32[]{:S(2)}) async-start(f32[16,6,8,128]{3,2,1,0:T(8,128)} %get-tuple-element.34), calls=%async_computation.4 | async-start | bytes 786432 | tf_op jit(solution)/shard_map/all_to_all | solution.py:150
  94.9 2.4 %shard_map.81 = (f32[16,8,128]{2,1,0:T(8,128)}, f32[16,6,8,128]{3,2,1,0:T(8,128)}) custom-call(s32[96]{0:T(128)} %convert_element_type.25.wanted_ref, f32[16,8,128]{2,1,0:T(8,128)} %slice.57.piece_ref, f32[16,6,8,128]{3,2,1,0:T(8,128)} %all_to_all.60.grad_ref), custom_call_target="tpu_custom_call" | custom-call | flops 1048576 | bytes 1048576 | tf_op jit(solution)/shard_map/pallas_call | solution.py:139
  97.2 11.9 %all-to-all-done.4.grad_ref = f32[16,6,8,128]{3,2,1,0:T(8,128)S(1)} async-done(((f32[16,6,8,128]{3,2,1,0:T(8,128)}), f32[16,6,8,128]{3,2,1,0:T(8,128)S(1)}, u32[]{:S(2)}, u32[]{:S(2)}) %all-to-all-start.4) | async-done | bytes 393248 | tf_op jit(solution)/shard_map/all_to_all | solution.py:150
  109.2 6.5 %all-to-all-start.7 = ((f32[16,6,8,128]{3,2,1,0:T(8,128)}), f32[16,6,8,128]{3,2,1,0:T(8,128)S(1)}, u32[]{:S(2)}, u32[]{:S(2)}) async-start(f32[16,6,8,128]{3,2,1,0:T(8,128)} %get-tuple-element.38), calls=%async_computation.7 | async-start | bytes 786432 | tf_op jit(solution)/shard_map/all_to_all | solution.py:150
  115.7 2.4 %shard_map.80 = (f32[16,8,128]{2,1,0:T(8,128)}, f32[16,6,8,128]{3,2,1,0:T(8,128)}) custom-call(s32[96]{0:T(128)} %convert_element_type.22.wanted_ref, f32[16,8,128]{2,1,0:T(8,128)} %slice.55.piece_ref, f32[16,6,8,128]{3,2,1,0:T(8,128)} %copy-done.1), custom_call_target="tpu_custom_call" | custom-call | flops 1048576 | bytes 1048576 | tf_op jit(solution)/shard_map/pallas_call | solution.py:139
  118.1 5.8 %all-to-all-done.7.b_ref = f32[16,6,8,128]{3,2,1,0:T(8,128)S(1)} async-done(((f32[16,6,8,128]{3,2,1,0:T(8,128)}), f32[16,6,8,128]{3,2,1,0:T(8,128)S(1)}, u32[]{:S(2)}, u32[]{:S(2)}) %all-to-all-start.7) | async-done | bytes 393248 | tf_op jit(solution)/shard_map/all_to_all | solution.py:150
  123.9 18.8 %all_to_all.61.a_ref = f32[16,6,8,128]{3,2,1,0:T(8,128)} all-to-all(f32[16,6,8,128]{3,2,1,0:T(8,128)} %get-tuple-element.36), channel_id=1, replica_groups=mesh['row'=16,'col'=16] {'col'}, dimensions={0} | all-to-all | bytes 786432 | tf_op jit(solution)/shard_map/all_to_all | solution.py:150
  142.7 8.1 %shard_map.82 = (f32[16,6,8,128]{3,2,1,0:T(8,128)}, f32[16,6,8,128]{3,2,1,0:T(8,128)}) custom-call(s32[18]{0:T(128)} %reshape.75.where_ref, s32[1]{0:T(128)} %bitcast.13.live_ref, f32[16,6,8,128]{3,2,1,0:T(8,128)} %all_to_all.61.a_ref, f32[16,6,8,128]{3,2,1,0:T(8,128)} %copy-done.3, f32[1024,128]{1,0:T(8,128)} %c_ref.3, s32[6,8,128,128]{3,2,1,0:T(8,128)} %bitcast.15), custom_call_target="tpu_custom_call" | custom-call | flops 1073741824 | bytes 6291456 | tf_op jit(solution)/shard_map/pallas_call | solution.py:90
  150.8 13.4 %all_to_all.62.grad_ref = f32[16,6,8,128]{3,2,1,0:T(8,128)} all-to-all(f32[16,6,8,128]{3,2,1,0:T(8,128)} %get-tuple-element.41), channel_id=1, replica_groups=mesh['row'=16,'col'=16] {'row'}, dimensions={0} | all-to-all | bytes 786432 | tf_op jit(solution)/shard_map/all_to_all | solution.py:150
  164.2 3.8 %all-to-all-start.8 = ((f32[16,6,8,128]{3,2,1,0:T(8,128)}), f32[16,6,8,128]{3,2,1,0:T(8,128)S(1)}, u32[]{:S(2)}, u32[]{:S(2)}) async-start(f32[16,6,8,128]{3,2,1,0:T(8,128)} %get-tuple-element.39), calls=%async_computation.8 | async-start | bytes 786432 | tf_op jit(solution)/shard_map/all_to_all | solution.py:150
  168.0 2.1 %shard_map.84 = f32[16,8,128]{2,1,0:T(8,128)} custom-call(s32[96]{0:T(128)} %convert_element_type.25.wanted_ref, f32[16,8,128]{2,1,0:T(8,128)} %get-tuple-element.40.piece_ref, f32[16,6,8,128]{3,2,1,0:T(8,128)} %all_to_all.62.grad_ref), custom_call_target="tpu_custom_call" | custom-call | flops 1048576 | bytes 1048576 | tf_op jit(solution)/shard_map/pallas_call | solution.py:139
  170.1 12.2 %all-to-all-done.8.grad_ref = f32[16,6,8,128]{3,2,1,0:T(8,128)S(1)} async-done(((f32[16,6,8,128]{3,2,1,0:T(8,128)}), f32[16,6,8,128]{3,2,1,0:T(8,128)S(1)}, u32[]{:S(2)}, u32[]{:S(2)}) %all-to-all-start.8) | async-done | bytes 393248 | tf_op jit(solution)/shard_map/all_to_all | solution.py:150
  182.3 6.5 %all-to-all-start.11 = ((f32[16,8,128]{2,1,0:T(8,128)}), f32[16,8,128]{2,1,0:T(8,128)S(1)}, u32[]{:S(2)}, u32[]{:S(2)}) async-start(f32[16,8,128]{2,1,0:T(8,128)} %shard_map.84), calls=%async_computation.11 | async-start | bytes 131072 | tf_op jit(solution)/shard_map/all_to_all | solution.py:150
  188.8 2.1 %shard_map.83 = f32[16,8,128]{2,1,0:T(8,128)} custom-call(s32[96]{0:T(128)} %convert_element_type.22.wanted_ref, f32[16,8,128]{2,1,0:T(8,128)} %get-tuple-element.35.piece_ref, f32[16,6,8,128]{3,2,1,0:T(8,128)} %copy-done.2), custom_call_target="tpu_custom_call" | custom-call | flops 1048576 | bytes 1048576 | tf_op jit(solution)/shard_map/pallas_call | solution.py:139
  190.9 3.7 %all-to-all-done.11 = f32[16,8,128]{2,1,0:T(8,128)S(1)} async-done(((f32[16,8,128]{2,1,0:T(8,128)}), f32[16,8,128]{2,1,0:T(8,128)S(1)}, u32[]{:S(2)}, u32[]{:S(2)}) %all-to-all-start.11) | async-done | bytes 65568 | tf_op jit(solution)/shard_map/all_to_all | solution.py:150
  194.6 3.5 %all-to-all-start.9 = ((f32[16,8,128]{2,1,0:T(8,128)}), f32[16,8,128]{2,1,0:T(8,128)S(1)}, u32[]{:S(2)}, u32[]{:S(2)}) async-start(f32[16,8,128]{2,1,0:T(8,128)} %shard_map.83), calls=%async_computation.9 | async-start | bytes 131072 | tf_op jit(solution)/shard_map/all_to_all | solution.py:150
  198.1 9.4 %all-to-all-done.9 = f32[16,8,128]{2,1,0:T(8,128)S(1)} async-done(((f32[16,8,128]{2,1,0:T(8,128)}), f32[16,8,128]{2,1,0:T(8,128)S(1)}, u32[]{:S(2)}, u32[]{:S(2)}) %all-to-all-start.9) | async-done | bytes 65568 | tf_op jit(solution)/shard_map/all_to_all | solution.py:150
  (26 shorter events, 5.3 us)
Async XLA Ops:
  0.6 53.6 %copy-start.5 = (s32[3,1,1,6]{3,2,1,0:T(1,128)S(1)}, s32[3,1,1,6]{3,2,1,0:T(1,128)}, u32[]{:S(2)}) copy-start(s32[3,1,1,6]{3,2,1,0:T(1,128)} %param.11) | copy-start | bytes 220
  3.5 12.9 %all-to-all-start.2 = ((f32[16,16,128]{2,1,0:T(8,128)}), f32[16,16,128]{2,1,0:T(8,128)S(1)}, u32[]{:S(2)}, u32[]{:S(2)}) async-start(f32[16,16,128]{2,1,0:T(8,128)} %pad_maximum_fusion.1), calls=%async_computation.2 | async-start | bytes 262144 | tf_op jit(solution)/shard_map/all_to_all | solution.py:150
  16.4 20.6 %all-to-all-start = ((f32[16,16,128]{2,1,0:T(8,128)}), f32[16,16,128]{2,1,0:T(8,128)S(1)}, u32[]{:S(2)}, u32[]{:S(2)}) async-start(f32[16,16,128]{2,1,0:T(8,128)} %pad_maximum_fusion), calls=%async_computation | async-start | bytes 262144 | tf_op jit(solution)/shard_map/all_to_all | solution.py:150
  37.0 13.7 %all-to-all-start.3 = ((f32[16,6,8,128]{3,2,1,0:T(8,128)}), f32[16,6,8,128]{3,2,1,0:T(8,128)S(1)}, u32[]{:S(2)}, u32[]{:S(2)}) async-start(f32[16,6,8,128]{3,2,1,0:T(8,128)} %shard_map.78), calls=%async_computation.3 | async-start | bytes 786432 | tf_op jit(solution)/shard_map/all_to_all | solution.py:150
  50.7 18.1 %copy-start = (f32[16,6,8,128]{3,2,1,0:T(8,128)}, f32[16,6,8,128]{3,2,1,0:T(8,128)S(1)}, u32[]{:S(2)}) copy-start(f32[16,6,8,128]{3,2,1,0:T(8,128)S(1)} %all-to-all-done.3.b_ref) | copy-start | bytes 1179652
  50.7 18.1 %all-to-all-start.1 = ((f32[16,6,8,128]{3,2,1,0:T(8,128)}), f32[16,6,8,128]{3,2,1,0:T(8,128)S(1)}, u32[]{:S(2)}, u32[]{:S(2)}) async-start(f32[16,6,8,128]{3,2,1,0:T(8,128)} %shard_map.77), calls=%async_computation.1 | async-start | bytes 786432 | tf_op jit(solution)/shard_map/all_to_all | solution.py:150
  68.8 0.7 copy-start.4
  91.1 18.1 %all-to-all-start.4 = ((f32[16,6,8,128]{3,2,1,0:T(8,128)}), f32[16,6,8,128]{3,2,1,0:T(8,128)S(1)}, u32[]{:S(2)}, u32[]{:S(2)}) async-start(f32[16,6,8,128]{3,2,1,0:T(8,128)} %get-tuple-element.34), calls=%async_computation.4 | async-start | bytes 786432 | tf_op jit(solution)/shard_map/all_to_all | solution.py:150
  109.2 6.5 %copy-start.1 = (f32[16,6,8,128]{3,2,1,0:T(8,128)}, f32[16,6,8,128]{3,2,1,0:T(8,128)S(1)}, u32[]{:S(2)}) copy-start(f32[16,6,8,128]{3,2,1,0:T(8,128)S(1)} %all-to-all-done.4.grad_ref) | copy-start | bytes 1179652
  109.2 14.7 %all-to-all-start.7 = ((f32[16,6,8,128]{3,2,1,0:T(8,128)}), f32[16,6,8,128]{3,2,1,0:T(8,128)S(1)}, u32[]{:S(2)}, u32[]{:S(2)}) async-start(f32[16,6,8,128]{3,2,1,0:T(8,128)} %get-tuple-element.38), calls=%async_computation.7 | async-start | bytes 786432 | tf_op jit(solution)/shard_map/all_to_all | solution.py:150
  123.9 18.8 %copy-start.3 = (f32[16,6,8,128]{3,2,1,0:T(8,128)}, f32[16,6,8,128]{3,2,1,0:T(8,128)S(1)}, u32[]{:S(2)}) copy-start(f32[16,6,8,128]{3,2,1,0:T(8,128)S(1)} %all-to-all-done.7.b_ref) | copy-start | bytes 1179652
  164.2 18.1 %all-to-all-start.8 = ((f32[16,6,8,128]{3,2,1,0:T(8,128)}), f32[16,6,8,128]{3,2,1,0:T(8,128)S(1)}, u32[]{:S(2)}, u32[]{:S(2)}) async-start(f32[16,6,8,128]{3,2,1,0:T(8,128)} %get-tuple-element.39), calls=%async_computation.8 | async-start | bytes 786432 | tf_op jit(solution)/shard_map/all_to_all | solution.py:150
  182.3 6.5 %copy-start.2 = (f32[16,6,8,128]{3,2,1,0:T(8,128)}, f32[16,6,8,128]{3,2,1,0:T(8,128)S(1)}, u32[]{:S(2)}) copy-start(f32[16,6,8,128]{3,2,1,0:T(8,128)S(1)} %all-to-all-done.8.grad_ref) | copy-start | bytes 1179652
  182.3 12.3 %all-to-all-start.11 = ((f32[16,8,128]{2,1,0:T(8,128)}), f32[16,8,128]{2,1,0:T(8,128)S(1)}, u32[]{:S(2)}, u32[]{:S(2)}) async-start(f32[16,8,128]{2,1,0:T(8,128)} %shard_map.84), calls=%async_computation.11 | async-start | bytes 131072 | tf_op jit(solution)/shard_map/all_to_all | solution.py:150
  194.6 12.9 %all-to-all-start.9 = ((f32[16,8,128]{2,1,0:T(8,128)}), f32[16,8,128]{2,1,0:T(8,128)S(1)}, u32[]{:S(2)}, u32[]{:S(2)}) async-start(f32[16,8,128]{2,1,0:T(8,128)} %shard_map.83), calls=%async_computation.9 | async-start | bytes 131072 | tf_op jit(solution)/shard_map/all_to_all | solution.py:150

commit v2 on v0

v2 whole, which is shorter than its diff:
```python
import functools

import jax
import jax.numpy as jnp
from jax import lax
from jax.experimental import pallas as pl
from jax.experimental.pallas import tpu as pltpu
from jax.sharding import PartitionSpec as P


STEPS = 2
step_rate = 0.004


vmem = pl.BlockSpec(memory_space=pltpu.VMEM)
smem = pl.BlockSpec(memory_space=pltpu.SMEM)
anywhere = pl.BlockSpec(memory_space=pl.ANY)
small_cost = pl.CostEstimate(flops=1 << 20, bytes_accessed=1 << 20, transcendentals=0)
chip_order = (6, 7, 5, 2, 4, 3, 1)


def shape_of(*sizes):
    return jax.ShapeDtypeStruct(sizes, jnp.float32)


def rows_at(index, rows):
    return pl.ds(pl.multiple_of(index * rows, rows), rows)


def split(value):
    high = value.astype(jnp.bfloat16)
    low = (value - high.astype(jnp.float32)).astype(jnp.bfloat16)
    return high, low


def two_halves(value):
    high, low = split(value)
    return jnp.concatenate([high, low], axis=1)


def pair_table(value):
    row = two_halves(value)
    return jnp.concatenate([row, row], axis=0)


def fold(product):
    return product[:, :128] + product[:, 128:]


def swap_col(sent):
    return lax.all_to_all(sent, "col", 0, 0, tiled=True)


def shift_row(value, change):
    members = lax.axis_size("row")
    return lax.ppermute(value, "row", [(member, member ^ change) for member in range(members)])


def swap_row(even, odd):
    passed = shift_row(odd, 1)
    both = [jnp.stack([even[pair], passed[pair]]) for pair in range(even.shape[0])]
    got = [both[0]] + [None] * len(chip_order)
    for pair in chip_order:
        got[pair] = shift_row(both[pair], 2 * pair)
    return got


def open_kernel(where_ref, live_ref, a_ref, b_ref, send_a, send_b):
    slots = where_ref.shape[0] // 3
    side, rank = a_ref.shape
    members = send_a.shape[0]
    rows = send_b.shape[0] - side
    lane = lax.broadcasted_iota(jnp.int32, (rows, rank), 1)

    def note(first):
        value = jnp.zeros((rows, rank), jnp.float32)
        for slot in range(slots):
            named = jnp.where(slot < live_ref[0], where_ref[first + slot], members).astype(jnp.float32)
            value = jnp.where(lane == slot, named, value)
        return value

    send_b[:side] = b_ref[...]
    send_b[side:] = note(slots)
    block, named = a_ref[...], note(0)
    for member in range(members):
        send_a[member, :side] = block
        send_a[member, side:] = named


def open_blocks(where, live, factor_a, factor_b, members):
    side, rank = factor_a.shape
    rows = side // members
    return pl.pallas_call(
        open_kernel,
        out_shape=(shape_of(members, side + rows, rank), shape_of(side + rows, rank)),
        in_specs=[smem, smem, vmem, vmem],
        out_specs=(vmem, vmem),
        cost_estimate=small_cost,
    )(where, live, factor_a, factor_b)


def start_kernel(slots, at_ref, *refs):
    a_ref, b_refs, refs = refs[0], refs[1:9], refs[9:]
    wanted_a, wanted_b, piece_a, piece_b, notes, held, sems = refs
    members, rows, _ = piece_a.shape
    side = members * rows
    copies = [
        pltpu.make_async_copy(a_ref.at[:, rows_at(at_ref[1], rows)], piece_a, sems.at[0]),
        pltpu.make_async_copy(a_ref.at[:, side], notes.at[0], sems.at[1]),
    ]
    for pair, ref in enumerate(b_refs):
        two = pl.ds(2 * pair, 2)
        copies.append(
            pltpu.make_async_copy(ref.at[:, rows_at(at_ref[0], rows)], held.at[two], sems.at[2 + 2 * pair])
        )
        copies.append(pltpu.make_async_copy(ref.at[:, side], notes.at[1, two], sems.at[3 + 2 * pair]))
    for copy in copies:
        copy.start()
    for copy in copies:
        copy.wait()
    for place in range(members):
        piece_b[at_ref[0] ^ place] = held[place]

    def name(place, carry):
        for slot in range(slots):
            wanted_a[place * slots + slot] = notes[0, place, slot].astype(jnp.int32)
            wanted_b[place * slots + slot] = notes[1, place, slot].astype(jnp.int32)
        return carry

    lax.fori_loop(0, members, name, 0)


def start_pieces(at, all_a, all_b, members, slots, rows, rank):
    names = jax.ShapeDtypeStruct((members * slots,), jnp.int32)
    return pl.pallas_call(
        functools.partial(start_kernel, slots),
        out_shape=(names, names, shape_of(members, rows, rank), shape_of(members, rows, rank)),
        in_specs=[smem] + [anywhere] * 9,
        out_specs=(smem, smem, vmem, vmem),
        scratch_shapes=[
            pltpu.SMEM((2, members, rank), jnp.float32),
            pltpu.VMEM((members, rows, rank), jnp.float32),
            pltpu.SemaphoreType.DMA((18,)),
        ],
        cost_estimate=small_cost,
    )(at, all_a, *all_b)


def slot_gradients(piece_a, piece_b, piece_c, observed):
    depth, (side, rank) = piece_c.shape[0], piece_a.shape
    scaled_a = (piece_c[:, None, :] * piece_a[None, :, :]).reshape(depth * side, rank)
    b_high, b_low = split(piece_b)
    b_rows = jnp.concatenate(
        [jnp.concatenate([b_high, b_high], axis=1), jnp.concatenate([b_low, b_low], axis=1)], axis=0
    )
    model = fold(
        lax.dot_general(two_halves(scaled_a), b_rows, (((1,), (1,)), ((), ())), preferred_element_type=jnp.float32)
    )
    residual = jnp.exp(model) - observed().reshape(depth * side, side).astype(jnp.float32)
    along_b = fold(jnp.dot(two_halves(residual), pair_table(piece_b), preferred_element_type=jnp.float32))
    turned = jnp.swapaxes(residual.reshape(depth, side, side), 1, 2).reshape(depth * side, side)
    along_a = fold(jnp.dot(two_halves(turned), pair_table(piece_a), preferred_element_type=jnp.float32))
    grad_a = (along_b.reshape(depth, side, rank) * piece_c[:, None, :]).sum(0)
    grad_b = (along_a.reshape(depth, side, rank) * piece_c[:, None, :]).sum(0)
    return grad_a, grad_b


class Fetches:
    def __init__(self, where_ref, live_ref, c_ref, counts_ref, part_c, seen, sems):
        self.refs = where_ref, live_ref, c_ref, counts_ref, part_c, seen, sems
        self.slots, self.depth = counts_ref.shape[:2]

    def copies(self, slot):
        where_ref, _, c_ref, counts_ref, part_c, seen, sems = self.refs
        start_c = pl.multiple_of(where_ref[2 * self.slots + slot] * self.depth, self.depth)
        return (
            pltpu.make_async_copy(c_ref.at[pl.ds(start_c, self.depth)], part_c.at[slot], sems.at[0, slot]),
            pltpu.make_async_copy(counts_ref.at[slot], seen.at[slot], sems.at[1, slot]),
        )

    def start(self):
        for slot in range(self.slots):

            @pl.when(slot < self.refs[1][0])
            def _():
                for copy in self.copies(slot):
                    copy.start()

    def factor(self, slot):
        self.copies(slot)[0].wait()
        return self.refs[4][slot]

    def observed(self, slot):
        self.copies(slot)[1].wait()
        return self.refs[5][slot]


def first_kernel(at_ref, where_ref, live_ref, *refs):
    a_ref, b_refs, (c_ref, counts_ref), refs = refs[0], refs[1:9], refs[9:11], refs[11:]
    ga_ref, gb_refs, refs = refs[0], refs[1:3], refs[3:]
    block_a, all_b, turned_b, part_c, seen, sems, sem_a, sem_b = refs
    slots, _, side, rank = counts_ref.shape
    members = a_ref.shape[0]
    rows = side // members
    live = live_ref[0]
    fetches = Fetches(where_ref, live_ref, c_ref, counts_ref, part_c, seen, sems)

    def fetch_a(slot):
        return pltpu.make_async_copy(a_ref.at[where_ref[slot], pl.ds(0, side)], block_a.at[slot], sem_a.at[slot])

    copies_b = [
        pltpu.make_async_copy(ref.at[:, pl.ds(0, side)], all_b.at[pl.ds(2 * pair, 2)], sem_b.at[pair])
        for pair, ref in enumerate(b_refs)
    ]
    for slot in range(slots):

        @pl.when(slot < live)
        def _():
            fetch_a(slot).start()

    for copy in copies_b:
        copy.start()
    fetches.start()
    for copy in copies_b:
        copy.wait()

    def visit(slot, carry):
        fetch_a(slot).wait()
        piece_b = all_b[where_ref[slots + slot] ^ at_ref[0]]
        grad_a, grad_b = slot_gradients(
            block_a[slot], piece_b, fetches.factor(slot), functools.partial(fetches.observed, slot)
        )
        ga_ref[:, slot] = grad_a.reshape(members, rows, rank)
        turned_b[...] = grad_b
        for place in range(members):
            gb_refs[place % 2][place // 2, slot] = turned_b[rows_at(at_ref[0] ^ place, rows), :]
        return carry

    lax.fori_loop(0, live, visit, 0)

    def clear(slot, carry):
        ga_ref[:, slot] = jnp.zeros((members, rows, rank), jnp.float32)
        for ref in gb_refs:
            ref[:, slot] = jnp.zeros((members // 2, rows, rank), jnp.float32)
        return carry

    lax.fori_loop(live, slots, clear, 0)


def last_kernel(at_ref, where_ref, live_ref, *refs):
    a_ref, b_refs, (c_ref, counts_ref), refs = refs[0], refs[1:9], refs[9:11], refs[11:]
    ga_ref, even_ref, odd_ref, base_b, refs = *refs[:4], refs[4:]
    block_a, all_b, block_b, part_c, seen, sems, sem_b = refs
    slots, _, side, rank = counts_ref.shape
    members = a_ref.shape[0]
    rows = side // members
    live = live_ref[0]
    me = at_ref[0]
    fetches = Fetches(where_ref, live_ref, c_ref, counts_ref, part_c, seen, sems)
    copies = [pltpu.make_async_copy(a_ref, block_a, sem_b.at[8])]
    for pair, ref in enumerate(b_refs):
        copies.append(pltpu.make_async_copy(ref, all_b.at[pl.ds(2 * pair, 2)], sem_b.at[pair]))
    for copy in copies:
        copy.start()
    fetches.start()
    for ref in (ga_ref, even_ref, odd_ref):
        ref[...] = jnp.zeros_like(ref)
    for copy in copies:
        copy.wait()
    for place in range(members):
        base_b[rows_at(me ^ place, rows), :] = all_b[place, slots]

    def visit(slot, carry):
        for place in range(members):
            block_b[rows_at(me ^ place, rows), :] = all_b[place, slot]
        grad_a, grad_b = slot_gradients(
            block_a[:, slot].reshape(side, rank),
            block_b[...],
            fetches.factor(slot),
            functools.partial(fetches.observed, slot),
        )
        ga_ref[where_ref[slot]] += grad_a
        place = where_ref[slots + slot] ^ me

        @pl.when(place % 2 == 0)
        def _():
            even_ref[place // 2] += grad_b

        @pl.when(place % 2 == 1)
        def _():
            odd_ref[place // 2] += grad_b

        return carry

    lax.fori_loop(0, live, visit, 0)


def block_gradients(at, where, live, held_a, held_b, c, counts, members, last):
    slots, depth, side, rank = counts.shape
    rows = side // members
    common = [
        pltpu.VMEM((slots, depth, rank), jnp.float32),
        pltpu.VMEM(counts.shape, jnp.int32),
        pltpu.SemaphoreType.DMA((2, slots)),
    ]
    if last:
        kernel = last_kernel
        half = shape_of(members // 2, side, rank)
        shapes = (shape_of(members, side, rank), half, half, shape_of(side, rank))
        scratch = [
            pltpu.VMEM(held_a.shape, jnp.float32),
            pltpu.VMEM((members, *held_b[0].shape[1:]), jnp.float32),
            pltpu.VMEM((side, rank), jnp.float32),
            *common,
            pltpu.SemaphoreType.DMA((9,)),
        ]
    else:
        kernel = first_kernel
        half = shape_of(members // 2, slots, rows, rank)
        shapes = (shape_of(members, slots, rows, rank), half, half)
        scratch = [
            pltpu.VMEM((slots, side, rank), jnp.float32),
            pltpu.VMEM((members, side, rank), jnp.float32),
            pltpu.VMEM((side, rank), jnp.float32),
            *common,
            pltpu.SemaphoreType.DMA((slots,)),
            pltpu.SemaphoreType.DMA((8,)),
        ]
    return pl.pallas_call(
        kernel,
        out_shape=shapes,
        in_specs=[smem] * 3 + [anywhere] * 11,
        out_specs=[vmem] * len(shapes),
        scratch_shapes=scratch,
        cost_estimate=pl.CostEstimate(flops=1 << 30, bytes_accessed=6 << 20, transcendentals=1 << 20),
    )(at, where, live, held_a, *held_b, c, counts)


def update_kernel(received, at_ref, wanted_ref, piece_ref, *refs):
    sources, refs = refs[:received], refs[received:]
    outs, (grads, total, sems) = refs[:-3], refs[-3:]
    members, slots, _, _ = grads.shape
    each = members // received
    copies = [
        pltpu.make_async_copy(ref, grads.at[pl.ds(each * index, each)], sems.at[index])
        for index, ref in enumerate(sources)
    ]
    for copy in copies:
        copy.start()
    total[...] = jnp.zeros_like(total)
    for copy in copies:
        copy.wait()

    def gather(place, carry):
        for slot in range(slots):
            block = wanted_ref[place * slots + slot]
            total[block] = total[block] + grads[place, slot]
        return carry

    lax.fori_loop(0, members, gather, 0)
    total[:members] = piece_ref[...] - step_rate * total[:members]

    def deal(index, carry):
        for way, out_ref in enumerate(outs):
            place = index * len(outs) + way
            owner = place if received == 1 else at_ref[0] ^ place
            for slot in range(slots):
                out_ref[index, slot] = total[jnp.minimum(wanted_ref[place * slots + slot], members - 1)]
            out_ref[index, slots] = total[owner]
        return carry

    lax.fori_loop(0, members // len(outs), deal, 0)


def update(at, wanted, pieces, grads):
    members, rows, rank = pieces.shape
    slots = grads[0].shape[1]
    if len(grads) == 1:
        shapes = [shape_of(members, slots + 1, rows, rank)]
    else:
        shapes = [shape_of(members // 2, slots + 1, rows, rank)] * 2
    return pl.pallas_call(
        functools.partial(update_kernel, len(grads)),
        out_shape=shapes,
        in_specs=[smem, smem, vmem] + [anywhere] * len(grads),
        out_specs=[vmem] * len(shapes),
        scratch_shapes=[
            pltpu.VMEM((members, slots, rows, rank), jnp.float32),
            pltpu.VMEM((members + 1, rows, rank), jnp.float32),
            pltpu.SemaphoreType.DMA((len(grads),)),
        ],
        cost_estimate=small_cost,
    )(at, wanted, pieces, *grads)


def local(counts, block_coords, block_count, factor_a, factor_b, factor_c):
    assert STEPS == 2
    slots = counts.shape[2]
    members = lax.axis_size("row")
    side, rank = factor_a.shape
    rows = side // members
    at = jnp.stack([lax.axis_index("row"), lax.axis_index("col")]).astype(jnp.int32)
    where = block_coords.reshape(3 * slots)
    live = block_count.reshape(1)
    counts = counts.reshape(counts.shape[2:])
    send_a, send_b = open_blocks(where, live, factor_a, factor_b, members)
    all_a = swap_col(send_a)
    both = jnp.stack([send_b, shift_row(send_b, 1)])
    all_b = [both] + [None] * len(chip_order)
    for pair in chip_order:
        all_b[pair] = shift_row(both, 2 * pair)
    grad_a, *grad_b = block_gradients(
        at, where, live, all_a, all_b, factor_c, counts, members, False
    )
    wanted_a, wanted_b, pieces_a, pieces_b = start_pieces(at, all_a, all_b, members, slots, rows, rank)
    back_a = swap_col(grad_a)
    back_b = swap_row(*grad_b)
    dealt_b = update(at, wanted_b, pieces_b, back_b)
    (dealt_a,) = update(at, wanted_a, pieces_a, [back_a])
    held_a = swap_col(dealt_a)
    held_b = swap_row(*dealt_b)
    grad_a, even_b, odd_b, base_b = block_gradients(at, where, live, held_a, held_b, factor_c, counts, members, True)
    terms_a = swap_col(grad_a)
    sums = even_b + shift_row(odd_b, 1)
    terms_b = [sums[0]] + [shift_row(sums[pair], 2 * pair) for pair in chip_order]
    new_b = base_b - step_rate * sum(terms_b)
    new_a = held_a[:, slots].reshape(side, rank) - step_rate * terms_a.sum(0)
    return (new_a, new_b)


def solution(mesh):
    return jax.shard_map(
        local,
        mesh=mesh,
        in_specs=(
            P("row", "col", None, None, None, None),
            P(None, "row", "col", None),
            P("row", "col"),
            P(("row", "col"), None),
            P(("col", "row"), None),
            P(),
        ),
        out_specs=(P(("row", "col"), None), P(("col", "row"), None)),
        check_vma=False,
    )
```

time: 935 us -> 171 us (0.18)
  the two profiles are of different devices: /device:TPU:1 before, /device:TPU:9 now
where the time goes in v2:
time: 171 us; the launch traced here: 170 us
  starting transfers between devices  90.3 us (53%)
  waiting for transfers between devices  47.2 us (28%)
  Pallas kernels  20.7 us (12%)
  other arithmetic  4.95 us (3%)
  local copies, waits for them, and re-layouts  4.7 us (3%)
  between operations  1.74 us (1%)
    ppermute x32, starting transfers between devices, shift_row(): lax.ppermute(value, 'row', [(member, member ^ change) for member in range...  51.2 us
    all_to_all x4, starting transfers between devices, swap_col(): return lax.all_to_all(sent, 'col', 0, 0, tiled=True)  39.1 us
    ppermute x32, waiting for transfers between devices, shift_row(): lax.ppermute(value, 'row', [(member, member ^ change) for member in range...  28.8 us
    all_to_all x4, waiting for transfers between devices, swap_col(): return lax.all_to_all(sent, 'col', 0, 0, tiled=True)  18.4 us
    pallas_call x2, Pallas kernels, block_gradients(): pl.pallas_call(kernel, out_shape=shapes, in_specs=[smem] * 3 + [anywhere]...  8.92 us
    pallas_call x2, Pallas kernels, update(): pl.pallas_call(functools.partial(update_kernel, len(grads)), out_shape=sh...  6.58 us
  transfers between devices with their start and end apart: 36, of which 18 were waited for; matrix products, arithmetic and copies ran while one was open for 2% of the time, Pallas kernels for 4%

profile of v2, /device:TPU:9, one launch (start us, length us, event | category | flops | bytes accessed | tf_op | source)
XLA Modules:
  0.0 169.5 jit_solution(8041654283059218489)
XLA Ops:
  2.6 2.0 %shard_map.77 = (f32[16,136,128]{2,1,0:T(8,128)}, f32[136,128]{1,0:T(8,128)}) custom-call(s32[18]{0:T(128)} %reshape.13.where_ref, s32[1]{0:T(128)} %bitcast.44.live_ref, f32[128,128]{1,0:T(8,128)} %a_ref.1, f32[128,128]{1,0:T(8,128)} %b_ref.1), custom_call_target="tpu_custom_call" | custom-call | flops 1048576 | bytes 1048576 | tf_op jit(solution)/shard_map/pallas_call | solution.py:93
  4.6 10.2 %all-to-all-start = ((f32[16,136,128]{2,1,0:T(8,128)}), f32[16,136,128]{2,1,0:T(8,128)S(1)}, u32[]{:S(2)}, u32[]{:S(2)}) async-start(f32[16,136,128]{2,1,0:T(8,128)} %get-tuple-element.17), calls=%async_computation | async-start | bytes 2228224 | tf_op jit(solution)/shard_map/all_to_all | solution.py:51
  18.0 2.5 %collective-permute-start.2 = (f32[2,136,128]{2,1,0:T(8,128)S(1)}, f32[2,136,128]{2,1,0:T(8,128)S(1)}, u32[]{:S(2)}, u32[]{:S(2)}) collective-permute-start(f32[2,136,128]{2,1,0:T(8,128)S(1)} %pad_maximum_fusion.refs_1_), channel_id=1, source_target_pairs={{0,64},{16,80},{32,96},{48,112},{64,0},{80,16},{96,32},{112,48},{1... | collective-permute-start | bytes 417800 | tf_op jit(solution)/shard_map/ppermute | solution.py:56
  21.9 4.4 %collective-permute-start.6 = (f32[2,136,128]{2,1,0:T(8,128)S(1)}, f32[2,136,128]{2,1,0:T(8,128)S(1)}, u32[]{:S(2)}, u32[]{:S(2)}) collective-permute-start(f32[2,136,128]{2,1,0:T(8,128)S(1)} %pad_maximum_fusion.refs_1_), channel_id=1, source_target_pairs={{0,192},{16,208},{32,224},{48,240},{64,128},{80,144},{96,160},{112... | collective-permute-start | bytes 417800 | tf_op jit(solution)/shard_map/ppermute | solution.py:56
  29.5 5.5 %collective-permute-done.6.refs_7_ = f32[2,136,128]{2,1,0:T(8,128)S(1)} collective-permute-done((f32[2,136,128]{2,1,0:T(8,128)S(1)}, f32[2,136,128]{2,1,0:T(8,128)S(1)}, u32[]{:S(2)}, u32[]{:S(2)}) %collective-permute-start.6) | collective-permute-done | bytes 139296 | tf_op jit(solution)/shard_map/ppermute | solution.py:56
  35.0 5.9 %collective-permute-done.7.refs_8_ = f32[2,136,128]{2,1,0:T(8,128)S(1)} collective-permute-done((f32[2,136,128]{2,1,0:T(8,128)S(1)}, f32[2,136,128]{2,1,0:T(8,128)S(1)}, u32[]{:S(2)}, u32[]{:S(2)}) %collective-permute-start.7) | collective-permute-done | bytes 139296 | tf_op jit(solution)/shard_map/ppermute | solution.py:56
  40.9 4.1 %all-to-all-done.refs_0_ = f32[16,136,128]{2,1,0:T(8,128)S(1)} async-done(((f32[16,136,128]{2,1,0:T(8,128)}), f32[16,136,128]{2,1,0:T(8,128)S(1)}, u32[]{:S(2)}, u32[]{:S(2)}) %all-to-all-start) | async-done | bytes 1114144 | tf_op jit(solution)/shard_map/all_to_all | solution.py:51
  46.0 4.3 %shard_map.79 = (f32[16,6,8,128]{3,2,1,0:T(8,128)}, f32[8,6,8,128]{3,2,1,0:T(8,128)}, f32[8,6,8,128]{3,2,1,0:T(8,128)}) custom-call(s32[2]{0:T(128)} %pad_add_fusion.at_ref, s32[18]{0:T(128)} %reshape.13.where_ref, s32[1]{0:T(128)} %bitcast.45.live_ref, f32[16,136,128]{2,1,0:T(8,128)} %copy-done, f32[2,136,128]{2,1,0:T(8,128)} %copy-done.3, ...), custom_call_target="tpu_custom_call" | custom-call | flops 1073741824 | bytes 6291456 | tf_op jit(solution)/shard_map/pallas_call | solution.py:329
  50.4 7.7 %collective-permute-start.8 = (f32[8,6,8,128]{3,2,1,0:T(8,128)}, f32[8,6,8,128]{3,2,1,0:T(8,128)S(1)}, u32[]{:S(2)}, u32[]{:S(2)}) collective-permute-start(f32[8,6,8,128]{3,2,1,0:T(8,128)} %get-tuple-element.25), channel_id=1, source_target_pairs={{0,16},{16,0},{32,48},{48,32},{64,80},{80,64},{96,112},{112,96},{1... | collective-permute-start | bytes 589832 | tf_op jit(solution)/shard_map/ppermute | solution.py:56
  58.1 6.3 %all-to-all-start.1 = ((f32[16,6,8,128]{3,2,1,0:T(8,128)}), f32[16,6,8,128]{3,2,1,0:T(8,128)S(1)}, u32[]{:S(2)}, u32[]{:S(2)}) async-start(f32[16,6,8,128]{3,2,1,0:T(8,128)} %get-tuple-element.21), calls=%async_computation.1 | async-start | bytes 786432 | tf_op jit(solution)/shard_map/all_to_all | solution.py:51
  64.4 3.2 %shard_map.78 = (s32[96]{0:T(128)}, s32[96]{0:T(128)}, f32[16,8,128]{2,1,0:T(8,128)}, f32[16,8,128]{2,1,0:T(8,128)}) custom-call(s32[2]{0:T(128)} %pad_add_fusion.at_ref, f32[16,136,128]{2,1,0:T(8,128)} %copy-done, f32[2,136,128]{2,1,0:T(8,128)} %copy-done.3, f32[2,136,128]{2,1,0:T(8,128)} %copy-done.4, f32[2,136,128]{2,1,0:T(8,128)} %copy-done.5, ...), custom_call_target="tpu_custom_call" | custom-call | flops 1048576 | bytes 1048576 | tf_op jit(solution)/shard_map/pallas_call | solution.py:135
  67.7 6.2 %collective-permute-start.15 = (f32[2,6,8,128]{3,2,1,0:T(8,128)S(1)}, f32[2,6,8,128]{3,2,1,0:T(8,128)S(1)}, u32[]{:S(2)}, u32[]{:S(2)}) collective-permute-start(f32[2,6,8,128]{3,2,1,0:T(8,128)S(1)} %pad_maximum_fusion.16), channel_id=1, source_target_pairs={{0,224},{16,240},{32,192},{48,208},{64,160},{80,176},{96,128},{112... | collective-permute-start | bytes 147464 | tf_op jit(solution)/shard_map/ppermute | solution.py:56
  75.8 2.4 %collective-permute-start.11 = (f32[2,6,8,128]{3,2,1,0:T(8,128)S(1)}, f32[2,6,8,128]{3,2,1,0:T(8,128)S(1)}, u32[]{:S(2)}, u32[]{:S(2)}) collective-permute-start(f32[2,6,8,128]{3,2,1,0:T(8,128)S(1)} %pad_maximum_fusion.12), channel_id=1, source_target_pairs={{0,96},{16,112},{32,64},{48,80},{64,32},{80,48},{96,0},{112,16},{1... | collective-permute-start | bytes 147464 | tf_op jit(solution)/shard_map/ppermute | solution.py:56
  83.7 3.3 %shard_map.81 = (f32[8,7,8,128]{3,2,1,0:T(8,128)}, f32[8,7,8,128]{3,2,1,0:T(8,128)}) custom-call(s32[2]{0:T(128)} %pad_add_fusion.at_ref, s32[96]{0:T(128)} %get-tuple-element.22.wanted_ref, f32[16,8,128]{2,1,0:T(8,128)} %get-tuple-element.23.piece_ref, f32[2,6,8,128]{3,2,1,0:T(8,128)} %pad_maximum_fusion.9.refs_0_, f32[2,6,8,128]{3,2,1,0:T(8,128)} %copy-done.28, ...), custom_call_target="tpu_custom_call" | custom-call | flops 1048576 | bytes 1048576 | tf_op jit(solution)/shard_map/pallas_call | solution.py:382
  87.0 2.7 %collective-permute-start.16 = (f32[8,7,8,128]{3,2,1,0:T(8,128)}, f32[8,7,8,128]{3,2,1,0:T(8,128)S(1)}, u32[]{:S(2)}, u32[]{:S(2)}) collective-permute-start(f32[8,7,8,128]{3,2,1,0:T(8,128)} %get-tuple-element.27), channel_id=1, source_target_pairs={{0,16},{16,0},{32,48},{48,32},{64,80},{80,64},{96,112},{112,96},{1... | collective-permute-start | bytes 688136 | tf_op jit(solution)/shard_map/ppermute | solution.py:56
  91.8 3.3 %shard_map.80 = f32[16,7,8,128]{3,2,1,0:T(8,128)} custom-call(s32[2]{0:T(128)} %pad_add_fusion.at_ref, s32[96]{0:T(128)} %get-tuple-element.19.wanted_ref, f32[16,8,128]{2,1,0:T(8,128)} %get-tuple-element.20.piece_ref, f32[16,6,8,128]{3,2,1,0:T(8,128)} %copy-done.2), custom_call_target="tpu_custom_call" | custom-call | flops 1048576 | bytes 1048576 | tf_op jit(solution)/shard_map/pallas_call | solution.py:382
  95.1 8.6 %all-to-all-start.2 = ((f32[16,7,8,128]{3,2,1,0:T(8,128)}), f32[16,7,8,128]{3,2,1,0:T(8,128)S(1)}, u32[]{:S(2)}, u32[]{:S(2)}) async-start(f32[16,7,8,128]{3,2,1,0:T(8,128)} %shard_map.80), calls=%async_computation.2 | async-start | bytes 917504 | tf_op jit(solution)/shard_map/all_to_all | solution.py:51
  103.7 3.8 %collective-permute-start.23 = (f32[2,7,8,128]{3,2,1,0:T(8,128)S(1)}, f32[2,7,8,128]{3,2,1,0:T(8,128)S(1)}, u32[]{:S(2)}, u32[]{:S(2)}) collective-permute-start(f32[2,7,8,128]{3,2,1,0:T(8,128)S(1)} %pad_maximum_fusion.8), channel_id=1, source_target_pairs={{0,224},{16,240},{32,192},{48,208},{64,160},{80,176},{96,128},{112... | collective-permute-start | bytes 172040 | tf_op jit(solution)/shard_map/ppermute | solution.py:56
  107.5 2.2 %collective-permute-start.21 = (f32[2,7,8,128]{3,2,1,0:T(8,128)S(1)}, f32[2,7,8,128]{3,2,1,0:T(8,128)S(1)}, u32[]{:S(2)}, u32[]{:S(2)}) collective-permute-start(f32[2,7,8,128]{3,2,1,0:T(8,128)S(1)} %pad_maximum_fusion.6), channel_id=1, source_target_pairs={{0,160},{16,176},{32,128},{48,144},{64,224},{80,240},{96,192},{112... | collective-permute-start | bytes 172040 | tf_op jit(solution)/shard_map/ppermute | solution.py:56
  110.0 1.8 %collective-permute-start.19 = (f32[2,7,8,128]{3,2,1,0:T(8,128)S(1)}, f32[2,7,8,128]{3,2,1,0:T(8,128)S(1)}, u32[]{:S(2)}, u32[]{:S(2)}) collective-permute-start(f32[2,7,8,128]{3,2,1,0:T(8,128)S(1)} %pad_maximum_fusion.4), channel_id=1, source_target_pairs={{0,96},{16,112},{32,64},{48,80},{64,32},{80,48},{96,0},{112,16},{1... | collective-permute-start | bytes 172040 | tf_op jit(solution)/shard_map/ppermute | solution.py:56
  114.1 4.1 %collective-permute-done.20.refs_5_ = f32[2,7,8,128]{3,2,1,0:T(8,128)S(1)} collective-permute-done((f32[2,7,8,128]{3,2,1,0:T(8,128)S(1)}, f32[2,7,8,128]{3,2,1,0:T(8,128)S(1)}, u32[]{:S(2)}, u32[]{:S(2)}) %collective-permute-start.20) | collective-permute-done | bytes 57376 | tf_op jit(solution)/shard_map/ppermute | solution.py:56
  118.3 1.6 all-to-all-done.2.refs_0_
  120.6 4.6 %shard_map.82 = (f32[16,128,128]{2,1,0:T(8,128)}, f32[8,128,128]{2,1,0:T(8,128)}, f32[8,128,128]{2,1,0:T(8,128)}, f32[128,128]{1,0:T(8,128)}) custom-call(s32[2]{0:T(128)} %pad_add_fusion.at_ref, s32[18]{0:T(128)} %reshape.13.where_ref, s32[1]{0:T(128)} %bitcast.46.live_ref, f32[16,7,8,128]{3,2,1,0:T(8,128)} %copy-done.1, ...), custom_call_target="tpu_custom_call" | custom-call | flops 1073741824 | bytes 6291456 | tf_op jit(solution)/shard_map/pallas_call | solution.py:329
  125.3 14.1 %all-to-all-start.3 = ((f32[16,128,128]{2,1,0:T(8,128)}), f32[16,128,128]{2,1,0:T(8,128)S(1)}, u32[]{:S(2)}, u32[]{:S(2)}) async-start(f32[16,128,128]{2,1,0:T(8,128)} %get-tuple-element.28), calls=%async_computation.3 | async-start | bytes 2097152 | tf_op jit(solution)/shard_map/all_to_all | solution.py:51
  139.5 1.9 %collective-permute-done.24 = f32[8,128,128]{2,1,0:T(8,128)S(1)} collective-permute-done((f32[8,128,128]{2,1,0:T(8,128)S(1)}, f32[8,128,128]{2,1,0:T(8,128)S(1)}, u32[]{:S(2)}, u32[]{:S(2)}) %collective-permute-start.24) | collective-permute-done | bytes 524320 | tf_op jit(solution)/shard_map/ppermute | solution.py:56
  141.5 1.8 %collective-permute-start.25 = (f32[128,128]{1,0:T(8,128)S(1)}, f32[128,128]{1,0:T(8,128)S(1)}, u32[]{:S(2)}, u32[]{:S(2)}) collective-permute-start(f32[128,128]{1,0:T(8,128)S(1)} %get-tuple-element.32), channel_id=1, source_target_pairs={{0,192},{16,208},{32,224},{48,240},{64,128},{80,144},{96,160},{112... | collective-permute-start | bytes 196616 | tf_op jit(solution)/shard_map/ppermute | solution.py:56
  143.3 1.6 collective-permute-start.26
  145.0 1.7 collective-permute-start.27
  148.4 1.6 collective-permute-start.30
  150.4 1.7 collective-permute-done.28
  152.1 2.5 %collective-permute-done.29 = f32[128,128]{1,0:T(8,128)S(1)} collective-permute-done((f32[128,128]{1,0:T(8,128)S(1)}, f32[128,128]{1,0:T(8,128)S(1)}, u32[]{:S(2)}, u32[]{:S(2)}) %collective-permute-start.29) | collective-permute-done | bytes 65568 | tf_op jit(solution)/shard_map/ppermute | solution.py:56
  155.3 12.7 %all-to-all-done.3 = f32[16,128,128]{2,1,0:T(8,128)S(1)} async-done(((f32[16,128,128]{2,1,0:T(8,128)}), f32[16,128,128]{2,1,0:T(8,128)S(1)}, u32[]{:S(2)}, u32[]{:S(2)}) %all-to-all-start.3) | async-done | bytes 1048608 | tf_op jit(solution)/shard_map/all_to_all | solution.py:51
  (135 shorter events, 27.5 us)
Async XLA Ops:
  4.6 40.4 %all-to-all-start = ((f32[16,136,128]{2,1,0:T(8,128)}), f32[16,136,128]{2,1,0:T(8,128)S(1)}, u32[]{:S(2)}, u32[]{:S(2)}) async-start(f32[16,136,128]{2,1,0:T(8,128)} %get-tuple-element.17), calls=%async_computation | async-start | bytes 2228224 | tf_op jit(solution)/shard_map/all_to_all | solution.py:51
  16.8 5.1 %collective-permute-start.1 = (f32[2,136,128]{2,1,0:T(8,128)S(1)}, f32[2,136,128]{2,1,0:T(8,128)S(1)}, u32[]{:S(2)}, u32[]{:S(2)}) collective-permute-start(f32[2,136,128]{2,1,0:T(8,128)S(1)} %pad_maximum_fusion.refs_1_), channel_id=1, source_target_pairs={{0,32},{16,48},{32,0},{48,16},{64,96},{80,112},{96,64},{112,80},{1... | collective-permute-start | bytes 417800 | tf_op jit(solution)/shard_map/ppermute | solution.py:56
  18.0 8.9 %collective-permute-start.2 = (f32[2,136,128]{2,1,0:T(8,128)S(1)}, f32[2,136,128]{2,1,0:T(8,128)S(1)}, u32[]{:S(2)}, u32[]{:S(2)}) collective-permute-start(f32[2,136,128]{2,1,0:T(8,128)S(1)} %pad_maximum_fusion.refs_1_), channel_id=1, source_target_pairs={{0,64},{16,80},{32,96},{48,112},{64,0},{80,16},{96,32},{112,48},{1... | collective-permute-start | bytes 417800 | tf_op jit(solution)/shard_map/ppermute | solution.py:56
  20.5 9.0 %collective-permute-start.3 = (f32[2,136,128]{2,1,0:T(8,128)S(1)}, f32[2,136,128]{2,1,0:T(8,128)S(1)}, u32[]{:S(2)}, u32[]{:S(2)}) collective-permute-start(f32[2,136,128]{2,1,0:T(8,128)S(1)} %pad_maximum_fusion.refs_1_), channel_id=1, source_target_pairs={{0,96},{16,112},{32,64},{48,80},{64,32},{80,48},{96,0},{112,16},{1... | collective-permute-start | bytes 417800 | tf_op jit(solution)/shard_map/ppermute | solution.py:56
  20.7 8.8 %collective-permute-start.4 = (f32[2,136,128]{2,1,0:T(8,128)S(1)}, f32[2,136,128]{2,1,0:T(8,128)S(1)}, u32[]{:S(2)}, u32[]{:S(2)}) collective-permute-start(f32[2,136,128]{2,1,0:T(8,128)S(1)} %pad_maximum_fusion.refs_1_), channel_id=1, source_target_pairs={{0,128},{16,144},{32,160},{48,176},{64,192},{80,208},{96,224},{112... | collective-permute-start | bytes 417800 | tf_op jit(solution)/shard_map/ppermute | solution.py:56
  21.8 7.7 %collective-permute-start.5 = (f32[2,136,128]{2,1,0:T(8,128)S(1)}, f32[2,136,128]{2,1,0:T(8,128)S(1)}, u32[]{:S(2)}, u32[]{:S(2)}) collective-permute-start(f32[2,136,128]{2,1,0:T(8,128)S(1)} %pad_maximum_fusion.refs_1_), channel_id=1, source_target_pairs={{0,160},{16,176},{32,128},{48,144},{64,224},{80,240},{96,192},{112... | collective-permute-start | bytes 417800 | tf_op jit(solution)/shard_map/ppermute | solution.py:56
  21.9 13.1 %collective-permute-start.6 = (f32[2,136,128]{2,1,0:T(8,128)S(1)}, f32[2,136,128]{2,1,0:T(8,128)S(1)}, u32[]{:S(2)}, u32[]{:S(2)}) collective-permute-start(f32[2,136,128]{2,1,0:T(8,128)S(1)} %pad_maximum_fusion.refs_1_), channel_id=1, source_target_pairs={{0,192},{16,208},{32,224},{48,240},{64,128},{80,144},{96,160},{112... | collective-permute-start | bytes 417800 | tf_op jit(solution)/shard_map/ppermute | solution.py:56
  26.9 13.9 %collective-permute-start.7 = (f32[2,136,128]{2,1,0:T(8,128)S(1)}, f32[2,136,128]{2,1,0:T(8,128)S(1)}, u32[]{:S(2)}, u32[]{:S(2)}) collective-permute-start(f32[2,136,128]{2,1,0:T(8,128)S(1)} %pad_maximum_fusion.refs_1_), channel_id=1, source_target_pairs={{0,224},{16,240},{32,192},{48,208},{64,160},{80,176},{96,128},{112... | collective-permute-start | bytes 417800 | tf_op jit(solution)/shard_map/ppermute | solution.py:56
  50.4 17.3 %collective-permute-start.8 = (f32[8,6,8,128]{3,2,1,0:T(8,128)}, f32[8,6,8,128]{3,2,1,0:T(8,128)S(1)}, u32[]{:S(2)}, u32[]{:S(2)}) collective-permute-start(f32[8,6,8,128]{3,2,1,0:T(8,128)} %get-tuple-element.25), channel_id=1, source_target_pairs={{0,16},{16,0},{32,48},{48,32},{64,80},{80,64},{96,112},{112,96},{1... | collective-permute-start | bytes 589832 | tf_op jit(solution)/shard_map/ppermute | solution.py:56
  58.1 33.0 %all-to-all-start.1 = ((f32[16,6,8,128]{3,2,1,0:T(8,128)}), f32[16,6,8,128]{3,2,1,0:T(8,128)S(1)}, u32[]{:S(2)}, u32[]{:S(2)}) async-start(f32[16,6,8,128]{3,2,1,0:T(8,128)} %get-tuple-element.21), calls=%async_computation.1 | async-start | bytes 786432 | tf_op jit(solution)/shard_map/all_to_all | solution.py:51
  67.7 10.5 %collective-permute-start.15 = (f32[2,6,8,128]{3,2,1,0:T(8,128)S(1)}, f32[2,6,8,128]{3,2,1,0:T(8,128)S(1)}, u32[]{:S(2)}, u32[]{:S(2)}) collective-permute-start(f32[2,6,8,128]{3,2,1,0:T(8,128)S(1)} %pad_maximum_fusion.16), channel_id=1, source_target_pairs={{0,224},{16,240},{32,192},{48,208},{64,160},{80,176},{96,128},{112... | collective-permute-start | bytes 147464 | tf_op jit(solution)/shard_map/ppermute | solution.py:56
  73.9 6.2 %collective-permute-start.14 = (f32[2,6,8,128]{3,2,1,0:T(8,128)S(1)}, f32[2,6,8,128]{3,2,1,0:T(8,128)S(1)}, u32[]{:S(2)}, u32[]{:S(2)}) collective-permute-start(f32[2,6,8,128]{3,2,1,0:T(8,128)S(1)} %pad_maximum_fusion.15), channel_id=1, source_target_pairs={{0,192},{16,208},{32,224},{48,240},{64,128},{80,144},{96,160},{112... | collective-permute-start | bytes 147464 | tf_op jit(solution)/shard_map/ppermute | solution.py:56
  73.9 6.8 %collective-permute-start.13 = (f32[2,6,8,128]{3,2,1,0:T(8,128)S(1)}, f32[2,6,8,128]{3,2,1,0:T(8,128)S(1)}, u32[]{:S(2)}, u32[]{:S(2)}) collective-permute-start(f32[2,6,8,128]{3,2,1,0:T(8,128)S(1)} %pad_maximum_fusion.14), channel_id=1, source_target_pairs={{0,160},{16,176},{32,128},{48,144},{64,224},{80,240},{96,192},{112... | collective-permute-start | bytes 147464 | tf_op jit(solution)/shard_map/ppermute | solution.py:56
  74.9 7.4 %collective-permute-start.12 = (f32[2,6,8,128]{3,2,1,0:T(8,128)S(1)}, f32[2,6,8,128]{3,2,1,0:T(8,128)S(1)}, u32[]{:S(2)}, u32[]{:S(2)}) collective-permute-start(f32[2,6,8,128]{3,2,1,0:T(8,128)S(1)} %pad_maximum_fusion.13), channel_id=1, source_target_pairs={{0,128},{16,144},{32,160},{48,176},{64,192},{80,208},{96,224},{112... | collective-permute-start | bytes 147464 | tf_op jit(solution)/shard_map/ppermute | solution.py:56
  75.8 6.5 %collective-permute-start.11 = (f32[2,6,8,128]{3,2,1,0:T(8,128)S(1)}, f32[2,6,8,128]{3,2,1,0:T(8,128)S(1)}, u32[]{:S(2)}, u32[]{:S(2)}) collective-permute-start(f32[2,6,8,128]{3,2,1,0:T(8,128)S(1)} %pad_maximum_fusion.12), channel_id=1, source_target_pairs={{0,96},{16,112},{32,64},{48,80},{64,32},{80,48},{96,0},{112,16},{1... | collective-permute-start | bytes 147464 | tf_op jit(solution)/shard_map/ppermute | solution.py:56
  78.2 4.5 %collective-permute-start.10 = (f32[2,6,8,128]{3,2,1,0:T(8,128)S(1)}, f32[2,6,8,128]{3,2,1,0:T(8,128)S(1)}, u32[]{:S(2)}, u32[]{:S(2)}) collective-permute-start(f32[2,6,8,128]{3,2,1,0:T(8,128)S(1)} %pad_maximum_fusion.11), channel_id=1, source_target_pairs={{0,64},{16,80},{32,96},{48,112},{64,0},{80,16},{96,32},{112,48},{1... | collective-permute-start | bytes 147464 | tf_op jit(solution)/shard_map/ppermute | solution.py:56
  95.1 24.8 %all-to-all-start.2 = ((f32[16,7,8,128]{3,2,1,0:T(8,128)}), f32[16,7,8,128]{3,2,1,0:T(8,128)S(1)}, u32[]{:S(2)}, u32[]{:S(2)}) async-start(f32[16,7,8,128]{3,2,1,0:T(8,128)} %shard_map.80), calls=%async_computation.2 | async-start | bytes 917504 | tf_op jit(solution)/shard_map/all_to_all | solution.py:51
  103.7 8.1 %collective-permute-start.23 = (f32[2,7,8,128]{3,2,1,0:T(8,128)S(1)}, f32[2,7,8,128]{3,2,1,0:T(8,128)S(1)}, u32[]{:S(2)}, u32[]{:S(2)}) collective-permute-start(f32[2,7,8,128]{3,2,1,0:T(8,128)S(1)} %pad_maximum_fusion.8), channel_id=1, source_target_pairs={{0,224},{16,240},{32,192},{48,208},{64,160},{80,176},{96,128},{112... | collective-permute-start | bytes 172040 | tf_op jit(solution)/shard_map/ppermute | solution.py:56
  107.5 6.0 %collective-permute-start.22 = (f32[2,7,8,128]{3,2,1,0:T(8,128)S(1)}, f32[2,7,8,128]{3,2,1,0:T(8,128)S(1)}, u32[]{:S(2)}, u32[]{:S(2)}) collective-permute-start(f32[2,7,8,128]{3,2,1,0:T(8,128)S(1)} %pad_maximum_fusion.7), channel_id=1, source_target_pairs={{0,192},{16,208},{32,224},{48,240},{64,128},{80,144},{96,160},{112... | collective-permute-start | bytes 172040 | tf_op jit(solution)/shard_map/ppermute | solution.py:56
  107.5 6.6 %collective-permute-start.21 = (f32[2,7,8,128]{3,2,1,0:T(8,128)S(1)}, f32[2,7,8,128]{3,2,1,0:T(8,128)S(1)}, u32[]{:S(2)}, u32[]{:S(2)}) collective-permute-start(f32[2,7,8,128]{3,2,1,0:T(8,128)S(1)} %pad_maximum_fusion.6), channel_id=1, source_target_pairs={{0,160},{16,176},{32,128},{48,144},{64,224},{80,240},{96,192},{112... | collective-permute-start | bytes 172040 | tf_op jit(solution)/shard_map/ppermute | solution.py:56
  109.8 8.5 %collective-permute-start.20 = (f32[2,7,8,128]{3,2,1,0:T(8,128)S(1)}, f32[2,7,8,128]{3,2,1,0:T(8,128)S(1)}, u32[]{:S(2)}, u32[]{:S(2)}) collective-permute-start(f32[2,7,8,128]{3,2,1,0:T(8,128)S(1)} %pad_maximum_fusion.5), channel_id=1, source_target_pairs={{0,128},{16,144},{32,160},{48,176},{64,192},{80,208},{96,224},{112... | collective-permute-start | bytes 172040 | tf_op jit(solution)/shard_map/ppermute | solution.py:56
  110.0 8.3 %collective-permute-start.19 = (f32[2,7,8,128]{3,2,1,0:T(8,128)S(1)}, f32[2,7,8,128]{3,2,1,0:T(8,128)S(1)}, u32[]{:S(2)}, u32[]{:S(2)}) collective-permute-start(f32[2,7,8,128]{3,2,1,0:T(8,128)S(1)} %pad_maximum_fusion.4), channel_id=1, source_target_pairs={{0,96},{16,112},{32,64},{48,80},{64,32},{80,48},{96,0},{112,16},{1... | collective-permute-start | bytes 172040 | tf_op jit(solution)/shard_map/ppermute | solution.py:56
  111.8 6.4 %collective-permute-start.18 = (f32[2,7,8,128]{3,2,1,0:T(8,128)S(1)}, f32[2,7,8,128]{3,2,1,0:T(8,128)S(1)}, u32[]{:S(2)}, u32[]{:S(2)}) collective-permute-start(f32[2,7,8,128]{3,2,1,0:T(8,128)S(1)} %pad_maximum_fusion.3), channel_id=1, source_target_pairs={{0,64},{16,80},{32,96},{48,112},{64,0},{80,16},{96,32},{112,48},{1... | collective-permute-start | bytes 172040 | tf_op jit(solution)/shard_map/ppermute | solution.py:56
  113.5 4.8 %collective-permute-start.17 = (f32[2,7,8,128]{3,2,1,0:T(8,128)S(1)}, f32[2,7,8,128]{3,2,1,0:T(8,128)S(1)}, u32[]{:S(2)}, u32[]{:S(2)}) collective-permute-start(f32[2,7,8,128]{3,2,1,0:T(8,128)S(1)} %pad_maximum_fusion.2), channel_id=1, source_target_pairs={{0,32},{16,48},{32,0},{48,16},{64,96},{80,112},{96,64},{112,80},{1... | collective-permute-start | bytes 172040 | tf_op jit(solution)/shard_map/ppermute | solution.py:56
  125.3 42.7 %all-to-all-start.3 = ((f32[16,128,128]{2,1,0:T(8,128)}), f32[16,128,128]{2,1,0:T(8,128)S(1)}, u32[]{:S(2)}, u32[]{:S(2)}) async-start(f32[16,128,128]{2,1,0:T(8,128)} %get-tuple-element.28), calls=%async_computation.3 | async-start | bytes 2097152 | tf_op jit(solution)/shard_map/all_to_all | solution.py:51
  141.5 6.9 %collective-permute-start.25 = (f32[128,128]{1,0:T(8,128)S(1)}, f32[128,128]{1,0:T(8,128)S(1)}, u32[]{:S(2)}, u32[]{:S(2)}) collective-permute-start(f32[128,128]{1,0:T(8,128)S(1)} %get-tuple-element.32), channel_id=1, source_target_pairs={{0,192},{16,208},{32,224},{48,240},{64,128},{80,144},{96,160},{112... | collective-permute-start | bytes 196616 | tf_op jit(solution)/shard_map/ppermute | solution.py:56
  143.3 6.7 %collective-permute-start.26 = (f32[128,128]{1,0:T(8,128)S(1)}, f32[128,128]{1,0:T(8,128)S(1)}, u32[]{:S(2)}, u32[]{:S(2)}) collective-permute-start(f32[128,128]{1,0:T(8,128)S(1)} %get-tuple-element.38), channel_id=1, source_target_pairs={{0,224},{16,240},{32,192},{48,208},{64,160},{80,176},{96,128},{112... | collective-permute-start | bytes 196616 | tf_op jit(solution)/shard_map/ppermute | solution.py:56
  145.0 5.5 %collective-permute-start.27 = (f32[128,128]{1,0:T(8,128)S(1)}, f32[128,128]{1,0:T(8,128)S(1)}, u32[]{:S(2)}, u32[]{:S(2)}) collective-permute-start(f32[128,128]{1,0:T(8,128)S(1)} %get-tuple-element.37), channel_id=1, source_target_pairs={{0,160},{16,176},{32,128},{48,144},{64,224},{80,240},{96,192},{112... | collective-permute-start | bytes 196616 | tf_op jit(solution)/shard_map/ppermute | solution.py:56
  146.6 5.5 %collective-permute-start.28 = (f32[128,128]{1,0:T(8,128)S(1)}, f32[128,128]{1,0:T(8,128)S(1)}, u32[]{:S(2)}, u32[]{:S(2)}) collective-permute-start(f32[128,128]{1,0:T(8,128)S(1)} %get-tuple-element.36), channel_id=1, source_target_pairs={{0,64},{16,80},{32,96},{48,112},{64,0},{80,16},{96,32},{112,48},{1... | collective-permute-start | bytes 196616 | tf_op jit(solution)/shard_map/ppermute | solution.py:56
  148.1 6.5 %collective-permute-start.29 = (f32[128,128]{1,0:T(8,128)S(1)}, f32[128,128]{1,0:T(8,128)S(1)}, u32[]{:S(2)}, u32[]{:S(2)}) collective-permute-start(f32[128,128]{1,0:T(8,128)S(1)} %get-tuple-element.35), channel_id=1, source_target_pairs={{0,128},{16,144},{32,160},{48,176},{64,192},{80,208},{96,224},{112... | collective-permute-start | bytes 196616 | tf_op jit(solution)/shard_map/ppermute | solution.py:56
  148.4 6.2 %collective-permute-start.30 = (f32[128,128]{1,0:T(8,128)S(1)}, f32[128,128]{1,0:T(8,128)S(1)}, u32[]{:S(2)}, u32[]{:S(2)}) collective-permute-start(f32[128,128]{1,0:T(8,128)S(1)} %get-tuple-element.34), channel_id=1, source_target_pairs={{0,96},{16,112},{32,64},{48,80},{64,32},{80,48},{96,0},{112,16},{1... | collective-permute-start | bytes 196616 | tf_op jit(solution)/shard_map/ppermute | solution.py:56
  150.0 4.6 %collective-permute-start.31 = (f32[128,128]{1,0:T(8,128)S(1)}, f32[128,128]{1,0:T(8,128)S(1)}, u32[]{:S(2)}, u32[]{:S(2)}) collective-permute-start(f32[128,128]{1,0:T(8,128)S(1)} %get-tuple-element.33), channel_id=1, source_target_pairs={{0,32},{16,48},{32,0},{48,16},{64,96},{80,112},{96,64},{112,80},{1... | collective-permute-start | bytes 196616 | tf_op jit(solution)/shard_map/ppermute | solution.py:56
  (34 other events, 240.2 us)

commit v3 on v2

v3 whole, which is shorter than its diff:
```python
import functools

import jax
import jax.numpy as jnp
from jax import lax
from jax.experimental import pallas as pl
from jax.experimental.pallas import tpu as pltpu
from jax.sharding import PartitionSpec as P


STEPS = 2
step_rate = 0.004


vmem = pl.BlockSpec(memory_space=pltpu.VMEM)
smem = pl.BlockSpec(memory_space=pltpu.SMEM)
anywhere = pl.BlockSpec(memory_space=pl.ANY)
small_cost = pl.CostEstimate(flops=1 << 20, bytes_accessed=1 << 20, transcendentals=0)
parts = 2
chip_order = (6, 7, 5, 2, 4, 3, 1)


def shape_of(*sizes):
    return jax.ShapeDtypeStruct(sizes, jnp.float32)


def rows_at(index, rows):
    return pl.ds(pl.multiple_of(index * rows, rows), rows)


def split(value):
    high = value.astype(jnp.bfloat16)
    low = (value - high.astype(jnp.float32)).astype(jnp.bfloat16)
    return high, low


def two_halves(value):
    high, low = split(value)
    return jnp.concatenate([high, low], axis=1)


def pair_table(value):
    row = two_halves(value)
    return jnp.concatenate([row, row], axis=0)


def fold(product):
    return product[:, :128] + product[:, 128:]


def near(value):
    return pltpu.with_memory_space_constraint(value, pltpu.VMEM)


def swap_col(sent):
    return lax.all_to_all(sent, "col", 0, 0, tiled=True)


def shift_row(value, change):
    members = lax.axis_size("row")
    return lax.ppermute(value, "row", [(member, member ^ change) for member in range(members)])


def swap_row(even, odd):
    passed = shift_row(odd, 1)
    both = [jnp.stack([even[pair], passed[pair]]) for pair in range(even.shape[0])]
    got = [both[0]] + [None] * len(chip_order)
    for pair in chip_order:
        got[pair] = shift_row(both[pair], 2 * pair)
    return got


def open_kernel(where_ref, live_ref, a_ref, b_ref, send_a, send_b):
    slots = where_ref.shape[3]
    side, rank = a_ref.shape
    members = send_a.shape[0]
    rows = send_b.shape[0] - side
    lane = lax.broadcasted_iota(jnp.int32, (rows, rank), 1)

    def note(kind):
        value = jnp.zeros((rows, rank), jnp.float32)
        for slot in range(slots):
            named = jnp.where(slot < live_ref[0, 0], where_ref[kind, 0, 0, slot], members).astype(jnp.float32)
            value = jnp.where(lane == slot, named, value)
        return value

    send_b[:side] = b_ref[...]
    send_b[side:] = note(1)
    block, named = a_ref[...], note(0)
    for member in range(members):
        send_a[member, :side] = block
        send_a[member, side:] = named


def open_blocks(where, live, factor_a, factor_b, members):
    side, rank = factor_a.shape
    rows = side // members
    return pl.pallas_call(
        open_kernel,
        out_shape=(shape_of(members, side + rows, rank), shape_of(side + rows, rank)),
        in_specs=[smem, smem, vmem, vmem],
        out_specs=(vmem, vmem),
        cost_estimate=small_cost,
    )(where, live, factor_a, factor_b)


def slot_gradients(piece_a, piece_b, piece_c, observed):
    depth, (side, rank) = piece_c.shape[0], piece_a.shape
    b_high, b_low = split(piece_b)
    b_rows = jnp.concatenate(
        [jnp.concatenate([b_high, b_high], axis=1), jnp.concatenate([b_low, b_low], axis=1)], axis=0
    )
    b_table, a_table = pair_table(piece_b), pair_table(piece_a)
    counted = observed()
    grad_a = grad_b = jnp.zeros((side, rank), jnp.float32)
    each = depth // parts
    for part in range(parts):
        own = slice(part * each, (part + 1) * each)
        part_c = piece_c[own][:, None, :]
        scaled_a = (part_c * piece_a[None, :, :]).reshape(each * side, rank)
        model = fold(
            lax.dot_general(
                two_halves(scaled_a), b_rows, (((1,), (1,)), ((), ())), preferred_element_type=jnp.float32
            )
        )
        residual = jnp.exp(model) - counted[own].reshape(each * side, side).astype(jnp.float32)
        along_b = fold(jnp.dot(two_halves(residual), b_table, preferred_element_type=jnp.float32))
        turned = jnp.swapaxes(residual.reshape(each, side, side), 1, 2).reshape(each * side, side)
        along_a = fold(jnp.dot(two_halves(turned), a_table, preferred_element_type=jnp.float32))
        grad_a += (along_b.reshape(each, side, rank) * part_c).sum(0)
        grad_b += (along_a.reshape(each, side, rank) * part_c).sum(0)
    return grad_a, grad_b


class Fetches:
    def __init__(self, where_ref, live_ref, c_ref, counts_ref, part_c, seen, sems):
        self.refs = where_ref, live_ref, c_ref, counts_ref, part_c, seen, sems
        self.slots, self.depth = counts_ref.shape[:2]

    def copy_c(self, slot):
        where_ref, _, c_ref, _, part_c, _, sems = self.refs
        start_c = pl.multiple_of(where_ref[2, 0, 0, slot] * self.depth, self.depth)
        return pltpu.make_async_copy(c_ref.at[pl.ds(start_c, self.depth)], part_c.at[slot], sems.at[0, slot])

    def copy_counts(self, slot):
        _, _, _, counts_ref, _, seen, sems = self.refs
        return pltpu.make_async_copy(counts_ref.at[slot], seen.at[slot], sems.at[1, slot])

    def start(self):
        for slot in range(self.slots):

            @pl.when(slot < self.refs[1][0, 0])
            def _():
                self.copy_c(slot).start()
                self.copy_counts(slot).start()

    def factor(self, slot):
        self.copy_c(slot).wait()
        return self.refs[4][slot]

    def observed(self, slot):
        self.copy_counts(slot).wait()
        return self.refs[5][slot]


def first_kernel(at_ref, where_ref, live_ref, *refs):
    a_ref, b_refs, (c_ref, counts_ref), refs = refs[0], refs[1:9], refs[9:11], refs[11:]
    ga_ref, gb_refs, refs = refs[0], refs[1:3], refs[3:]
    block_a, all_b, turned_b, part_c, seen, sems, sem_a, sem_b = refs
    slots, _, side, rank = counts_ref.shape
    members = a_ref.shape[0]
    rows = side // members
    live = live_ref[0, 0]
    fetches = Fetches(where_ref, live_ref, c_ref, counts_ref, part_c, seen, sems)

    def fetch_a(slot):
        return pltpu.make_async_copy(a_ref.at[where_ref[0, 0, 0, slot], pl.ds(0, side)], block_a.at[slot], sem_a.at[slot])

    copies_b = [
        pltpu.make_async_copy(ref.at[:, pl.ds(0, side)], all_b.at[pl.ds(2 * pair, 2)], sem_b.at[pair])
        for pair, ref in enumerate(b_refs)
    ]
    for slot in range(slots):

        @pl.when(slot < live)
        def _():
            fetch_a(slot).start()

    for copy in copies_b:
        copy.start()
    fetches.start()
    for copy in copies_b:
        copy.wait()

    def visit(slot, carry):
        fetch_a(slot).wait()
        piece_b = all_b[where_ref[1, 0, 0, slot] ^ at_ref[0]]
        grad_a, grad_b = slot_gradients(
            block_a[slot], piece_b, fetches.factor(slot), functools.partial(fetches.observed, slot)
        )
        ga_ref[:, slot] = grad_a.reshape(members, rows, rank)
        turned_b[...] = grad_b
        for place in range(members):
            gb_refs[place % 2][place // 2, slot] = turned_b[rows_at(at_ref[0] ^ place, rows), :]
        return carry

    lax.fori_loop(0, live, visit, 0)

    def clear(slot, carry):
        ga_ref[:, slot] = jnp.zeros((members, rows, rank), jnp.float32)
        for ref in gb_refs:
            ref[:, slot] = jnp.zeros((members // 2, rows, rank), jnp.float32)
        return carry

    lax.fori_loop(live, slots, clear, 0)


def last_kernel(at_ref, where_ref, live_ref, *refs):
    a_ref, b_refs, (c_ref, counts_ref), refs = refs[0], refs[1:9], refs[9:11], refs[11:]
    ga_ref, even_ref, odd_ref, base_b, refs = *refs[:4], refs[4:]
    block_a, all_b, block_b, part_c, seen, sems, sem_b = refs
    slots, _, side, rank = counts_ref.shape
    members = a_ref.shape[0]
    rows = side // members
    live = live_ref[0, 0]
    me = at_ref[0]
    fetches = Fetches(where_ref, live_ref, c_ref, counts_ref, part_c, seen, sems)
    copies = [pltpu.make_async_copy(a_ref, block_a, sem_b.at[8])]
    for pair, ref in enumerate(b_refs):
        copies.append(pltpu.make_async_copy(ref, all_b.at[pl.ds(2 * pair, 2)], sem_b.at[pair]))
    for copy in copies:
        copy.start()
    fetches.start()
    for ref in (ga_ref, even_ref, odd_ref):
        ref[...] = jnp.zeros_like(ref)
    for copy in copies:
        copy.wait()
    for place in range(members):
        base_b[rows_at(me ^ place, rows), :] = all_b[place, slots]

    def visit(slot, carry):
        for place in range(members):
            block_b[rows_at(me ^ place, rows), :] = all_b[place, slot]
        grad_a, grad_b = slot_gradients(
            block_a[:, slot].reshape(side, rank),
            block_b[...],
            fetches.factor(slot),
            functools.partial(fetches.observed, slot),
        )
        ga_ref[where_ref[0, 0, 0, slot]] += grad_a
        place = where_ref[1, 0, 0, slot] ^ me

        @pl.when(place % 2 == 0)
        def _():
            even_ref[place // 2] += grad_b

        @pl.when(place % 2 == 1)
        def _():
            odd_ref[place // 2] += grad_b

        return carry

    lax.fori_loop(0, live, visit, 0)


def block_gradients(at, where, live, held_a, held_b, c, counts, members, last):
    slots, depth, side, rank = counts.shape
    rows = side // members
    common = [
        pltpu.VMEM((slots, depth, rank), jnp.float32),
        pltpu.VMEM(counts.shape, jnp.int32),
        pltpu.SemaphoreType.DMA((2, slots)),
    ]
    if last:
        kernel = last_kernel
        half = shape_of(members // 2, side, rank)
        shapes = (shape_of(members, side, rank), half, half, shape_of(side, rank))
        scratch = [
            pltpu.VMEM(held_a.shape, jnp.float32),
            pltpu.VMEM((members, *held_b[0].shape[1:]), jnp.float32),
            pltpu.VMEM((side, rank), jnp.float32),
            *common,
            pltpu.SemaphoreType.DMA((9,)),
        ]
    else:
        kernel = first_kernel
        half = shape_of(members // 2, slots, rows, rank)
        shapes = (shape_of(members, slots, rows, rank), half, half)
        scratch = [
            pltpu.VMEM((slots, side, rank), jnp.float32),
            pltpu.VMEM((members, side, rank), jnp.float32),
            pltpu.VMEM((side, rank), jnp.float32),
            *common,
            pltpu.SemaphoreType.DMA((slots,)),
            pltpu.SemaphoreType.DMA((8,)),
        ]
    return pl.pallas_call(
        kernel,
        out_shape=shapes,
        in_specs=[smem] * 3 + [anywhere] * 11,
        out_specs=[vmem] * len(shapes),
        scratch_shapes=scratch,
        cost_estimate=pl.CostEstimate(flops=1 << 30, bytes_accessed=6 << 20, transcendentals=1 << 20),
    )(at, where, live, near(held_a), *map(near, held_b), c, counts)


def name_of(notes, side, place, slot):
    return notes[side, place, slot].astype(jnp.int32)


def update_kernel(at_ref, *refs):
    all_refs, back_refs, outs, refs = refs[:9], refs[9:18], refs[18:21], refs[21:]
    grads, pieces, totals, notes, sems = refs
    members, slots, rows, _ = grads.shape[1:]
    side = members * rows
    copies = []
    for index in range(9):
        kind = 0 if index == 0 else 1
        to = pl.ds(0, members) if index == 0 else pl.ds(2 * (index - 1), 2)
        at = rows_at(at_ref[1 - kind], rows)
        copies.append(pltpu.make_async_copy(all_refs[index].at[:, side], notes.at[kind, to], sems.at[0, index]))
        copies.append(pltpu.make_async_copy(back_refs[index], grads.at[kind, to], sems.at[1, index]))
        copies.append(pltpu.make_async_copy(all_refs[index].at[:, at], pieces.at[kind, to], sems.at[2, index]))
    for copy in copies:
        copy.start()
    totals[...] = jnp.zeros_like(totals)
    for copy in copies:
        copy.wait()

    def gather(place, carry):
        for slot in range(slots):
            for kind in range(2):
                block = name_of(notes, kind, place, slot)
                totals[kind, block] = totals[kind, block] + grads[kind, place, slot]
        return carry

    lax.fori_loop(0, members, gather, 0)
    totals[0, :members] = pieces[0] - step_rate * totals[0, :members]
    for place in range(members):
        owner = at_ref[0] ^ place
        totals[1, owner] = pieces[1, place] - step_rate * totals[1, owner]

    def deal(index, carry):
        for way in range(2):
            place = 2 * index + way
            for slot in range(slots):
                outs[0][place, slot] = totals[0, jnp.minimum(name_of(notes, 0, place, slot), members - 1)]
                outs[1 + way][index, slot] = totals[1, jnp.minimum(name_of(notes, 1, place, slot), members - 1)]
            outs[0][place, slots] = totals[0, place]
            outs[1 + way][index, slots] = totals[1, at_ref[0] ^ place]
        return carry

    lax.fori_loop(0, members // 2, deal, 0)


def update(at, all_a, all_b, back_a, back_b):
    members, slots, rows, rank = back_a.shape
    half = shape_of(members // 2, slots + 1, rows, rank)
    return pl.pallas_call(
        update_kernel,
        out_shape=(shape_of(members, slots + 1, rows, rank), half, half),
        in_specs=[smem] + [anywhere] * 18,
        out_specs=(vmem, vmem, vmem),
        scratch_shapes=[
            pltpu.VMEM((2, members, slots, rows, rank), jnp.float32),
            pltpu.VMEM((2, members, rows, rank), jnp.float32),
            pltpu.VMEM((2, members + 1, rows, rank), jnp.float32),
            pltpu.SMEM((2, members, rank), jnp.float32),
            pltpu.SemaphoreType.DMA((3, 9)),
        ],
        cost_estimate=small_cost,
    )(at, *map(near, (all_a, *all_b, back_a, *back_b)))


def local(counts, block_coords, block_count, factor_a, factor_b, factor_c):
    assert STEPS == 2
    slots = counts.shape[2]
    members = lax.axis_size("row")
    side, rank = factor_a.shape
    at = jnp.stack([lax.axis_index("row"), lax.axis_index("col")]).astype(jnp.int32)
    where, live = block_coords, block_count
    counts = counts.reshape(counts.shape[2:])
    send_a, send_b = open_blocks(where, live, factor_a, factor_b, members)
    all_a = swap_col(send_a)
    both = jnp.stack([send_b, shift_row(send_b, 1)])
    all_b = [both] + [None] * len(chip_order)
    for pair in chip_order:
        all_b[pair] = shift_row(both, 2 * pair)
    grad_a, *grad_b = block_gradients(
        at, where, live, all_a, all_b, factor_c, counts, members, False
    )
    back_a = swap_col(grad_a)
    back_b = swap_row(*grad_b)
    dealt_a, *dealt_b = update(at, all_a, all_b, back_a, back_b)
    held_a = swap_col(dealt_a)
    held_b = swap_row(*dealt_b)
    grad_a, even_b, odd_b, base_b = block_gradients(at, where, live, held_a, held_b, factor_c, counts, members, True)
    terms_a = swap_col(grad_a)
    sums = even_b + shift_row(odd_b, 1)
    terms_b = [sums[0]]
    for pair in chip_order:
        terms_b.append(shift_row(sums[pair], 2 * pair))
    new_b = base_b - step_rate * sum(terms_b)
    new_a = held_a[:, slots].reshape(side, rank) - step_rate * terms_a.sum(0)
    return (new_a, new_b)


def solution(mesh):
    return jax.shard_map(
        local,
        mesh=mesh,
        in_specs=(
            P("row", "col", None, None, None, None),
            P(None, "row", "col", None),
            P("row", "col"),
            P(("row", "col"), None),
            P(("col", "row"), None),
            P(),
        ),
        out_specs=(P(("row", "col"), None), P(("col", "row"), None)),
        check_vma=False,
    )
```

time: 171 us -> 158 us (0.924)
  the two profiles are of different devices: /device:TPU:9 before, /device:TPU:8 now
where the time goes in v3:
time: 158 us
  starting transfers between devices  90.5 us (57%)
  waiting for transfers between devices  40.6 us (26%)
  Pallas kernels  20.9 us (13%)
  other arithmetic  2.16 us (1%)
  local copies, waits for them, and re-layouts  1.85 us (1%)
  between operations  1.6 us (1%)
    ppermute x32, starting transfers between devices, shift_row(): lax.ppermute(value, 'row', [(member, member ^ change) for member in range...  55.9 us
    all_to_all x4, starting transfers between devices, swap_col(): return lax.all_to_all(sent, 'col', 0, 0, tiled=True)  34.6 us
    ppermute x32, waiting for transfers between devices, shift_row(): lax.ppermute(value, 'row', [(member, member ^ change) for member in range...  27 us
    pallas_call x2, Pallas kernels, block_gradients(): pl.pallas_call(kernel, out_shape=shapes, in_specs=[smem] * 3 + [anywhere]...  14.3 us
    all_to_all x4, waiting for transfers between devices, swap_col(): return lax.all_to_all(sent, 'col', 0, 0, tiled=True)  13.5 us
    pallas_call x1, Pallas kernels, update(): pl.pallas_call(update_kernel, out_shape=(shape_of(members, slots + 1, row...  4.63 us
  transfers between devices with their start and end apart: 36, of which 15 were waited for; matrix products, arithmetic and copies ran while one was open for 2% of the time, Pallas kernels for 0%

profile of v3, /device:TPU:8, one launch (start us, length us, event | category | flops | bytes accessed | tf_op | source)
XLA Modules:
  0.0 157.6 jit_solution(9859769924226608358)
XLA Ops:
  1.3 2.0 %shard_map.77 = (f32[16,136,128]{2,1,0:T(8,128)}, f32[136,128]{1,0:T(8,128)}) custom-call(s32[3,1,1,6]{3,2,1,0:T(1,128)} %where_ref.5, s32[1,1]{1,0:T(1,128)S(6)} %copy.8.live_ref, f32[128,128]{1,0:T(8,128)} %a_ref.1, f32[128,128]{1,0:T(8,128)} %b_ref.1), custom_call_target="tpu_custom_call" | custom-call | flops 1048576 | bytes 1048576 | tf_op jit(solution)/shard_map/pallas_call | solution.py:98
  3.3 10.4 %all-to-all-start = ((f32[16,136,128]{2,1,0:T(8,128)}), f32[16,136,128]{2,1,0:T(8,128)S(1)}, u32[]{:S(2)}, u32[]{:S(2)}) async-start(f32[16,136,128]{2,1,0:T(8,128)} %get-tuple-element.14), calls=%async_computation | async-start | bytes 2228224 | tf_op jit(solution)/shard_map/all_to_all | solution.py:56
  15.1 3.6 %collective-permute-start.7 = (f32[2,136,128]{2,1,0:T(8,128)S(1)}, f32[2,136,128]{2,1,0:T(8,128)S(1)}, u32[]{:S(2)}, u32[]{:S(2)}) collective-permute-start(f32[2,136,128]{2,1,0:T(8,128)S(1)} %pad_maximum_fusion.refs_1_), channel_id=1, source_target_pairs={{0,224},{16,240},{32,192},{48,208},{64,160},{80,176},{96,128},{112... | collective-permute-start | bytes 417800 | tf_op jit(solution)/shard_map/ppermute | solution.py:61
  21.6 2.8 %collective-permute-start.3 = (f32[2,136,128]{2,1,0:T(8,128)S(1)}, f32[2,136,128]{2,1,0:T(8,128)S(1)}, u32[]{:S(2)}, u32[]{:S(2)}) collective-permute-start(f32[2,136,128]{2,1,0:T(8,128)S(1)} %pad_maximum_fusion.refs_1_), channel_id=1, source_target_pairs={{0,96},{16,112},{32,64},{48,80},{64,32},{80,48},{96,0},{112,16},{1... | collective-permute-start | bytes 417800 | tf_op jit(solution)/shard_map/ppermute | solution.py:61
  24.4 1.8 %collective-permute-done.7.refs_8_ = f32[2,136,128]{2,1,0:T(8,128)S(1)} collective-permute-done((f32[2,136,128]{2,1,0:T(8,128)S(1)}, f32[2,136,128]{2,1,0:T(8,128)S(1)}, u32[]{:S(2)}, u32[]{:S(2)}) %collective-permute-start.7) | collective-permute-done | bytes 139296 | tf_op jit(solution)/shard_map/ppermute | solution.py:61
  26.2 2.0 %collective-permute-start.2 = (f32[2,136,128]{2,1,0:T(8,128)S(1)}, f32[2,136,128]{2,1,0:T(8,128)S(1)}, u32[]{:S(2)}, u32[]{:S(2)}) collective-permute-start(f32[2,136,128]{2,1,0:T(8,128)S(1)} %pad_maximum_fusion.refs_1_), channel_id=1, source_target_pairs={{0,64},{16,80},{32,96},{48,112},{64,0},{80,16},{96,32},{112,48},{1... | collective-permute-start | bytes 417800 | tf_op jit(solution)/shard_map/ppermute | solution.py:61
  29.1 3.1 %collective-permute-start.1 = (f32[2,136,128]{2,1,0:T(8,128)S(1)}, f32[2,136,128]{2,1,0:T(8,128)S(1)}, u32[]{:S(2)}, u32[]{:S(2)}) collective-permute-start(f32[2,136,128]{2,1,0:T(8,128)S(1)} %pad_maximum_fusion.refs_1_), channel_id=1, source_target_pairs={{0,32},{16,48},{32,0},{48,16},{64,96},{80,112},{96,64},{112,80},{1... | collective-permute-start | bytes 417800 | tf_op jit(solution)/shard_map/ppermute | solution.py:61
  32.8 4.5 %collective-permute-done.4.refs_5_ = f32[2,136,128]{2,1,0:T(8,128)S(1)} collective-permute-done((f32[2,136,128]{2,1,0:T(8,128)S(1)}, f32[2,136,128]{2,1,0:T(8,128)S(1)}, u32[]{:S(2)}, u32[]{:S(2)}) %collective-permute-start.4) | collective-permute-done | bytes 139296 | tf_op jit(solution)/shard_map/ppermute | solution.py:61
  37.3 6.8 %all-to-all-done.refs_0_ = f32[16,136,128]{2,1,0:T(8,128)S(1)} async-done(((f32[16,136,128]{2,1,0:T(8,128)}), f32[16,136,128]{2,1,0:T(8,128)S(1)}, u32[]{:S(2)}, u32[]{:S(2)}) %all-to-all-start) | async-done | bytes 1114144 | tf_op jit(solution)/shard_map/all_to_all | solution.py:56
  44.1 7.1 %shard_map.78 = (f32[16,6,8,128]{3,2,1,0:T(8,128)}, f32[8,6,8,128]{3,2,1,0:T(8,128)}, f32[8,6,8,128]{3,2,1,0:T(8,128)}) custom-call(s32[2]{0:T(128)} %pad_add_fusion.at_ref, s32[3,1,1,6]{3,2,1,0:T(1,128)} %where_ref.5, s32[1,1]{1,0:T(1,128)S(6)} %copy.8.live_ref, f32[16,136,128]{2,1,0:T(8,128)S(1)} %all-to-all-done.refs_0_, ...), custom_call_target="tpu_custom_call" | custom-call | flops 1073741824 | bytes 6291456 | tf_op jit(solution)/shard_map/pallas_call | solution.py:297
  51.2 7.5 %all-to-all-start.1 = ((f32[16,6,8,128]{3,2,1,0:T(8,128)}), f32[16,6,8,128]{3,2,1,0:T(8,128)S(1)}, u32[]{:S(2)}, u32[]{:S(2)}) async-start(f32[16,6,8,128]{3,2,1,0:T(8,128)} %get-tuple-element.16), calls=%async_computation.1 | async-start | bytes 786432 | tf_op jit(solution)/shard_map/all_to_all | solution.py:56
  58.7 2.2 %collective-permute-start.8 = (f32[8,6,8,128]{3,2,1,0:T(8,128)}, f32[8,6,8,128]{3,2,1,0:T(8,128)S(1)}, u32[]{:S(2)}, u32[]{:S(2)}) collective-permute-start(f32[8,6,8,128]{3,2,1,0:T(8,128)} %get-tuple-element.18), channel_id=1, source_target_pairs={{0,16},{16,0},{32,48},{48,32},{64,80},{80,64},{96,112},{112,96},{1... | collective-permute-start | bytes 589832 | tf_op jit(solution)/shard_map/ppermute | solution.py:61
  62.3 4.0 %collective-permute-start.10 = (f32[2,6,8,128]{3,2,1,0:T(8,128)S(1)}, f32[2,6,8,128]{3,2,1,0:T(8,128)S(1)}, u32[]{:S(2)}, u32[]{:S(2)}) collective-permute-start(f32[2,6,8,128]{3,2,1,0:T(8,128)S(1)} %pad_maximum_fusion.11), channel_id=1, source_target_pairs={{0,64},{16,80},{32,96},{48,112},{64,0},{80,16},{96,32},{112,48},{1... | collective-permute-start | bytes 147464 | tf_op jit(solution)/shard_map/ppermute | solution.py:61
  67.0 1.6 %collective-permute-start.12 = (f32[2,6,8,128]{3,2,1,0:T(8,128)S(1)}, f32[2,6,8,128]{3,2,1,0:T(8,128)S(1)}, u32[]{:S(2)}, u32[]{:S(2)}) collective-permute-start(f32[2,6,8,128]{3,2,1,0:T(8,128)S(1)} %pad_maximum_fusion.13), channel_id=1, source_target_pairs={{0,128},{16,144},{32,160},{48,176},{64,192},{80,208},{96,224},{112... | collective-permute-start | bytes 147464 | tf_op jit(solution)/shard_map/ppermute | solution.py:61
  68.6 5.6 %collective-permute-start.14 = (f32[2,6,8,128]{3,2,1,0:T(8,128)S(1)}, f32[2,6,8,128]{3,2,1,0:T(8,128)S(1)}, u32[]{:S(2)}, u32[]{:S(2)}) collective-permute-start(f32[2,6,8,128]{3,2,1,0:T(8,128)S(1)} %pad_maximum_fusion.15), channel_id=1, source_target_pairs={{0,192},{16,208},{32,224},{48,240},{64,128},{80,144},{96,160},{112... | collective-permute-start | bytes 147464 | tf_op jit(solution)/shard_map/ppermute | solution.py:61
  74.2 2.4 %collective-permute-done.14.refs_16_ = f32[2,6,8,128]{3,2,1,0:T(8,128)S(1)} collective-permute-done((f32[2,6,8,128]{3,2,1,0:T(8,128)S(1)}, f32[2,6,8,128]{3,2,1,0:T(8,128)S(1)}, u32[]{:S(2)}, u32[]{:S(2)}) %collective-permute-start.14) | collective-permute-done | bytes 49184 | tf_op jit(solution)/shard_map/ppermute | solution.py:61
  76.7 3.7 %collective-permute-done.15.refs_17_ = f32[2,6,8,128]{3,2,1,0:T(8,128)S(1)} collective-permute-done((f32[2,6,8,128]{3,2,1,0:T(8,128)S(1)}, f32[2,6,8,128]{3,2,1,0:T(8,128)S(1)}, u32[]{:S(2)}, u32[]{:S(2)}) %collective-permute-start.15) | collective-permute-done | bytes 49184 | tf_op jit(solution)/shard_map/ppermute | solution.py:61
  80.4 4.6 %shard_map.79 = (f32[16,7,8,128]{3,2,1,0:T(8,128)}, f32[8,7,8,128]{3,2,1,0:T(8,128)}, f32[8,7,8,128]{3,2,1,0:T(8,128)}) custom-call(s32[2]{0:T(128)} %pad_add_fusion.at_ref, f32[16,136,128]{2,1,0:T(8,128)S(1)} %copy-done.1, f32[2,136,128]{2,1,0:T(8,128)S(1)} %pad_maximum_fusion.refs_1_, f32[2,136,128]{2,1,0:T(8,128)S(1)} %collective-permute-done.1.refs_2_, ...), custom_call_target="tpu_custom_call" | custom-call | flops 1048576 | bytes 1048576 | tf_op jit(solution)/shard_map/pallas_call | solution.py:359
  85.0 8.9 %all-to-all-start.2 = ((f32[16,7,8,128]{3,2,1,0:T(8,128)}), f32[16,7,8,128]{3,2,1,0:T(8,128)S(1)}, u32[]{:S(2)}, u32[]{:S(2)}) async-start(f32[16,7,8,128]{3,2,1,0:T(8,128)} %get-tuple-element.19), calls=%async_computation.2 | async-start | bytes 917504 | tf_op jit(solution)/shard_map/all_to_all | solution.py:56
  97.6 3.1 %collective-permute-start.19 = (f32[2,7,8,128]{3,2,1,0:T(8,128)S(1)}, f32[2,7,8,128]{3,2,1,0:T(8,128)S(1)}, u32[]{:S(2)}, u32[]{:S(2)}) collective-permute-start(f32[2,7,8,128]{3,2,1,0:T(8,128)S(1)} %pad_maximum_fusion.4), channel_id=1, source_target_pairs={{0,96},{16,112},{32,64},{48,80},{64,32},{80,48},{96,0},{112,16},{1... | collective-permute-start | bytes 172040 | tf_op jit(solution)/shard_map/ppermute | solution.py:61
  101.9 2.8 %collective-permute-start.22 = (f32[2,7,8,128]{3,2,1,0:T(8,128)S(1)}, f32[2,7,8,128]{3,2,1,0:T(8,128)S(1)}, u32[]{:S(2)}, u32[]{:S(2)}) collective-permute-start(f32[2,7,8,128]{3,2,1,0:T(8,128)S(1)} %pad_maximum_fusion.7), channel_id=1, source_target_pairs={{0,192},{16,208},{32,224},{48,240},{64,128},{80,144},{96,160},{112... | collective-permute-start | bytes 172040 | tf_op jit(solution)/shard_map/ppermute | solution.py:61
  104.7 3.2 %collective-permute-start.23 = (f32[2,7,8,128]{3,2,1,0:T(8,128)S(1)}, f32[2,7,8,128]{3,2,1,0:T(8,128)S(1)}, u32[]{:S(2)}, u32[]{:S(2)}) collective-permute-start(f32[2,7,8,128]{3,2,1,0:T(8,128)S(1)} %pad_maximum_fusion.8), channel_id=1, source_target_pairs={{0,224},{16,240},{32,192},{48,208},{64,160},{80,176},{96,128},{112... | collective-permute-start | bytes 172040 | tf_op jit(solution)/shard_map/ppermute | solution.py:61
  108.7 2.3 %collective-permute-done.23.refs_8_ = f32[2,7,8,128]{3,2,1,0:T(8,128)S(1)} collective-permute-done((f32[2,7,8,128]{3,2,1,0:T(8,128)S(1)}, f32[2,7,8,128]{3,2,1,0:T(8,128)S(1)}, u32[]{:S(2)}, u32[]{:S(2)}) %collective-permute-start.23) | collective-permute-done | bytes 57376 | tf_op jit(solution)/shard_map/ppermute | solution.py:61
  111.0 7.3 %shard_map.80 = (f32[16,128,128]{2,1,0:T(8,128)}, f32[8,128,128]{2,1,0:T(8,128)}, f32[8,128,128]{2,1,0:T(8,128)}, f32[128,128]{1,0:T(8,128)}) custom-call(s32[2]{0:T(128)} %pad_add_fusion.at_ref, s32[3,1,1,6]{3,2,1,0:T(1,128)} %where_ref.5, s32[1,1]{1,0:T(1,128)S(6)} %copy.8.live_ref, f32[16,7,8,128]{3,2,1,0:T(8,128)S(1)} %all-to-all-done.2.refs_0_, ...), custom_call_target="tpu_custom_call" | custom-call | flops 1073741824 | bytes 6291456 | tf_op jit(solution)/shard_map/pallas_call | solution.py:297
  118.3 7.8 %all-to-all-start.3 = ((f32[16,128,128]{2,1,0:T(8,128)}), f32[16,128,128]{2,1,0:T(8,128)S(1)}, u32[]{:S(2)}, u32[]{:S(2)}) async-start(f32[16,128,128]{2,1,0:T(8,128)} %get-tuple-element.22), calls=%async_computation.3 | async-start | bytes 2097152 | tf_op jit(solution)/shard_map/all_to_all | solution.py:56
  128.4 2.7 %collective-permute-start.25 = (f32[128,128]{1,0:T(8,128)S(1)}, f32[128,128]{1,0:T(8,128)S(1)}, u32[]{:S(2)}, u32[]{:S(2)}) collective-permute-start(f32[128,128]{1,0:T(8,128)S(1)} %get-tuple-element.26), channel_id=1, source_target_pairs={{0,192},{16,208},{32,224},{48,240},{64,128},{80,144},{96,160},{112... | collective-permute-start | bytes 196616 | tf_op jit(solution)/shard_map/ppermute | solution.py:61
  131.1 5.4 %collective-permute-start.31 = (f32[128,128]{1,0:T(8,128)S(1)}, f32[128,128]{1,0:T(8,128)S(1)}, u32[]{:S(2)}, u32[]{:S(2)}) collective-permute-start(f32[128,128]{1,0:T(8,128)S(1)} %get-tuple-element.27), channel_id=1, source_target_pairs={{0,32},{16,48},{32,0},{48,16},{64,96},{80,112},{96,64},{112,80},{1... | collective-permute-start | bytes 196616 | tf_op jit(solution)/shard_map/ppermute | solution.py:61
  136.5 2.1 %collective-permute-start.28 = (f32[128,128]{1,0:T(8,128)S(1)}, f32[128,128]{1,0:T(8,128)S(1)}, u32[]{:S(2)}, u32[]{:S(2)}) collective-permute-start(f32[128,128]{1,0:T(8,128)S(1)} %get-tuple-element.30), channel_id=1, source_target_pairs={{0,64},{16,80},{32,96},{48,112},{64,0},{80,16},{96,32},{112,48},{1... | collective-permute-start | bytes 196616 | tf_op jit(solution)/shard_map/ppermute | solution.py:61
  138.6 3.5 %collective-permute-start.27 = (f32[128,128]{1,0:T(8,128)S(1)}, f32[128,128]{1,0:T(8,128)S(1)}, u32[]{:S(2)}, u32[]{:S(2)}) collective-permute-start(f32[128,128]{1,0:T(8,128)S(1)} %get-tuple-element.31), channel_id=1, source_target_pairs={{0,160},{16,176},{32,128},{48,144},{64,224},{80,240},{96,192},{112... | collective-permute-start | bytes 196616 | tf_op jit(solution)/shard_map/ppermute | solution.py:61
  142.9 2.8 %collective-permute-done.27 = f32[128,128]{1,0:T(8,128)S(1)} collective-permute-done((f32[128,128]{1,0:T(8,128)S(1)}, f32[128,128]{1,0:T(8,128)S(1)}, u32[]{:S(2)}, u32[]{:S(2)}) %collective-permute-start.27) | collective-permute-done | bytes 65568 | tf_op jit(solution)/shard_map/ppermute | solution.py:61
  145.7 3.8 %collective-permute-done.26 = f32[128,128]{1,0:T(8,128)S(1)} collective-permute-done((f32[128,128]{1,0:T(8,128)S(1)}, f32[128,128]{1,0:T(8,128)S(1)}, u32[]{:S(2)}, u32[]{:S(2)}) %collective-permute-start.26) | collective-permute-done | bytes 65568 | tf_op jit(solution)/shard_map/ppermute | solution.py:61
  150.2 6.7 %all-to-all-done.3 = f32[16,128,128]{2,1,0:T(8,128)S(1)} async-done(((f32[16,128,128]{2,1,0:T(8,128)}), f32[16,128,128]{2,1,0:T(8,128)S(1)}, u32[]{:S(2)}, u32[]{:S(2)}) %all-to-all-start.3) | async-done | bytes 1048608 | tf_op jit(solution)/shard_map/all_to_all | solution.py:56
  (83 shorter events, 17.9 us)
Async XLA Ops:
  3.3 40.8 %all-to-all-start = ((f32[16,136,128]{2,1,0:T(8,128)}), f32[16,136,128]{2,1,0:T(8,128)S(1)}, u32[]{:S(2)}, u32[]{:S(2)}) async-start(f32[16,136,128]{2,1,0:T(8,128)} %get-tuple-element.14), calls=%async_computation | async-start | bytes 2228224 | tf_op jit(solution)/shard_map/all_to_all | solution.py:56
  15.1 11.1 %collective-permute-start.7 = (f32[2,136,128]{2,1,0:T(8,128)S(1)}, f32[2,136,128]{2,1,0:T(8,128)S(1)}, u32[]{:S(2)}, u32[]{:S(2)}) collective-permute-start(f32[2,136,128]{2,1,0:T(8,128)S(1)} %pad_maximum_fusion.refs_1_), channel_id=1, source_target_pairs={{0,224},{16,240},{32,192},{48,208},{64,160},{80,176},{96,128},{112... | collective-permute-start | bytes 417800 | tf_op jit(solution)/shard_map/ppermute | solution.py:61
  18.7 10.4 %collective-permute-start.6 = (f32[2,136,128]{2,1,0:T(8,128)S(1)}, f32[2,136,128]{2,1,0:T(8,128)S(1)}, u32[]{:S(2)}, u32[]{:S(2)}) collective-permute-start(f32[2,136,128]{2,1,0:T(8,128)S(1)} %pad_maximum_fusion.refs_1_), channel_id=1, source_target_pairs={{0,192},{16,208},{32,224},{48,240},{64,128},{80,144},{96,160},{112... | collective-permute-start | bytes 417800 | tf_op jit(solution)/shard_map/ppermute | solution.py:61
  19.6 13.1 %collective-permute-start.5 = (f32[2,136,128]{2,1,0:T(8,128)S(1)}, f32[2,136,128]{2,1,0:T(8,128)S(1)}, u32[]{:S(2)}, u32[]{:S(2)}) collective-permute-start(f32[2,136,128]{2,1,0:T(8,128)S(1)} %pad_maximum_fusion.refs_1_), channel_id=1, source_target_pairs={{0,160},{16,176},{32,128},{48,144},{64,224},{80,240},{96,192},{112... | collective-permute-start | bytes 417800 | tf_op jit(solution)/shard_map/ppermute | solution.py:61
  21.0 16.3 %collective-permute-start.4 = (f32[2,136,128]{2,1,0:T(8,128)S(1)}, f32[2,136,128]{2,1,0:T(8,128)S(1)}, u32[]{:S(2)}, u32[]{:S(2)}) collective-permute-start(f32[2,136,128]{2,1,0:T(8,128)S(1)} %pad_maximum_fusion.refs_1_), channel_id=1, source_target_pairs={{0,128},{16,144},{32,160},{48,176},{64,192},{80,208},{96,224},{112... | collective-permute-start | bytes 417800 | tf_op jit(solution)/shard_map/ppermute | solution.py:61
  21.6 15.6 %collective-permute-start.3 = (f32[2,136,128]{2,1,0:T(8,128)S(1)}, f32[2,136,128]{2,1,0:T(8,128)S(1)}, u32[]{:S(2)}, u32[]{:S(2)}) collective-permute-start(f32[2,136,128]{2,1,0:T(8,128)S(1)} %pad_maximum_fusion.refs_1_), channel_id=1, source_target_pairs={{0,96},{16,112},{32,64},{48,80},{64,32},{80,48},{96,0},{112,16},{1... | collective-permute-start | bytes 417800 | tf_op jit(solution)/shard_map/ppermute | solution.py:61
  26.2 11.1 %collective-permute-start.2 = (f32[2,136,128]{2,1,0:T(8,128)S(1)}, f32[2,136,128]{2,1,0:T(8,128)S(1)}, u32[]{:S(2)}, u32[]{:S(2)}) collective-permute-start(f32[2,136,128]{2,1,0:T(8,128)S(1)} %pad_maximum_fusion.refs_1_), channel_id=1, source_target_pairs={{0,64},{16,80},{32,96},{48,112},{64,0},{80,16},{96,32},{112,48},{1... | collective-permute-start | bytes 417800 | tf_op jit(solution)/shard_map/ppermute | solution.py:61
  29.1 8.2 %collective-permute-start.1 = (f32[2,136,128]{2,1,0:T(8,128)S(1)}, f32[2,136,128]{2,1,0:T(8,128)S(1)}, u32[]{:S(2)}, u32[]{:S(2)}) collective-permute-start(f32[2,136,128]{2,1,0:T(8,128)S(1)} %pad_maximum_fusion.refs_1_), channel_id=1, source_target_pairs={{0,32},{16,48},{32,0},{48,16},{64,96},{80,112},{96,64},{112,80},{1... | collective-permute-start | bytes 417800 | tf_op jit(solution)/shard_map/ppermute | solution.py:61
  51.2 29.2 %all-to-all-start.1 = ((f32[16,6,8,128]{3,2,1,0:T(8,128)}), f32[16,6,8,128]{3,2,1,0:T(8,128)S(1)}, u32[]{:S(2)}, u32[]{:S(2)}) async-start(f32[16,6,8,128]{3,2,1,0:T(8,128)} %get-tuple-element.16), calls=%async_computation.1 | async-start | bytes 786432 | tf_op jit(solution)/shard_map/all_to_all | solution.py:56
  62.2 6.4 %collective-permute-start.9 = (f32[2,6,8,128]{3,2,1,0:T(8,128)S(1)}, f32[2,6,8,128]{3,2,1,0:T(8,128)S(1)}, u32[]{:S(2)}, u32[]{:S(2)}) collective-permute-start(f32[2,6,8,128]{3,2,1,0:T(8,128)S(1)} %pad_maximum_fusion.10), channel_id=1, source_target_pairs={{0,32},{16,48},{32,0},{48,16},{64,96},{80,112},{96,64},{112,80},{1... | collective-permute-start | bytes 147464 | tf_op jit(solution)/shard_map/ppermute | solution.py:61
  62.3 11.9 %collective-permute-start.10 = (f32[2,6,8,128]{3,2,1,0:T(8,128)S(1)}, f32[2,6,8,128]{3,2,1,0:T(8,128)S(1)}, u32[]{:S(2)}, u32[]{:S(2)}) collective-permute-start(f32[2,6,8,128]{3,2,1,0:T(8,128)S(1)} %pad_maximum_fusion.11), channel_id=1, source_target_pairs={{0,64},{16,80},{32,96},{48,112},{64,0},{80,16},{96,32},{112,48},{1... | collective-permute-start | bytes 147464 | tf_op jit(solution)/shard_map/ppermute | solution.py:61
  66.3 7.9 %collective-permute-start.11 = (f32[2,6,8,128]{3,2,1,0:T(8,128)S(1)}, f32[2,6,8,128]{3,2,1,0:T(8,128)S(1)}, u32[]{:S(2)}, u32[]{:S(2)}) collective-permute-start(f32[2,6,8,128]{3,2,1,0:T(8,128)S(1)} %pad_maximum_fusion.12), channel_id=1, source_target_pairs={{0,96},{16,112},{32,64},{48,80},{64,32},{80,48},{96,0},{112,16},{1... | collective-permute-start | bytes 147464 | tf_op jit(solution)/shard_map/ppermute | solution.py:61
  67.0 7.2 %collective-permute-start.12 = (f32[2,6,8,128]{3,2,1,0:T(8,128)S(1)}, f32[2,6,8,128]{3,2,1,0:T(8,128)S(1)}, u32[]{:S(2)}, u32[]{:S(2)}) collective-permute-start(f32[2,6,8,128]{3,2,1,0:T(8,128)S(1)} %pad_maximum_fusion.13), channel_id=1, source_target_pairs={{0,128},{16,144},{32,160},{48,176},{64,192},{80,208},{96,224},{112... | collective-permute-start | bytes 147464 | tf_op jit(solution)/shard_map/ppermute | solution.py:61
  68.6 5.7 %collective-permute-start.13 = (f32[2,6,8,128]{3,2,1,0:T(8,128)S(1)}, f32[2,6,8,128]{3,2,1,0:T(8,128)S(1)}, u32[]{:S(2)}, u32[]{:S(2)}) collective-permute-start(f32[2,6,8,128]{3,2,1,0:T(8,128)S(1)} %pad_maximum_fusion.14), channel_id=1, source_target_pairs={{0,160},{16,176},{32,128},{48,144},{64,224},{80,240},{96,192},{112... | collective-permute-start | bytes 147464 | tf_op jit(solution)/shard_map/ppermute | solution.py:61
  68.6 8.1 %collective-permute-start.14 = (f32[2,6,8,128]{3,2,1,0:T(8,128)S(1)}, f32[2,6,8,128]{3,2,1,0:T(8,128)S(1)}, u32[]{:S(2)}, u32[]{:S(2)}) collective-permute-start(f32[2,6,8,128]{3,2,1,0:T(8,128)S(1)} %pad_maximum_fusion.15), channel_id=1, source_target_pairs={{0,192},{16,208},{32,224},{48,240},{64,128},{80,144},{96,160},{112... | collective-permute-start | bytes 147464 | tf_op jit(solution)/shard_map/ppermute | solution.py:61
  74.2 6.2 %collective-permute-start.15 = (f32[2,6,8,128]{3,2,1,0:T(8,128)S(1)}, f32[2,6,8,128]{3,2,1,0:T(8,128)S(1)}, u32[]{:S(2)}, u32[]{:S(2)}) collective-permute-start(f32[2,6,8,128]{3,2,1,0:T(8,128)S(1)} %pad_maximum_fusion.16), channel_id=1, source_target_pairs={{0,224},{16,240},{32,192},{48,208},{64,160},{80,176},{96,128},{112... | collective-permute-start | bytes 147464 | tf_op jit(solution)/shard_map/ppermute | solution.py:61
  85.0 26.0 %all-to-all-start.2 = ((f32[16,7,8,128]{3,2,1,0:T(8,128)}), f32[16,7,8,128]{3,2,1,0:T(8,128)S(1)}, u32[]{:S(2)}, u32[]{:S(2)}) async-start(f32[16,7,8,128]{3,2,1,0:T(8,128)} %get-tuple-element.19), calls=%async_computation.2 | async-start | bytes 917504 | tf_op jit(solution)/shard_map/all_to_all | solution.py:56
  95.8 6.1 %collective-permute-start.17 = (f32[2,7,8,128]{3,2,1,0:T(8,128)S(1)}, f32[2,7,8,128]{3,2,1,0:T(8,128)S(1)}, u32[]{:S(2)}, u32[]{:S(2)}) collective-permute-start(f32[2,7,8,128]{3,2,1,0:T(8,128)S(1)} %pad_maximum_fusion.2), channel_id=1, source_target_pairs={{0,32},{16,48},{32,0},{48,16},{64,96},{80,112},{96,64},{112,80},{1... | collective-permute-start | bytes 172040 | tf_op jit(solution)/shard_map/ppermute | solution.py:61
  96.1 8.6 %collective-permute-start.18 = (f32[2,7,8,128]{3,2,1,0:T(8,128)S(1)}, f32[2,7,8,128]{3,2,1,0:T(8,128)S(1)}, u32[]{:S(2)}, u32[]{:S(2)}) collective-permute-start(f32[2,7,8,128]{3,2,1,0:T(8,128)S(1)} %pad_maximum_fusion.3), channel_id=1, source_target_pairs={{0,64},{16,80},{32,96},{48,112},{64,0},{80,16},{96,32},{112,48},{1... | collective-permute-start | bytes 172040 | tf_op jit(solution)/shard_map/ppermute | solution.py:61
  97.6 10.3 %collective-permute-start.19 = (f32[2,7,8,128]{3,2,1,0:T(8,128)S(1)}, f32[2,7,8,128]{3,2,1,0:T(8,128)S(1)}, u32[]{:S(2)}, u32[]{:S(2)}) collective-permute-start(f32[2,7,8,128]{3,2,1,0:T(8,128)S(1)} %pad_maximum_fusion.4), channel_id=1, source_target_pairs={{0,96},{16,112},{32,64},{48,80},{64,32},{80,48},{96,0},{112,16},{1... | collective-permute-start | bytes 172040 | tf_op jit(solution)/shard_map/ppermute | solution.py:61
  100.8 7.2 %collective-permute-start.20 = (f32[2,7,8,128]{3,2,1,0:T(8,128)S(1)}, f32[2,7,8,128]{3,2,1,0:T(8,128)S(1)}, u32[]{:S(2)}, u32[]{:S(2)}) collective-permute-start(f32[2,7,8,128]{3,2,1,0:T(8,128)S(1)} %pad_maximum_fusion.5), channel_id=1, source_target_pairs={{0,128},{16,144},{32,160},{48,176},{64,192},{80,208},{96,224},{112... | collective-permute-start | bytes 172040 | tf_op jit(solution)/shard_map/ppermute | solution.py:61
  101.8 6.1 %collective-permute-start.21 = (f32[2,7,8,128]{3,2,1,0:T(8,128)S(1)}, f32[2,7,8,128]{3,2,1,0:T(8,128)S(1)}, u32[]{:S(2)}, u32[]{:S(2)}) collective-permute-start(f32[2,7,8,128]{3,2,1,0:T(8,128)S(1)} %pad_maximum_fusion.6), channel_id=1, source_target_pairs={{0,160},{16,176},{32,128},{48,144},{64,224},{80,240},{96,192},{112... | collective-permute-start | bytes 172040 | tf_op jit(solution)/shard_map/ppermute | solution.py:61
  101.9 6.8 %collective-permute-start.22 = (f32[2,7,8,128]{3,2,1,0:T(8,128)S(1)}, f32[2,7,8,128]{3,2,1,0:T(8,128)S(1)}, u32[]{:S(2)}, u32[]{:S(2)}) collective-permute-start(f32[2,7,8,128]{3,2,1,0:T(8,128)S(1)} %pad_maximum_fusion.7), channel_id=1, source_target_pairs={{0,192},{16,208},{32,224},{48,240},{64,128},{80,144},{96,160},{112... | collective-permute-start | bytes 172040 | tf_op jit(solution)/shard_map/ppermute | solution.py:61
  104.7 6.3 %collective-permute-start.23 = (f32[2,7,8,128]{3,2,1,0:T(8,128)S(1)}, f32[2,7,8,128]{3,2,1,0:T(8,128)S(1)}, u32[]{:S(2)}, u32[]{:S(2)}) collective-permute-start(f32[2,7,8,128]{3,2,1,0:T(8,128)S(1)} %pad_maximum_fusion.8), channel_id=1, source_target_pairs={{0,224},{16,240},{32,192},{48,208},{64,160},{80,176},{96,128},{112... | collective-permute-start | bytes 172040 | tf_op jit(solution)/shard_map/ppermute | solution.py:61
  118.3 38.6 %all-to-all-start.3 = ((f32[16,128,128]{2,1,0:T(8,128)}), f32[16,128,128]{2,1,0:T(8,128)S(1)}, u32[]{:S(2)}, u32[]{:S(2)}) async-start(f32[16,128,128]{2,1,0:T(8,128)} %get-tuple-element.22), calls=%async_computation.3 | async-start | bytes 2097152 | tf_op jit(solution)/shard_map/all_to_all | solution.py:56
  128.4 10.2 %collective-permute-start.25 = (f32[128,128]{1,0:T(8,128)S(1)}, f32[128,128]{1,0:T(8,128)S(1)}, u32[]{:S(2)}, u32[]{:S(2)}) collective-permute-start(f32[128,128]{1,0:T(8,128)S(1)} %get-tuple-element.26), channel_id=1, source_target_pairs={{0,192},{16,208},{32,224},{48,240},{64,128},{80,144},{96,160},{112... | collective-permute-start | bytes 196616 | tf_op jit(solution)/shard_map/ppermute | solution.py:61
  131.1 10.9 %collective-permute-start.31 = (f32[128,128]{1,0:T(8,128)S(1)}, f32[128,128]{1,0:T(8,128)S(1)}, u32[]{:S(2)}, u32[]{:S(2)}) collective-permute-start(f32[128,128]{1,0:T(8,128)S(1)} %get-tuple-element.27), channel_id=1, source_target_pairs={{0,32},{16,48},{32,0},{48,16},{64,96},{80,112},{96,64},{112,80},{1... | collective-permute-start | bytes 196616 | tf_op jit(solution)/shard_map/ppermute | solution.py:61
  136.5 6.4 %collective-permute-start.30 = (f32[128,128]{1,0:T(8,128)S(1)}, f32[128,128]{1,0:T(8,128)S(1)}, u32[]{:S(2)}, u32[]{:S(2)}) collective-permute-start(f32[128,128]{1,0:T(8,128)S(1)} %get-tuple-element.28), channel_id=1, source_target_pairs={{0,96},{16,112},{32,64},{48,80},{64,32},{80,48},{96,0},{112,16},{1... | collective-permute-start | bytes 196616 | tf_op jit(solution)/shard_map/ppermute | solution.py:61
  136.5 6.4 %collective-permute-start.29 = (f32[128,128]{1,0:T(8,128)S(1)}, f32[128,128]{1,0:T(8,128)S(1)}, u32[]{:S(2)}, u32[]{:S(2)}) collective-permute-start(f32[128,128]{1,0:T(8,128)S(1)} %get-tuple-element.29), channel_id=1, source_target_pairs={{0,128},{16,144},{32,160},{48,176},{64,192},{80,208},{96,224},{112... | collective-permute-start | bytes 196616 | tf_op jit(solution)/shard_map/ppermute | solution.py:61
  136.5 6.4 %collective-permute-start.28 = (f32[128,128]{1,0:T(8,128)S(1)}, f32[128,128]{1,0:T(8,128)S(1)}, u32[]{:S(2)}, u32[]{:S(2)}) collective-permute-start(f32[128,128]{1,0:T(8,128)S(1)} %get-tuple-element.30), channel_id=1, source_target_pairs={{0,64},{16,80},{32,96},{48,112},{64,0},{80,16},{96,32},{112,48},{1... | collective-permute-start | bytes 196616 | tf_op jit(solution)/shard_map/ppermute | solution.py:61
  138.6 7.1 %collective-permute-start.27 = (f32[128,128]{1,0:T(8,128)S(1)}, f32[128,128]{1,0:T(8,128)S(1)}, u32[]{:S(2)}, u32[]{:S(2)}) collective-permute-start(f32[128,128]{1,0:T(8,128)S(1)} %get-tuple-element.31), channel_id=1, source_target_pairs={{0,160},{16,176},{32,128},{48,144},{64,224},{80,240},{96,192},{112... | collective-permute-start | bytes 196616 | tf_op jit(solution)/shard_map/ppermute | solution.py:61
  142.1 7.5 %collective-permute-start.26 = (f32[128,128]{1,0:T(8,128)S(1)}, f32[128,128]{1,0:T(8,128)S(1)}, u32[]{:S(2)}, u32[]{:S(2)}) collective-permute-start(f32[128,128]{1,0:T(8,128)S(1)} %get-tuple-element.32), channel_id=1, source_target_pairs={{0,224},{16,240},{32,192},{48,208},{64,160},{80,176},{96,128},{112... | collective-permute-start | bytes 196616 | tf_op jit(solution)/shard_map/ppermute | solution.py:61
  (10 other events, 94.6 us)

commit v4 on v3

--- a/solution.py
+++ b/solution.py
@@ -166,37 +166,23 @@
 def first_kernel(at_ref, where_ref, live_ref, *refs):
     a_ref, b_refs, (c_ref, counts_ref), refs = refs[0], refs[1:9], refs[9:11], refs[11:]
     ga_ref, gb_refs, refs = refs[0], refs[1:3], refs[3:]
-    block_a, all_b, turned_b, part_c, seen, sems, sem_a, sem_b = refs
+    all_b, turned_b, part_c, seen, sems = refs
     slots, _, side, rank = counts_ref.shape
     members = a_ref.shape[0]
     rows = side // members
     live = live_ref[0, 0]
     fetches = Fetches(where_ref, live_ref, c_ref, counts_ref, part_c, seen, sems)
 
-    def fetch_a(slot):
-        return pltpu.make_async_copy(a_ref.at[where_ref[0, 0, 0, slot], pl.ds(0, side)], block_a.at[slot], sem_a.at[slot])
-
-    copies_b = [
-        pltpu.make_async_copy(ref.at[:, pl.ds(0, side)], all_b.at[pl.ds(2 * pair, 2)], sem_b.at[pair])
-        for pair, ref in enumerate(b_refs)
-    ]
-    for slot in range(slots):
-
-        @pl.when(slot < live)
-        def _():
-            fetch_a(slot).start()
-
-    for copy in copies_b:
-        copy.start()
     fetches.start()
-    for copy in copies_b:
-        copy.wait()
+    for place in range(members):
+        all_b[place] = b_refs[place // 2][place % 2, :side]
 
     def visit(slot, carry):
-        fetch_a(slot).wait()
-        piece_b = all_b[where_ref[1, 0, 0, slot] ^ at_ref[0]]
         grad_a, grad_b = slot_gradients(
-            block_a[slot], piece_b, fetches.factor(slot), functools.partial(fetches.observed, slot)
+            a_ref[where_ref[0, 0, 0, slot], :side],
+            all_b[where_ref[1, 0, 0, slot] ^ at_ref[0]],
+            fetches.factor(slot),
+            functools.partial(fetches.observed, slot),
         )
         ga_ref[:, slot] = grad_a.reshape(members, rows, rank)
         turned_b[...] = grad_b
@@ -218,31 +204,24 @@
 def last_kernel(at_ref, where_ref, live_ref, *refs):
     a_ref, b_refs, (c_ref, counts_ref), refs = refs[0], refs[1:9], refs[9:11], refs[11:]
     ga_ref, even_ref, odd_ref, base_b, refs = *refs[:4], refs[4:]
-    block_a, all_b, block_b, part_c, seen, sems, sem_b = refs
+    block_b, part_c, seen, sems = refs
     slots, _, side, rank = counts_ref.shape
     members = a_ref.shape[0]
     rows = side // members
     live = live_ref[0, 0]
     me = at_ref[0]
     fetches = Fetches(where_ref, live_ref, c_ref, counts_ref, part_c, seen, sems)
-    copies = [pltpu.make_async_copy(a_ref, block_a, sem_b.at[8])]
-    for pair, ref in enumerate(b_refs):
-        copies.append(pltpu.make_async_copy(ref, all_b.at[pl.ds(2 * pair, 2)], sem_b.at[pair]))
-    for copy in copies:
-        copy.start()
     fetches.start()
     for ref in (ga_ref, even_ref, odd_ref):
         ref[...] = jnp.zeros_like(ref)
-    for copy in copies:
-        copy.wait()
     for place in range(members):
-        base_b[rows_at(me ^ place, rows), :] = all_b[place, slots]
+        base_b[rows_at(me ^ place, rows), :] = b_refs[place // 2][place % 2, slots]
 
     def visit(slot, carry):
         for place in range(members):
-            block_b[rows_at(me ^ place, rows), :] = all_b[place, slot]
+            block_b[rows_at(me ^ place, rows), :] = b_refs[place // 2][place % 2, slot]
         grad_a, grad_b = slot_gradients(
-            block_a[:, slot].reshape(side, rank),
+            a_ref[:, slot].reshape(side, rank),
             block_b[...],
             fetches.factor(slot),
             functools.partial(fetches.observed, slot),
@@ -276,28 +255,22 @@
         half = shape_of(members // 2, side, rank)
         shapes = (shape_of(members, side, rank), half, half, shape_of(side, rank))
         scratch = [
-            pltpu.VMEM(held_a.shape, jnp.float32),
-            pltpu.VMEM((members, *held_b[0].shape[1:]), jnp.float32),
             pltpu.VMEM((side, rank), jnp.float32),
             *common,
-            pltpu.SemaphoreType.DMA((9,)),
         ]
     else:
         kernel = first_kernel
         half = shape_of(members // 2, slots, rows, rank)
         shapes = (shape_of(members, slots, rows, rank), half, half)
         scratch = [
-            pltpu.VMEM((slots, side, rank), jnp.float32),
             pltpu.VMEM((members, side, rank), jnp.float32),
             pltpu.VMEM((side, rank), jnp.float32),
             *common,
-            pltpu.SemaphoreType.DMA((slots,)),
-            pltpu.SemaphoreType.DMA((8,)),
         ]
     return pl.pallas_call(
         kernel,
         out_shape=shapes,
-        in_specs=[smem] * 3 + [anywhere] * 11,
+        in_specs=[smem] * 3 + [vmem] * 9 + [anywhere] * 2,
         out_specs=[vmem] * len(shapes),
         scratch_shapes=scratch,
         cost_estimate=pl.CostEstimate(flops=1 << 30, bytes_accessed=6 << 20, transcendentals=1 << 20),
@@ -310,8 +283,9 @@
 
 def update_kernel(at_ref, *refs):
     all_refs, back_refs, outs, refs = refs[:9], refs[9:18], refs[18:21], refs[21:]
-    grads, pieces, totals, notes, sems = refs
-    members, slots, rows, _ = grads.shape[1:]
+    pieces, sums_a, sums_b, others_a, others_b, notes, sems = refs
+    members, slots, rows, _ = back_refs[0].shape
+    totals, others = (sums_a, sums_b), (others_a, others_b)
     side = members * rows
     copies = []
     for index in range(9):
@@ -319,35 +293,32 @@
         to = pl.ds(0, members) if index == 0 else pl.ds(2 * (index - 1), 2)
         at = rows_at(at_ref[1 - kind], rows)
         copies.append(pltpu.make_async_copy(all_refs[index].at[:, side], notes.at[kind, to], sems.at[0, index]))
-        copies.append(pltpu.make_async_copy(back_refs[index], grads.at[kind, to], sems.at[1, index]))
-        copies.append(pltpu.make_async_copy(all_refs[index].at[:, at], pieces.at[kind, to], sems.at[2, index]))
+        copies.append(pltpu.make_async_copy(all_refs[index].at[:, at], pieces.at[kind, to], sems.at[1, index]))
     for copy in copies:
         copy.start()
-    totals[...] = jnp.zeros_like(totals)
+    for ref in (*totals, *others):
+        ref[...] = jnp.zeros_like(ref)
     for copy in copies:
         copy.wait()
-
-    def gather(place, carry):
+    for place in range(members):
+        sums = others if place % 2 else totals
         for slot in range(slots):
-            for kind in range(2):
+            for kind, grad in enumerate((back_refs[0][place, slot], back_refs[1 + place // 2][place % 2, slot])):
                 block = name_of(notes, kind, place, slot)
-                totals[kind, block] = totals[kind, block] + grads[kind, place, slot]
-        return carry
-
-    lax.fori_loop(0, members, gather, 0)
-    totals[0, :members] = pieces[0] - step_rate * totals[0, :members]
+                sums[kind][block] = sums[kind][block] + grad
+    sums_a[:members] = pieces[0] - step_rate * (sums_a[:members] + others_a[:members])
     for place in range(members):
         owner = at_ref[0] ^ place
-        totals[1, owner] = pieces[1, place] - step_rate * totals[1, owner]
+        sums_b[owner] = pieces[1, place] - step_rate * (sums_b[owner] + others_b[owner])
 
     def deal(index, carry):
         for way in range(2):
             place = 2 * index + way
             for slot in range(slots):
-                outs[0][place, slot] = totals[0, jnp.minimum(name_of(notes, 0, place, slot), members - 1)]
-                outs[1 + way][index, slot] = totals[1, jnp.minimum(name_of(notes, 1, place, slot), members - 1)]
-            outs[0][place, slots] = totals[0, place]
-            outs[1 + way][index, slots] = totals[1, at_ref[0] ^ place]
+                outs[0][place, slot] = sums_a[jnp.minimum(name_of(notes, 0, place, slot), members - 1)]
+                outs[1 + way][index, slot] = sums_b[jnp.minimum(name_of(notes, 1, place, slot), members - 1)]
+            outs[0][place, slots] = sums_a[place]
+            outs[1 + way][index, slots] = sums_b[at_ref[0] ^ place]
         return carry
 
     lax.fori_loop(0, members // 2, deal, 0)
@@ -359,14 +330,13 @@
     return pl.pallas_call(
         update_kernel,
         out_shape=(shape_of(members, slots + 1, rows, rank), half, half),
-        in_specs=[smem] + [anywhere] * 18,
+        in_specs=[smem] + [anywhere] * 9 + [vmem] * 9,
         out_specs=(vmem, vmem, vmem),
         scratch_shapes=[
-            pltpu.VMEM((2, members, slots, rows, rank), jnp.float32),
             pltpu.VMEM((2, members, rows, rank), jnp.float32),
-            pltpu.VMEM((2, members + 1, rows, rank), jnp.float32),
+            *[pltpu.VMEM((members + 1, rows, rank), jnp.float32)] * 4,
             pltpu.SMEM((2, members, rank), jnp.float32),
-            pltpu.SemaphoreType.DMA((3, 9)),
+            pltpu.SemaphoreType.DMA((2, 9)),
         ],
         cost_estimate=small_cost,
     )(at, *map(near, (all_a, *all_b, back_a, *back_b)))

time: 158 us -> 155 us (0.981)
  Pallas kernels: 20.9 us -> 18 us
    pallas_call x2, Pallas kernels: 14.3 us -> 12.2 us  [block_gradients(): pl.pallas_call(kernel, out_shape=shapes, in_specs=[smem] * 3 + [vmem] * 9...]
where the time goes in v4:
time: 155 us; the launch traced here: 154 us
  starting transfers between devices  90.2 us (58%)
  waiting for transfers between devices  40.7 us (26%)
  Pallas kernels  18 us (12%)
  other arithmetic  2.16 us (1%)
  local copies, waits for them, and re-layouts  1.85 us (1%)
  between operations  1.6 us (1%)
    ppermute x32, starting transfers between devices, shift_row(): lax.ppermute(value, 'row', [(member, member ^ change) for member in range...  55.8 us
    all_to_all x4, starting transfers between devices, swap_col(): return lax.all_to_all(sent, 'col', 0, 0, tiled=True)  34.4 us
    ppermute x32, waiting for transfers between devices, shift_row(): lax.ppermute(value, 'row', [(member, member ^ change) for member in range...  27 us
    all_to_all x4, waiting for transfers between devices, swap_col(): return lax.all_to_all(sent, 'col', 0, 0, tiled=True)  13.7 us
    pallas_call x2, Pallas kernels, block_gradients(): pl.pallas_call(kernel, out_shape=shapes, in_specs=[smem] * 3 + [vmem] * 9...  12.2 us
    pallas_call x1, Pallas kernels, update(): pl.pallas_call(update_kernel, out_shape=(shape_of(members, slots + 1, row...  3.74 us
  transfers between devices with their start and end apart: 36, of which 15 were waited for; matrix products, arithmetic and copies ran while one was open for 2% of the time, Pallas kernels for 0%

profile of v4, /device:TPU:8, one launch (start us, length us, event | category | flops | bytes accessed | tf_op | source)
XLA Modules:
  0.0 154.4 jit_solution(13866901563984323844)
XLA Ops:
  1.3 2.0 %shard_map.77 = (f32[16,136,128]{2,1,0:T(8,128)}, f32[136,128]{1,0:T(8,128)}) custom-call(s32[3,1,1,6]{3,2,1,0:T(1,128)} %where_ref.5, s32[1,1]{1,0:T(1,128)S(6)} %copy.8.live_ref, f32[128,128]{1,0:T(8,128)} %a_ref.1, f32[128,128]{1,0:T(8,128)} %b_ref.1), custom_call_target="tpu_custom_call" | custom-call | flops 1048576 | bytes 1048576 | tf_op jit(solution)/shard_map/pallas_call | solution.py:98
  3.3 10.4 %all-to-all-start = ((f32[16,136,128]{2,1,0:T(8,128)}), f32[16,136,128]{2,1,0:T(8,128)S(1)}, u32[]{:S(2)}, u32[]{:S(2)}) async-start(f32[16,136,128]{2,1,0:T(8,128)} %get-tuple-element.14), calls=%async_computation | async-start | bytes 2228224 | tf_op jit(solution)/shard_map/all_to_all | solution.py:56
  15.1 3.6 %collective-permute-start.7 = (f32[2,136,128]{2,1,0:T(8,128)S(1)}, f32[2,136,128]{2,1,0:T(8,128)S(1)}, u32[]{:S(2)}, u32[]{:S(2)}) collective-permute-start(f32[2,136,128]{2,1,0:T(8,128)S(1)} %pad_maximum_fusion.refs_1_), channel_id=1, source_target_pairs={{0,224},{16,240},{32,192},{48,208},{64,160},{80,176},{96,128},{112... | collective-permute-start | bytes 417800 | tf_op jit(solution)/shard_map/ppermute | solution.py:61
  21.6 2.8 %collective-permute-start.3 = (f32[2,136,128]{2,1,0:T(8,128)S(1)}, f32[2,136,128]{2,1,0:T(8,128)S(1)}, u32[]{:S(2)}, u32[]{:S(2)}) collective-permute-start(f32[2,136,128]{2,1,0:T(8,128)S(1)} %pad_maximum_fusion.refs_1_), channel_id=1, source_target_pairs={{0,96},{16,112},{32,64},{48,80},{64,32},{80,48},{96,0},{112,16},{1... | collective-permute-start | bytes 417800 | tf_op jit(solution)/shard_map/ppermute | solution.py:61
  24.4 1.8 %collective-permute-done.7.refs_8_ = f32[2,136,128]{2,1,0:T(8,128)S(1)} collective-permute-done((f32[2,136,128]{2,1,0:T(8,128)S(1)}, f32[2,136,128]{2,1,0:T(8,128)S(1)}, u32[]{:S(2)}, u32[]{:S(2)}) %collective-permute-start.7) | collective-permute-done | bytes 139296 | tf_op jit(solution)/shard_map/ppermute | solution.py:61
  26.2 2.0 %collective-permute-start.2 = (f32[2,136,128]{2,1,0:T(8,128)S(1)}, f32[2,136,128]{2,1,0:T(8,128)S(1)}, u32[]{:S(2)}, u32[]{:S(2)}) collective-permute-start(f32[2,136,128]{2,1,0:T(8,128)S(1)} %pad_maximum_fusion.refs_1_), channel_id=1, source_target_pairs={{0,64},{16,80},{32,96},{48,112},{64,0},{80,16},{96,32},{112,48},{1... | collective-permute-start | bytes 417800 | tf_op jit(solution)/shard_map/ppermute | solution.py:61
  29.1 3.1 %collective-permute-start.1 = (f32[2,136,128]{2,1,0:T(8,128)S(1)}, f32[2,136,128]{2,1,0:T(8,128)S(1)}, u32[]{:S(2)}, u32[]{:S(2)}) collective-permute-start(f32[2,136,128]{2,1,0:T(8,128)S(1)} %pad_maximum_fusion.refs_1_), channel_id=1, source_target_pairs={{0,32},{16,48},{32,0},{48,16},{64,96},{80,112},{96,64},{112,80},{1... | collective-permute-start | bytes 417800 | tf_op jit(solution)/shard_map/ppermute | solution.py:61
  32.8 4.5 %collective-permute-done.4.refs_5_ = f32[2,136,128]{2,1,0:T(8,128)S(1)} collective-permute-done((f32[2,136,128]{2,1,0:T(8,128)S(1)}, f32[2,136,128]{2,1,0:T(8,128)S(1)}, u32[]{:S(2)}, u32[]{:S(2)}) %collective-permute-start.4) | collective-permute-done | bytes 139296 | tf_op jit(solution)/shard_map/ppermute | solution.py:61
  37.3 6.8 %all-to-all-done.refs_0_ = f32[16,136,128]{2,1,0:T(8,128)S(1)} async-done(((f32[16,136,128]{2,1,0:T(8,128)}), f32[16,136,128]{2,1,0:T(8,128)S(1)}, u32[]{:S(2)}, u32[]{:S(2)}) %all-to-all-start) | async-done | bytes 1114144 | tf_op jit(solution)/shard_map/all_to_all | solution.py:56
  44.1 5.9 %shard_map.78 = (f32[16,6,8,128]{3,2,1,0:T(8,128)}, f32[8,6,8,128]{3,2,1,0:T(8,128)}, f32[8,6,8,128]{3,2,1,0:T(8,128)}) custom-call(s32[2]{0:T(128)} %pad_add_fusion.at_ref, s32[3,1,1,6]{3,2,1,0:T(1,128)} %where_ref.5, s32[1,1]{1,0:T(1,128)S(6)} %copy.8.live_ref, f32[16,136,128]{2,1,0:T(8,128)S(1)} %all-to-all-done.refs_0_, ...), custom_call_target="tpu_custom_call" | custom-call | flops 1073741824 | bytes 6291456 | tf_op jit(solution)/shard_map/pallas_call | solution.py:270
  50.0 7.4 %all-to-all-start.1 = ((f32[16,6,8,128]{3,2,1,0:T(8,128)}), f32[16,6,8,128]{3,2,1,0:T(8,128)S(1)}, u32[]{:S(2)}, u32[]{:S(2)}) async-start(f32[16,6,8,128]{3,2,1,0:T(8,128)} %get-tuple-element.16), calls=%async_computation.1 | async-start | bytes 786432 | tf_op jit(solution)/shard_map/all_to_all | solution.py:56
  57.4 2.1 %collective-permute-start.8 = (f32[8,6,8,128]{3,2,1,0:T(8,128)}, f32[8,6,8,128]{3,2,1,0:T(8,128)S(1)}, u32[]{:S(2)}, u32[]{:S(2)}) collective-permute-start(f32[8,6,8,128]{3,2,1,0:T(8,128)} %get-tuple-element.18), channel_id=1, source_target_pairs={{0,16},{16,0},{32,48},{48,32},{64,80},{80,64},{96,112},{112,96},{1... | collective-permute-start | bytes 589832 | tf_op jit(solution)/shard_map/ppermute | solution.py:61
  60.9 4.1 %collective-permute-start.10 = (f32[2,6,8,128]{3,2,1,0:T(8,128)S(1)}, f32[2,6,8,128]{3,2,1,0:T(8,128)S(1)}, u32[]{:S(2)}, u32[]{:S(2)}) collective-permute-start(f32[2,6,8,128]{3,2,1,0:T(8,128)S(1)} %pad_maximum_fusion.11), channel_id=1, source_target_pairs={{0,64},{16,80},{32,96},{48,112},{64,0},{80,16},{96,32},{112,48},{1... | collective-permute-start | bytes 147464 | tf_op jit(solution)/shard_map/ppermute | solution.py:61
  65.6 1.6 %collective-permute-start.12 = (f32[2,6,8,128]{3,2,1,0:T(8,128)S(1)}, f32[2,6,8,128]{3,2,1,0:T(8,128)S(1)}, u32[]{:S(2)}, u32[]{:S(2)}) collective-permute-start(f32[2,6,8,128]{3,2,1,0:T(8,128)S(1)} %pad_maximum_fusion.13), channel_id=1, source_target_pairs={{0,128},{16,144},{32,160},{48,176},{64,192},{80,208},{96,224},{112... | collective-permute-start | bytes 147464 | tf_op jit(solution)/shard_map/ppermute | solution.py:61
  67.3 5.6 %collective-permute-start.14 = (f32[2,6,8,128]{3,2,1,0:T(8,128)S(1)}, f32[2,6,8,128]{3,2,1,0:T(8,128)S(1)}, u32[]{:S(2)}, u32[]{:S(2)}) collective-permute-start(f32[2,6,8,128]{3,2,1,0:T(8,128)S(1)} %pad_maximum_fusion.15), channel_id=1, source_target_pairs={{0,192},{16,208},{32,224},{48,240},{64,128},{80,144},{96,160},{112... | collective-permute-start | bytes 147464 | tf_op jit(solution)/shard_map/ppermute | solution.py:61
  72.9 2.4 %collective-permute-done.14.refs_16_ = f32[2,6,8,128]{3,2,1,0:T(8,128)S(1)} collective-permute-done((f32[2,6,8,128]{3,2,1,0:T(8,128)S(1)}, f32[2,6,8,128]{3,2,1,0:T(8,128)S(1)}, u32[]{:S(2)}, u32[]{:S(2)}) %collective-permute-start.14) | collective-permute-done | bytes 49184 | tf_op jit(solution)/shard_map/ppermute | solution.py:61
  75.3 3.7 %collective-permute-done.15.refs_17_ = f32[2,6,8,128]{3,2,1,0:T(8,128)S(1)} collective-permute-done((f32[2,6,8,128]{3,2,1,0:T(8,128)S(1)}, f32[2,6,8,128]{3,2,1,0:T(8,128)S(1)}, u32[]{:S(2)}, u32[]{:S(2)}) %collective-permute-start.15) | collective-permute-done | bytes 49184 | tf_op jit(solution)/shard_map/ppermute | solution.py:61
  79.1 3.7 %shard_map.79 = (f32[16,7,8,128]{3,2,1,0:T(8,128)}, f32[8,7,8,128]{3,2,1,0:T(8,128)}, f32[8,7,8,128]{3,2,1,0:T(8,128)}) custom-call(s32[2]{0:T(128)} %pad_add_fusion.at_ref, f32[16,136,128]{2,1,0:T(8,128)S(1)} %copy-done.1, f32[2,136,128]{2,1,0:T(8,128)S(1)} %pad_maximum_fusion.refs_1_, f32[2,136,128]{2,1,0:T(8,128)S(1)} %collective-permute-done.1.refs_2_, ...), custom_call_target="tpu_custom_call" | custom-call | flops 1048576 | bytes 1048576 | tf_op jit(solution)/shard_map/pallas_call | solution.py:330
  82.8 9.0 %all-to-all-start.2 = ((f32[16,7,8,128]{3,2,1,0:T(8,128)}), f32[16,7,8,128]{3,2,1,0:T(8,128)S(1)}, u32[]{:S(2)}, u32[]{:S(2)}) async-start(f32[16,7,8,128]{3,2,1,0:T(8,128)} %get-tuple-element.19), calls=%async_computation.2 | async-start | bytes 917504 | tf_op jit(solution)/shard_map/all_to_all | solution.py:56
  95.4 3.1 %collective-permute-start.19 = (f32[2,7,8,128]{3,2,1,0:T(8,128)S(1)}, f32[2,7,8,128]{3,2,1,0:T(8,128)S(1)}, u32[]{:S(2)}, u32[]{:S(2)}) collective-permute-start(f32[2,7,8,128]{3,2,1,0:T(8,128)S(1)} %pad_maximum_fusion.4), channel_id=1, source_target_pairs={{0,96},{16,112},{32,64},{48,80},{64,32},{80,48},{96,0},{112,16},{1... | collective-permute-start | bytes 172040 | tf_op jit(solution)/shard_map/ppermute | solution.py:61
  99.8 2.7 %collective-permute-start.22 = (f32[2,7,8,128]{3,2,1,0:T(8,128)S(1)}, f32[2,7,8,128]{3,2,1,0:T(8,128)S(1)}, u32[]{:S(2)}, u32[]{:S(2)}) collective-permute-start(f32[2,7,8,128]{3,2,1,0:T(8,128)S(1)} %pad_maximum_fusion.7), channel_id=1, source_target_pairs={{0,192},{16,208},{32,224},{48,240},{64,128},{80,144},{96,160},{112... | collective-permute-start | bytes 172040 | tf_op jit(solution)/shard_map/ppermute | solution.py:61
  102.5 3.3 %collective-permute-start.23 = (f32[2,7,8,128]{3,2,1,0:T(8,128)S(1)}, f32[2,7,8,128]{3,2,1,0:T(8,128)S(1)}, u32[]{:S(2)}, u32[]{:S(2)}) collective-permute-start(f32[2,7,8,128]{3,2,1,0:T(8,128)S(1)} %pad_maximum_fusion.8), channel_id=1, source_target_pairs={{0,224},{16,240},{32,192},{48,208},{64,160},{80,176},{96,128},{112... | collective-permute-start | bytes 172040 | tf_op jit(solution)/shard_map/ppermute | solution.py:61
  106.5 2.3 %collective-permute-done.23.refs_8_ = f32[2,7,8,128]{3,2,1,0:T(8,128)S(1)} collective-permute-done((f32[2,7,8,128]{3,2,1,0:T(8,128)S(1)}, f32[2,7,8,128]{3,2,1,0:T(8,128)S(1)}, u32[]{:S(2)}, u32[]{:S(2)}) %collective-permute-start.23) | collective-permute-done | bytes 57376 | tf_op jit(solution)/shard_map/ppermute | solution.py:61
  108.8 6.3 %shard_map.80 = (f32[16,128,128]{2,1,0:T(8,128)}, f32[8,128,128]{2,1,0:T(8,128)}, f32[8,128,128]{2,1,0:T(8,128)}, f32[128,128]{1,0:T(8,128)}) custom-call(s32[2]{0:T(128)} %pad_add_fusion.at_ref, s32[3,1,1,6]{3,2,1,0:T(1,128)} %where_ref.5, s32[1,1]{1,0:T(1,128)S(6)} %copy.8.live_ref, f32[16,7,8,128]{3,2,1,0:T(8,128)S(1)} %all-to-all-done.2.refs_0_, ...), custom_call_target="tpu_custom_call" | custom-call | flops 1073741824 | bytes 6291456 | tf_op jit(solution)/shard_map/pallas_call | solution.py:270
  115.2 7.6 %all-to-all-start.3 = ((f32[16,128,128]{2,1,0:T(8,128)}), f32[16,128,128]{2,1,0:T(8,128)S(1)}, u32[]{:S(2)}, u32[]{:S(2)}) async-start(f32[16,128,128]{2,1,0:T(8,128)} %get-tuple-element.22), calls=%async_computation.3 | async-start | bytes 2097152 | tf_op jit(solution)/shard_map/all_to_all | solution.py:56
  125.1 2.7 %collective-permute-start.25 = (f32[128,128]{1,0:T(8,128)S(1)}, f32[128,128]{1,0:T(8,128)S(1)}, u32[]{:S(2)}, u32[]{:S(2)}) collective-permute-start(f32[128,128]{1,0:T(8,128)S(1)} %get-tuple-element.26), channel_id=1, source_target_pairs={{0,192},{16,208},{32,224},{48,240},{64,128},{80,144},{96,160},{112... | collective-permute-start | bytes 196616 | tf_op jit(solution)/shard_map/ppermute | solution.py:61
  127.8 5.4 %collective-permute-start.31 = (f32[128,128]{1,0:T(8,128)S(1)}, f32[128,128]{1,0:T(8,128)S(1)}, u32[]{:S(2)}, u32[]{:S(2)}) collective-permute-start(f32[128,128]{1,0:T(8,128)S(1)} %get-tuple-element.27), channel_id=1, source_target_pairs={{0,32},{16,48},{32,0},{48,16},{64,96},{80,112},{96,64},{112,80},{1... | collective-permute-start | bytes 196616 | tf_op jit(solution)/shard_map/ppermute | solution.py:61
  133.2 2.1 %collective-permute-start.28 = (f32[128,128]{1,0:T(8,128)S(1)}, f32[128,128]{1,0:T(8,128)S(1)}, u32[]{:S(2)}, u32[]{:S(2)}) collective-permute-start(f32[128,128]{1,0:T(8,128)S(1)} %get-tuple-element.30), channel_id=1, source_target_pairs={{0,64},{16,80},{32,96},{48,112},{64,0},{80,16},{96,32},{112,48},{1... | collective-permute-start | bytes 196616 | tf_op jit(solution)/shard_map/ppermute | solution.py:61
  135.3 3.5 %collective-permute-start.27 = (f32[128,128]{1,0:T(8,128)S(1)}, f32[128,128]{1,0:T(8,128)S(1)}, u32[]{:S(2)}, u32[]{:S(2)}) collective-permute-start(f32[128,128]{1,0:T(8,128)S(1)} %get-tuple-element.31), channel_id=1, source_target_pairs={{0,160},{16,176},{32,128},{48,144},{64,224},{80,240},{96,192},{112... | collective-permute-start | bytes 196616 | tf_op jit(solution)/shard_map/ppermute | solution.py:61
  139.6 2.8 %collective-permute-done.27 = f32[128,128]{1,0:T(8,128)S(1)} collective-permute-done((f32[128,128]{1,0:T(8,128)S(1)}, f32[128,128]{1,0:T(8,128)S(1)}, u32[]{:S(2)}, u32[]{:S(2)}) %collective-permute-start.27) | collective-permute-done | bytes 65568 | tf_op jit(solution)/shard_map/ppermute | solution.py:61
  142.4 3.8 %collective-permute-done.26 = f32[128,128]{1,0:T(8,128)S(1)} collective-permute-done((f32[128,128]{1,0:T(8,128)S(1)}, f32[128,128]{1,0:T(8,128)S(1)}, u32[]{:S(2)}, u32[]{:S(2)}) %collective-permute-start.26) | collective-permute-done | bytes 65568 | tf_op jit(solution)/shard_map/ppermute | solution.py:61
  146.9 6.9 %all-to-all-done.3 = f32[16,128,128]{2,1,0:T(8,128)S(1)} async-done(((f32[16,128,128]{2,1,0:T(8,128)}), f32[16,128,128]{2,1,0:T(8,128)S(1)}, u32[]{:S(2)}, u32[]{:S(2)}) %all-to-all-start.3) | async-done | bytes 1048608 | tf_op jit(solution)/shard_map/all_to_all | solution.py:56
  (83 shorter events, 18.1 us)
Async XLA Ops:
  3.3 40.8 %all-to-all-start = ((f32[16,136,128]{2,1,0:T(8,128)}), f32[16,136,128]{2,1,0:T(8,128)S(1)}, u32[]{:S(2)}, u32[]{:S(2)}) async-start(f32[16,136,128]{2,1,0:T(8,128)} %get-tuple-element.14), calls=%async_computation | async-start | bytes 2228224 | tf_op jit(solution)/shard_map/all_to_all | solution.py:56
  15.1 11.1 %collective-permute-start.7 = (f32[2,136,128]{2,1,0:T(8,128)S(1)}, f32[2,136,128]{2,1,0:T(8,128)S(1)}, u32[]{:S(2)}, u32[]{:S(2)}) collective-permute-start(f32[2,136,128]{2,1,0:T(8,128)S(1)} %pad_maximum_fusion.refs_1_), channel_id=1, source_target_pairs={{0,224},{16,240},{32,192},{48,208},{64,160},{80,176},{96,128},{112... | collective-permute-start | bytes 417800 | tf_op jit(solution)/shard_map/ppermute | solution.py:61
  18.7 10.4 %collective-permute-start.6 = (f32[2,136,128]{2,1,0:T(8,128)S(1)}, f32[2,136,128]{2,1,0:T(8,128)S(1)}, u32[]{:S(2)}, u32[]{:S(2)}) collective-permute-start(f32[2,136,128]{2,1,0:T(8,128)S(1)} %pad_maximum_fusion.refs_1_), channel_id=1, source_target_pairs={{0,192},{16,208},{32,224},{48,240},{64,128},{80,144},{96,160},{112... | collective-permute-start | bytes 417800 | tf_op jit(solution)/shard_map/ppermute | solution.py:61
  19.6 13.1 %collective-permute-start.5 = (f32[2,136,128]{2,1,0:T(8,128)S(1)}, f32[2,136,128]{2,1,0:T(8,128)S(1)}, u32[]{:S(2)}, u32[]{:S(2)}) collective-permute-start(f32[2,136,128]{2,1,0:T(8,128)S(1)} %pad_maximum_fusion.refs_1_), channel_id=1, source_target_pairs={{0,160},{16,176},{32,128},{48,144},{64,224},{80,240},{96,192},{112... | collective-permute-start | bytes 417800 | tf_op jit(solution)/shard_map/ppermute | solution.py:61
  21.0 16.3 %collective-permute-start.4 = (f32[2,136,128]{2,1,0:T(8,128)S(1)}, f32[2,136,128]{2,1,0:T(8,128)S(1)}, u32[]{:S(2)}, u32[]{:S(2)}) collective-permute-start(f32[2,136,128]{2,1,0:T(8,128)S(1)} %pad_maximum_fusion.refs_1_), channel_id=1, source_target_pairs={{0,128},{16,144},{32,160},{48,176},{64,192},{80,208},{96,224},{112... | collective-permute-start | bytes 417800 | tf_op jit(solution)/shard_map/ppermute | solution.py:61
  21.6 15.6 %collective-permute-start.3 = (f32[2,136,128]{2,1,0:T(8,128)S(1)}, f32[2,136,128]{2,1,0:T(8,128)S(1)}, u32[]{:S(2)}, u32[]{:S(2)}) collective-permute-start(f32[2,136,128]{2,1,0:T(8,128)S(1)} %pad_maximum_fusion.refs_1_), channel_id=1, source_target_pairs={{0,96},{16,112},{32,64},{48,80},{64,32},{80,48},{96,0},{112,16},{1... | collective-permute-start | bytes 417800 | tf_op jit(solution)/shard_map/ppermute | solution.py:61
  26.2 11.1 %collective-permute-start.2 = (f32[2,136,128]{2,1,0:T(8,128)S(1)}, f32[2,136,128]{2,1,0:T(8,128)S(1)}, u32[]{:S(2)}, u32[]{:S(2)}) collective-permute-start(f32[2,136,128]{2,1,0:T(8,128)S(1)} %pad_maximum_fusion.refs_1_), channel_id=1, source_target_pairs={{0,64},{16,80},{32,96},{48,112},{64,0},{80,16},{96,32},{112,48},{1... | collective-permute-start | bytes 417800 | tf_op jit(solution)/shard_map/ppermute | solution.py:61
  29.1 8.2 %collective-permute-start.1 = (f32[2,136,128]{2,1,0:T(8,128)S(1)}, f32[2,136,128]{2,1,0:T(8,128)S(1)}, u32[]{:S(2)}, u32[]{:S(2)}) collective-permute-start(f32[2,136,128]{2,1,0:T(8,128)S(1)} %pad_maximum_fusion.refs_1_), channel_id=1, source_target_pairs={{0,32},{16,48},{32,0},{48,16},{64,96},{80,112},{96,64},{112,80},{1... | collective-permute-start | bytes 417800 | tf_op jit(solution)/shard_map/ppermute | solution.py:61
  50.0 29.1 %all-to-all-start.1 = ((f32[16,6,8,128]{3,2,1,0:T(8,128)}), f32[16,6,8,128]{3,2,1,0:T(8,128)S(1)}, u32[]{:S(2)}, u32[]{:S(2)}) async-start(f32[16,6,8,128]{3,2,1,0:T(8,128)} %get-tuple-element.16), calls=%async_computation.1 | async-start | bytes 786432 | tf_op jit(solution)/shard_map/all_to_all | solution.py:56
  60.8 6.4 %collective-permute-start.9 = (f32[2,6,8,128]{3,2,1,0:T(8,128)S(1)}, f32[2,6,8,128]{3,2,1,0:T(8,128)S(1)}, u32[]{:S(2)}, u32[]{:S(2)}) collective-permute-start(f32[2,6,8,128]{3,2,1,0:T(8,128)S(1)} %pad_maximum_fusion.10), channel_id=1, source_target_pairs={{0,32},{16,48},{32,0},{48,16},{64,96},{80,112},{96,64},{112,80},{1... | collective-permute-start | bytes 147464 | tf_op jit(solution)/shard_map/ppermute | solution.py:61
  60.9 11.9 %collective-permute-start.10 = (f32[2,6,8,128]{3,2,1,0:T(8,128)S(1)}, f32[2,6,8,128]{3,2,1,0:T(8,128)S(1)}, u32[]{:S(2)}, u32[]{:S(2)}) collective-permute-start(f32[2,6,8,128]{3,2,1,0:T(8,128)S(1)} %pad_maximum_fusion.11), channel_id=1, source_target_pairs={{0,64},{16,80},{32,96},{48,112},{64,0},{80,16},{96,32},{112,48},{1... | collective-permute-start | bytes 147464 | tf_op jit(solution)/shard_map/ppermute | solution.py:61
  65.0 7.8 %collective-permute-start.11 = (f32[2,6,8,128]{3,2,1,0:T(8,128)S(1)}, f32[2,6,8,128]{3,2,1,0:T(8,128)S(1)}, u32[]{:S(2)}, u32[]{:S(2)}) collective-permute-start(f32[2,6,8,128]{3,2,1,0:T(8,128)S(1)} %pad_maximum_fusion.12), channel_id=1, source_target_pairs={{0,96},{16,112},{32,64},{48,80},{64,32},{80,48},{96,0},{112,16},{1... | collective-permute-start | bytes 147464 | tf_op jit(solution)/shard_map/ppermute | solution.py:61
  65.6 7.2 %collective-permute-start.12 = (f32[2,6,8,128]{3,2,1,0:T(8,128)S(1)}, f32[2,6,8,128]{3,2,1,0:T(8,128)S(1)}, u32[]{:S(2)}, u32[]{:S(2)}) collective-permute-start(f32[2,6,8,128]{3,2,1,0:T(8,128)S(1)} %pad_maximum_fusion.13), channel_id=1, source_target_pairs={{0,128},{16,144},{32,160},{48,176},{64,192},{80,208},{96,224},{112... | collective-permute-start | bytes 147464 | tf_op jit(solution)/shard_map/ppermute | solution.py:61
  67.2 5.7 %collective-permute-start.13 = (f32[2,6,8,128]{3,2,1,0:T(8,128)S(1)}, f32[2,6,8,128]{3,2,1,0:T(8,128)S(1)}, u32[]{:S(2)}, u32[]{:S(2)}) collective-permute-start(f32[2,6,8,128]{3,2,1,0:T(8,128)S(1)} %pad_maximum_fusion.14), channel_id=1, source_target_pairs={{0,160},{16,176},{32,128},{48,144},{64,224},{80,240},{96,192},{112... | collective-permute-start | bytes 147464 | tf_op jit(solution)/shard_map/ppermute | solution.py:61
  67.3 8.1 %collective-permute-start.14 = (f32[2,6,8,128]{3,2,1,0:T(8,128)S(1)}, f32[2,6,8,128]{3,2,1,0:T(8,128)S(1)}, u32[]{:S(2)}, u32[]{:S(2)}) collective-permute-start(f32[2,6,8,128]{3,2,1,0:T(8,128)S(1)} %pad_maximum_fusion.15), channel_id=1, source_target_pairs={{0,192},{16,208},{32,224},{48,240},{64,128},{80,144},{96,160},{112... | collective-permute-start | bytes 147464 | tf_op jit(solution)/shard_map/ppermute | solution.py:61
  72.8 6.2 %collective-permute-start.15 = (f32[2,6,8,128]{3,2,1,0:T(8,128)S(1)}, f32[2,6,8,128]{3,2,1,0:T(8,128)S(1)}, u32[]{:S(2)}, u32[]{:S(2)}) collective-permute-start(f32[2,6,8,128]{3,2,1,0:T(8,128)S(1)} %pad_maximum_fusion.16), channel_id=1, source_target_pairs={{0,224},{16,240},{32,192},{48,208},{64,160},{80,176},{96,128},{112... | collective-permute-start | bytes 147464 | tf_op jit(solution)/shard_map/ppermute | solution.py:61
  82.8 26.0 %all-to-all-start.2 = ((f32[16,7,8,128]{3,2,1,0:T(8,128)}), f32[16,7,8,128]{3,2,1,0:T(8,128)S(1)}, u32[]{:S(2)}, u32[]{:S(2)}) async-start(f32[16,7,8,128]{3,2,1,0:T(8,128)} %get-tuple-element.19), calls=%async_computation.2 | async-start | bytes 917504 | tf_op jit(solution)/shard_map/all_to_all | solution.py:56
  93.8 6.0 %collective-permute-start.17 = (f32[2,7,8,128]{3,2,1,0:T(8,128)S(1)}, f32[2,7,8,128]{3,2,1,0:T(8,128)S(1)}, u32[]{:S(2)}, u32[]{:S(2)}) collective-permute-start(f32[2,7,8,128]{3,2,1,0:T(8,128)S(1)} %pad_maximum_fusion.2), channel_id=1, source_target_pairs={{0,32},{16,48},{32,0},{48,16},{64,96},{80,112},{96,64},{112,80},{1... | collective-permute-start | bytes 172040 | tf_op jit(solution)/shard_map/ppermute | solution.py:61
  93.9 8.6 %collective-permute-start.18 = (f32[2,7,8,128]{3,2,1,0:T(8,128)S(1)}, f32[2,7,8,128]{3,2,1,0:T(8,128)S(1)}, u32[]{:S(2)}, u32[]{:S(2)}) collective-permute-start(f32[2,7,8,128]{3,2,1,0:T(8,128)S(1)} %pad_maximum_fusion.3), channel_id=1, source_target_pairs={{0,64},{16,80},{32,96},{48,112},{64,0},{80,16},{96,32},{112,48},{1... | collective-permute-start | bytes 172040 | tf_op jit(solution)/shard_map/ppermute | solution.py:61
  95.4 10.3 %collective-permute-start.19 = (f32[2,7,8,128]{3,2,1,0:T(8,128)S(1)}, f32[2,7,8,128]{3,2,1,0:T(8,128)S(1)}, u32[]{:S(2)}, u32[]{:S(2)}) collective-permute-start(f32[2,7,8,128]{3,2,1,0:T(8,128)S(1)} %pad_maximum_fusion.4), channel_id=1, source_target_pairs={{0,96},{16,112},{32,64},{48,80},{64,32},{80,48},{96,0},{112,16},{1... | collective-permute-start | bytes 172040 | tf_op jit(solution)/shard_map/ppermute | solution.py:61
  98.6 7.2 %collective-permute-start.20 = (f32[2,7,8,128]{3,2,1,0:T(8,128)S(1)}, f32[2,7,8,128]{3,2,1,0:T(8,128)S(1)}, u32[]{:S(2)}, u32[]{:S(2)}) collective-permute-start(f32[2,7,8,128]{3,2,1,0:T(8,128)S(1)} %pad_maximum_fusion.5), channel_id=1, source_target_pairs={{0,128},{16,144},{32,160},{48,176},{64,192},{80,208},{96,224},{112... | collective-permute-start | bytes 172040 | tf_op jit(solution)/shard_map/ppermute | solution.py:61
  99.7 6.1 %collective-permute-start.21 = (f32[2,7,8,128]{3,2,1,0:T(8,128)S(1)}, f32[2,7,8,128]{3,2,1,0:T(8,128)S(1)}, u32[]{:S(2)}, u32[]{:S(2)}) collective-permute-start(f32[2,7,8,128]{3,2,1,0:T(8,128)S(1)} %pad_maximum_fusion.6), channel_id=1, source_target_pairs={{0,160},{16,176},{32,128},{48,144},{64,224},{80,240},{96,192},{112... | collective-permute-start | bytes 172040 | tf_op jit(solution)/shard_map/ppermute | solution.py:61
  99.8 6.8 %collective-permute-start.22 = (f32[2,7,8,128]{3,2,1,0:T(8,128)S(1)}, f32[2,7,8,128]{3,2,1,0:T(8,128)S(1)}, u32[]{:S(2)}, u32[]{:S(2)}) collective-permute-start(f32[2,7,8,128]{3,2,1,0:T(8,128)S(1)} %pad_maximum_fusion.7), channel_id=1, source_target_pairs={{0,192},{16,208},{32,224},{48,240},{64,128},{80,144},{96,160},{112... | collective-permute-start | bytes 172040 | tf_op jit(solution)/shard_map/ppermute | solution.py:61
  102.5 6.3 %collective-permute-start.23 = (f32[2,7,8,128]{3,2,1,0:T(8,128)S(1)}, f32[2,7,8,128]{3,2,1,0:T(8,128)S(1)}, u32[]{:S(2)}, u32[]{:S(2)}) collective-permute-start(f32[2,7,8,128]{3,2,1,0:T(8,128)S(1)} %pad_maximum_fusion.8), channel_id=1, source_target_pairs={{0,224},{16,240},{32,192},{48,208},{64,160},{80,176},{96,128},{112... | collective-permute-start | bytes 172040 | tf_op jit(solution)/shard_map/ppermute | solution.py:61
  115.2 38.6 %all-to-all-start.3 = ((f32[16,128,128]{2,1,0:T(8,128)}), f32[16,128,128]{2,1,0:T(8,128)S(1)}, u32[]{:S(2)}, u32[]{:S(2)}) async-start(f32[16,128,128]{2,1,0:T(8,128)} %get-tuple-element.22), calls=%async_computation.3 | async-start | bytes 2097152 | tf_op jit(solution)/shard_map/all_to_all | solution.py:56
  125.1 10.1 %collective-permute-start.25 = (f32[128,128]{1,0:T(8,128)S(1)}, f32[128,128]{1,0:T(8,128)S(1)}, u32[]{:S(2)}, u32[]{:S(2)}) collective-permute-start(f32[128,128]{1,0:T(8,128)S(1)} %get-tuple-element.26), channel_id=1, source_target_pairs={{0,192},{16,208},{32,224},{48,240},{64,128},{80,144},{96,160},{112... | collective-permute-start | bytes 196616 | tf_op jit(solution)/shard_map/ppermute | solution.py:61
  127.8 11.0 %collective-permute-start.31 = (f32[128,128]{1,0:T(8,128)S(1)}, f32[128,128]{1,0:T(8,128)S(1)}, u32[]{:S(2)}, u32[]{:S(2)}) collective-permute-start(f32[128,128]{1,0:T(8,128)S(1)} %get-tuple-element.27), channel_id=1, source_target_pairs={{0,32},{16,48},{32,0},{48,16},{64,96},{80,112},{96,64},{112,80},{1... | collective-permute-start | bytes 196616 | tf_op jit(solution)/shard_map/ppermute | solution.py:61
  133.2 6.4 %collective-permute-start.30 = (f32[128,128]{1,0:T(8,128)S(1)}, f32[128,128]{1,0:T(8,128)S(1)}, u32[]{:S(2)}, u32[]{:S(2)}) collective-permute-start(f32[128,128]{1,0:T(8,128)S(1)} %get-tuple-element.28), channel_id=1, source_target_pairs={{0,96},{16,112},{32,64},{48,80},{64,32},{80,48},{96,0},{112,16},{1... | collective-permute-start | bytes 196616 | tf_op jit(solution)/shard_map/ppermute | solution.py:61
  133.2 6.4 %collective-permute-start.29 = (f32[128,128]{1,0:T(8,128)S(1)}, f32[128,128]{1,0:T(8,128)S(1)}, u32[]{:S(2)}, u32[]{:S(2)}) collective-permute-start(f32[128,128]{1,0:T(8,128)S(1)} %get-tuple-element.29), channel_id=1, source_target_pairs={{0,128},{16,144},{32,160},{48,176},{64,192},{80,208},{96,224},{112... | collective-permute-start | bytes 196616 | tf_op jit(solution)/shard_map/ppermute | solution.py:61
  133.2 6.4 %collective-permute-start.28 = (f32[128,128]{1,0:T(8,128)S(1)}, f32[128,128]{1,0:T(8,128)S(1)}, u32[]{:S(2)}, u32[]{:S(2)}) collective-permute-start(f32[128,128]{1,0:T(8,128)S(1)} %get-tuple-element.30), channel_id=1, source_target_pairs={{0,64},{16,80},{32,96},{48,112},{64,0},{80,16},{96,32},{112,48},{1... | collective-permute-start | bytes 196616 | tf_op jit(solution)/shard_map/ppermute | solution.py:61
  135.3 7.1 %collective-permute-start.27 = (f32[128,128]{1,0:T(8,128)S(1)}, f32[128,128]{1,0:T(8,128)S(1)}, u32[]{:S(2)}, u32[]{:S(2)}) collective-permute-start(f32[128,128]{1,0:T(8,128)S(1)} %get-tuple-element.31), channel_id=1, source_target_pairs={{0,160},{16,176},{32,128},{48,144},{64,224},{80,240},{96,192},{112... | collective-permute-start | bytes 196616 | tf_op jit(solution)/shard_map/ppermute | solution.py:61
  138.8 7.5 %collective-permute-start.26 = (f32[128,128]{1,0:T(8,128)S(1)}, f32[128,128]{1,0:T(8,128)S(1)}, u32[]{:S(2)}, u32[]{:S(2)}) collective-permute-start(f32[128,128]{1,0:T(8,128)S(1)} %get-tuple-element.32), channel_id=1, source_target_pairs={{0,224},{16,240},{32,192},{48,208},{64,160},{80,176},{96,128},{112... | collective-permute-start | bytes 196616 | tf_op jit(solution)/shard_map/ppermute | solution.py:61
  (10 other events, 93.1 us)

commit v5 on v4

--- a/solution.py
+++ b/solution.py
@@ -283,7 +283,7 @@
 
 def update_kernel(at_ref, *refs):
     all_refs, back_refs, outs, refs = refs[:9], refs[9:18], refs[18:21], refs[21:]
-    pieces, sums_a, sums_b, others_a, others_b, notes, sems = refs
+    pieces, sums_a, sums_b, others_a, others_b, notes, names, sems = refs
     members, slots, rows, _ = back_refs[0].shape
     totals, others = (sums_a, sums_b), (others_a, others_b)
     side = members * rows
@@ -305,23 +305,20 @@
         for slot in range(slots):
             for kind, grad in enumerate((back_refs[0][place, slot], back_refs[1 + place // 2][place % 2, slot])):
                 block = name_of(notes, kind, place, slot)
+                names[kind, place, slot] = jnp.minimum(block, members - 1)
                 sums[kind][block] = sums[kind][block] + grad
     sums_a[:members] = pieces[0] - step_rate * (sums_a[:members] + others_a[:members])
     for place in range(members):
         owner = at_ref[0] ^ place
         sums_b[owner] = pieces[1, place] - step_rate * (sums_b[owner] + others_b[owner])
 
-    def deal(index, carry):
-        for way in range(2):
-            place = 2 * index + way
-            for slot in range(slots):
-                outs[0][place, slot] = sums_a[jnp.minimum(name_of(notes, 0, place, slot), members - 1)]
-                outs[1 + way][index, slot] = sums_b[jnp.minimum(name_of(notes, 1, place, slot), members - 1)]
-            outs[0][place, slots] = sums_a[place]
-            outs[1 + way][index, slots] = sums_b[at_ref[0] ^ place]
-        return carry
-
-    lax.fori_loop(0, members // 2, deal, 0)
+    for place in range(members):
+        out_b = outs[1 + place % 2].at[place // 2]
+        for slot in range(slots):
+            outs[0][place, slot] = sums_a[names[0, place, slot]]
+            out_b[slot] = sums_b[names[1, place, slot]]
+        outs[0][place, slots] = sums_a[place]
+        out_b[slots] = sums_b[at_ref[0] ^ place]
 
 
 def update(at, all_a, all_b, back_a, back_b):
@@ -336,6 +333,7 @@
             pltpu.VMEM((2, members, rows, rank), jnp.float32),
             *[pltpu.VMEM((members + 1, rows, rank), jnp.float32)] * 4,
             pltpu.SMEM((2, members, rank), jnp.float32),
+            pltpu.SMEM((2, members, slots), jnp.int32),
             pltpu.SemaphoreType.DMA((2, 9)),
         ],
         cost_estimate=small_cost,
@@ -364,7 +362,9 @@
     dealt_a, *dealt_b = update(at, all_a, all_b, back_a, back_b)
     held_a = swap_col(dealt_a)
     held_b = swap_row(*dealt_b)
-    grad_a, even_b, odd_b, base_b = block_gradients(at, where, live, held_a, held_b, factor_c, counts, members, True)
+    grad_a, even_b, odd_b, base_b = block_gradients(
+        at, where, live, held_a, held_b, factor_c, counts, members, True
+    )
     terms_a = swap_col(grad_a)
     sums = even_b + shift_row(odd_b, 1)
     terms_b = [sums[0]]

time: 155 us -> 155 us (level)
  no operation moved by 1% of the time
where the time goes in v5:
time: 155 us; the launch traced here: 154 us
  starting transfers between devices  90.2 us (58%)
  waiting for transfers between devices  40.6 us (26%)
  Pallas kernels  17.5 us (11%)
  other arithmetic  2.16 us (1%)
  local copies, waits for them, and re-layouts  1.85 us (1%)
  between operations  1.6 us (1%)
    ppermute x32, starting transfers between devices, shift_row(): lax.ppermute(value, 'row', [(member, member ^ change) for member in range...  55.9 us
    all_to_all x4, starting transfers between devices, swap_col(): return lax.all_to_all(sent, 'col', 0, 0, tiled=True)  34.4 us
    ppermute x32, waiting for transfers between devices, shift_row(): lax.ppermute(value, 'row', [(member, member ^ change) for member in range...  27 us
    all_to_all x4, waiting for transfers between devices, swap_col(): return lax.all_to_all(sent, 'col', 0, 0, tiled=True)  13.7 us
    pallas_call x2, Pallas kernels, block_gradients(): pl.pallas_call(kernel, out_shape=shapes, in_specs=[smem] * 3 + [vmem] * 9...  12.2 us
    pallas_call x1, Pallas kernels, update(): pl.pallas_call(update_kernel, out_shape=(shape_of(members, slots + 1, row...  3.32 us
  transfers between devices with their start and end apart: 36, of which 15 were waited for; matrix products, arithmetic and copies ran while one was open for 2% of the time, Pallas kernels for 0%

profile of v5, /device:TPU:8, one launch (start us, length us, event | category | flops | bytes accessed | tf_op | source)
XLA Modules:
  0.0 154.0 jit_solution(3870324388219240147)
XLA Ops:
  1.3 2.0 %shard_map.77 = (f32[16,136,128]{2,1,0:T(8,128)}, f32[136,128]{1,0:T(8,128)}) custom-call(s32[3,1,1,6]{3,2,1,0:T(1,128)} %where_ref.5, s32[1,1]{1,0:T(1,128)S(6)} %copy.8.live_ref, f32[128,128]{1,0:T(8,128)} %a_ref.1, f32[128,128]{1,0:T(8,128)} %b_ref.1), custom_call_target="tpu_custom_call" | custom-call | flops 1048576 | bytes 1048576 | tf_op jit(solution)/shard_map/pallas_call | solution.py:98
  3.3 10.4 %all-to-all-start = ((f32[16,136,128]{2,1,0:T(8,128)}), f32[16,136,128]{2,1,0:T(8,128)S(1)}, u32[]{:S(2)}, u32[]{:S(2)}) async-start(f32[16,136,128]{2,1,0:T(8,128)} %get-tuple-element.14), calls=%async_computation | async-start | bytes 2228224 | tf_op jit(solution)/shard_map/all_to_all | solution.py:56
  15.1 3.6 %collective-permute-start.7 = (f32[2,136,128]{2,1,0:T(8,128)S(1)}, f32[2,136,128]{2,1,0:T(8,128)S(1)}, u32[]{:S(2)}, u32[]{:S(2)}) collective-permute-start(f32[2,136,128]{2,1,0:T(8,128)S(1)} %pad_maximum_fusion.refs_1_), channel_id=1, source_target_pairs={{0,224},{16,240},{32,192},{48,208},{64,160},{80,176},{96,128},{112... | collective-permute-start | bytes 417800 | tf_op jit(solution)/shard_map/ppermute | solution.py:61
  21.6 2.8 %collective-permute-start.3 = (f32[2,136,128]{2,1,0:T(8,128)S(1)}, f32[2,136,128]{2,1,0:T(8,128)S(1)}, u32[]{:S(2)}, u32[]{:S(2)}) collective-permute-start(f32[2,136,128]{2,1,0:T(8,128)S(1)} %pad_maximum_fusion.refs_1_), channel_id=1, source_target_pairs={{0,96},{16,112},{32,64},{48,80},{64,32},{80,48},{96,0},{112,16},{1... | collective-permute-start | bytes 417800 | tf_op jit(solution)/shard_map/ppermute | solution.py:61
  24.4 1.8 %collective-permute-done.7.refs_8_ = f32[2,136,128]{2,1,0:T(8,128)S(1)} collective-permute-done((f32[2,136,128]{2,1,0:T(8,128)S(1)}, f32[2,136,128]{2,1,0:T(8,128)S(1)}, u32[]{:S(2)}, u32[]{:S(2)}) %collective-permute-start.7) | collective-permute-done | bytes 139296 | tf_op jit(solution)/shard_map/ppermute | solution.py:61
  26.2 2.0 %collective-permute-start.2 = (f32[2,136,128]{2,1,0:T(8,128)S(1)}, f32[2,136,128]{2,1,0:T(8,128)S(1)}, u32[]{:S(2)}, u32[]{:S(2)}) collective-permute-start(f32[2,136,128]{2,1,0:T(8,128)S(1)} %pad_maximum_fusion.refs_1_), channel_id=1, source_target_pairs={{0,64},{16,80},{32,96},{48,112},{64,0},{80,16},{96,32},{112,48},{1... | collective-permute-start | bytes 417800 | tf_op jit(solution)/shard_map/ppermute | solution.py:61
  29.1 3.1 %collective-permute-start.1 = (f32[2,136,128]{2,1,0:T(8,128)S(1)}, f32[2,136,128]{2,1,0:T(8,128)S(1)}, u32[]{:S(2)}, u32[]{:S(2)}) collective-permute-start(f32[2,136,128]{2,1,0:T(8,128)S(1)} %pad_maximum_fusion.refs_1_), channel_id=1, source_target_pairs={{0,32},{16,48},{32,0},{48,16},{64,96},{80,112},{96,64},{112,80},{1... | collective-permute-start | bytes 417800 | tf_op jit(solution)/shard_map/ppermute | solution.py:61
  32.8 4.5 %collective-permute-done.4.refs_5_ = f32[2,136,128]{2,1,0:T(8,128)S(1)} collective-permute-done((f32[2,136,128]{2,1,0:T(8,128)S(1)}, f32[2,136,128]{2,1,0:T(8,128)S(1)}, u32[]{:S(2)}, u32[]{:S(2)}) %collective-permute-start.4) | collective-permute-done | bytes 139296 | tf_op jit(solution)/shard_map/ppermute | solution.py:61
  37.3 6.8 %all-to-all-done.refs_0_ = f32[16,136,128]{2,1,0:T(8,128)S(1)} async-done(((f32[16,136,128]{2,1,0:T(8,128)}), f32[16,136,128]{2,1,0:T(8,128)S(1)}, u32[]{:S(2)}, u32[]{:S(2)}) %all-to-all-start) | async-done | bytes 1114144 | tf_op jit(solution)/shard_map/all_to_all | solution.py:56
  44.1 5.9 %shard_map.78 = (f32[16,6,8,128]{3,2,1,0:T(8,128)}, f32[8,6,8,128]{3,2,1,0:T(8,128)}, f32[8,6,8,128]{3,2,1,0:T(8,128)}) custom-call(s32[2]{0:T(128)} %pad_add_fusion.at_ref, s32[3,1,1,6]{3,2,1,0:T(1,128)} %where_ref.5, s32[1,1]{1,0:T(1,128)S(6)} %copy.8.live_ref, f32[16,136,128]{2,1,0:T(8,128)S(1)} %all-to-all-done.refs_0_, ...), custom_call_target="tpu_custom_call" | custom-call | flops 1073741824 | bytes 6291456 | tf_op jit(solution)/shard_map/pallas_call | solution.py:270
  50.0 7.4 %all-to-all-start.1 = ((f32[16,6,8,128]{3,2,1,0:T(8,128)}), f32[16,6,8,128]{3,2,1,0:T(8,128)S(1)}, u32[]{:S(2)}, u32[]{:S(2)}) async-start(f32[16,6,8,128]{3,2,1,0:T(8,128)} %get-tuple-element.16), calls=%async_computation.1 | async-start | bytes 786432 | tf_op jit(solution)/shard_map/all_to_all | solution.py:56
  57.4 2.1 %collective-permute-start.8 = (f32[8,6,8,128]{3,2,1,0:T(8,128)}, f32[8,6,8,128]{3,2,1,0:T(8,128)S(1)}, u32[]{:S(2)}, u32[]{:S(2)}) collective-permute-start(f32[8,6,8,128]{3,2,1,0:T(8,128)} %get-tuple-element.18), channel_id=1, source_target_pairs={{0,16},{16,0},{32,48},{48,32},{64,80},{80,64},{96,112},{112,96},{1... | collective-permute-start | bytes 589832 | tf_op jit(solution)/shard_map/ppermute | solution.py:61
  60.9 4.1 %collective-permute-start.10 = (f32[2,6,8,128]{3,2,1,0:T(8,128)S(1)}, f32[2,6,8,128]{3,2,1,0:T(8,128)S(1)}, u32[]{:S(2)}, u32[]{:S(2)}) collective-permute-start(f32[2,6,8,128]{3,2,1,0:T(8,128)S(1)} %pad_maximum_fusion.11), channel_id=1, source_target_pairs={{0,64},{16,80},{32,96},{48,112},{64,0},{80,16},{96,32},{112,48},{1... | collective-permute-start | bytes 147464 | tf_op jit(solution)/shard_map/ppermute | solution.py:61
  65.6 1.6 %collective-permute-start.12 = (f32[2,6,8,128]{3,2,1,0:T(8,128)S(1)}, f32[2,6,8,128]{3,2,1,0:T(8,128)S(1)}, u32[]{:S(2)}, u32[]{:S(2)}) collective-permute-start(f32[2,6,8,128]{3,2,1,0:T(8,128)S(1)} %pad_maximum_fusion.13), channel_id=1, source_target_pairs={{0,128},{16,144},{32,160},{48,176},{64,192},{80,208},{96,224},{112... | collective-permute-start | bytes 147464 | tf_op jit(solution)/shard_map/ppermute | solution.py:61
  67.3 5.6 %collective-permute-start.14 = (f32[2,6,8,128]{3,2,1,0:T(8,128)S(1)}, f32[2,6,8,128]{3,2,1,0:T(8,128)S(1)}, u32[]{:S(2)}, u32[]{:S(2)}) collective-permute-start(f32[2,6,8,128]{3,2,1,0:T(8,128)S(1)} %pad_maximum_fusion.15), channel_id=1, source_target_pairs={{0,192},{16,208},{32,224},{48,240},{64,128},{80,144},{96,160},{112... | collective-permute-start | bytes 147464 | tf_op jit(solution)/shard_map/ppermute | solution.py:61
  72.9 2.4 %collective-permute-done.14.refs_16_ = f32[2,6,8,128]{3,2,1,0:T(8,128)S(1)} collective-permute-done((f32[2,6,8,128]{3,2,1,0:T(8,128)S(1)}, f32[2,6,8,128]{3,2,1,0:T(8,128)S(1)}, u32[]{:S(2)}, u32[]{:S(2)}) %collective-permute-start.14) | collective-permute-done | bytes 49184 | tf_op jit(solution)/shard_map/ppermute | solution.py:61
  75.3 3.7 %collective-permute-done.15.refs_17_ = f32[2,6,8,128]{3,2,1,0:T(8,128)S(1)} collective-permute-done((f32[2,6,8,128]{3,2,1,0:T(8,128)S(1)}, f32[2,6,8,128]{3,2,1,0:T(8,128)S(1)}, u32[]{:S(2)}, u32[]{:S(2)}) %collective-permute-start.15) | collective-permute-done | bytes 49184 | tf_op jit(solution)/shard_map/ppermute | solution.py:61
  79.1 3.3 %shard_map.79 = (f32[16,7,8,128]{3,2,1,0:T(8,128)}, f32[8,7,8,128]{3,2,1,0:T(8,128)}, f32[8,7,8,128]{3,2,1,0:T(8,128)}) custom-call(s32[2]{0:T(128)} %pad_add_fusion.at_ref, f32[16,136,128]{2,1,0:T(8,128)S(1)} %copy-done.1, f32[2,136,128]{2,1,0:T(8,128)S(1)} %pad_maximum_fusion.refs_1_, f32[2,136,128]{2,1,0:T(8,128)S(1)} %collective-permute-done.1.refs_2_, ...), custom_call_target="tpu_custom_call" | custom-call | flops 1048576 | bytes 1048576 | tf_op jit(solution)/shard_map/pallas_call | solution.py:327
  82.4 8.9 %all-to-all-start.2 = ((f32[16,7,8,128]{3,2,1,0:T(8,128)}), f32[16,7,8,128]{3,2,1,0:T(8,128)S(1)}, u32[]{:S(2)}, u32[]{:S(2)}) async-start(f32[16,7,8,128]{3,2,1,0:T(8,128)} %get-tuple-element.19), calls=%async_computation.2 | async-start | bytes 917504 | tf_op jit(solution)/shard_map/all_to_all | solution.py:56
  95.0 3.1 %collective-permute-start.19 = (f32[2,7,8,128]{3,2,1,0:T(8,128)S(1)}, f32[2,7,8,128]{3,2,1,0:T(8,128)S(1)}, u32[]{:S(2)}, u32[]{:S(2)}) collective-permute-start(f32[2,7,8,128]{3,2,1,0:T(8,128)S(1)} %pad_maximum_fusion.4), channel_id=1, source_target_pairs={{0,96},{16,112},{32,64},{48,80},{64,32},{80,48},{96,0},{112,16},{1... | collective-permute-start | bytes 172040 | tf_op jit(solution)/shard_map/ppermute | solution.py:61
  99.3 2.7 %collective-permute-start.22 = (f32[2,7,8,128]{3,2,1,0:T(8,128)S(1)}, f32[2,7,8,128]{3,2,1,0:T(8,128)S(1)}, u32[]{:S(2)}, u32[]{:S(2)}) collective-permute-start(f32[2,7,8,128]{3,2,1,0:T(8,128)S(1)} %pad_maximum_fusion.7), channel_id=1, source_target_pairs={{0,192},{16,208},{32,224},{48,240},{64,128},{80,144},{96,160},{112... | collective-permute-start | bytes 172040 | tf_op jit(solution)/shard_map/ppermute | solution.py:61
  102.1 3.3 %collective-permute-start.23 = (f32[2,7,8,128]{3,2,1,0:T(8,128)S(1)}, f32[2,7,8,128]{3,2,1,0:T(8,128)S(1)}, u32[]{:S(2)}, u32[]{:S(2)}) collective-permute-start(f32[2,7,8,128]{3,2,1,0:T(8,128)S(1)} %pad_maximum_fusion.8), channel_id=1, source_target_pairs={{0,224},{16,240},{32,192},{48,208},{64,160},{80,176},{96,128},{112... | collective-permute-start | bytes 172040 | tf_op jit(solution)/shard_map/ppermute | solution.py:61
  106.1 2.3 %collective-permute-done.23.refs_8_ = f32[2,7,8,128]{3,2,1,0:T(8,128)S(1)} collective-permute-done((f32[2,7,8,128]{3,2,1,0:T(8,128)S(1)}, f32[2,7,8,128]{3,2,1,0:T(8,128)S(1)}, u32[]{:S(2)}, u32[]{:S(2)}) %collective-permute-start.23) | collective-permute-done | bytes 57376 | tf_op jit(solution)/shard_map/ppermute | solution.py:61
  108.4 6.3 %shard_map.80 = (f32[16,128,128]{2,1,0:T(8,128)}, f32[8,128,128]{2,1,0:T(8,128)}, f32[8,128,128]{2,1,0:T(8,128)}, f32[128,128]{1,0:T(8,128)}) custom-call(s32[2]{0:T(128)} %pad_add_fusion.at_ref, s32[3,1,1,6]{3,2,1,0:T(1,128)} %where_ref.5, s32[1,1]{1,0:T(1,128)S(6)} %copy.8.live_ref, f32[16,7,8,128]{3,2,1,0:T(8,128)S(1)} %all-to-all-done.2.refs_0_, ...), custom_call_target="tpu_custom_call" | custom-call | flops 1073741824 | bytes 6291456 | tf_op jit(solution)/shard_map/pallas_call | solution.py:270
  114.7 7.6 %all-to-all-start.3 = ((f32[16,128,128]{2,1,0:T(8,128)}), f32[16,128,128]{2,1,0:T(8,128)S(1)}, u32[]{:S(2)}, u32[]{:S(2)}) async-start(f32[16,128,128]{2,1,0:T(8,128)} %get-tuple-element.22), calls=%async_computation.3 | async-start | bytes 2097152 | tf_op jit(solution)/shard_map/all_to_all | solution.py:56
  124.8 2.7 %collective-permute-start.25 = (f32[128,128]{1,0:T(8,128)S(1)}, f32[128,128]{1,0:T(8,128)S(1)}, u32[]{:S(2)}, u32[]{:S(2)}) collective-permute-start(f32[128,128]{1,0:T(8,128)S(1)} %get-tuple-element.26), channel_id=1, source_target_pairs={{0,192},{16,208},{32,224},{48,240},{64,128},{80,144},{96,160},{112... | collective-permute-start | bytes 196616 | tf_op jit(solution)/shard_map/ppermute | solution.py:61
  127.4 5.4 %collective-permute-start.31 = (f32[128,128]{1,0:T(8,128)S(1)}, f32[128,128]{1,0:T(8,128)S(1)}, u32[]{:S(2)}, u32[]{:S(2)}) collective-permute-start(f32[128,128]{1,0:T(8,128)S(1)} %get-tuple-element.27), channel_id=1, source_target_pairs={{0,32},{16,48},{32,0},{48,16},{64,96},{80,112},{96,64},{112,80},{1... | collective-permute-start | bytes 196616 | tf_op jit(solution)/shard_map/ppermute | solution.py:61
  132.8 2.1 %collective-permute-start.28 = (f32[128,128]{1,0:T(8,128)S(1)}, f32[128,128]{1,0:T(8,128)S(1)}, u32[]{:S(2)}, u32[]{:S(2)}) collective-permute-start(f32[128,128]{1,0:T(8,128)S(1)} %get-tuple-element.30), channel_id=1, source_target_pairs={{0,64},{16,80},{32,96},{48,112},{64,0},{80,16},{96,32},{112,48},{1... | collective-permute-start | bytes 196616 | tf_op jit(solution)/shard_map/ppermute | solution.py:61
  134.9 3.5 %collective-permute-start.27 = (f32[128,128]{1,0:T(8,128)S(1)}, f32[128,128]{1,0:T(8,128)S(1)}, u32[]{:S(2)}, u32[]{:S(2)}) collective-permute-start(f32[128,128]{1,0:T(8,128)S(1)} %get-tuple-element.31), channel_id=1, source_target_pairs={{0,160},{16,176},{32,128},{48,144},{64,224},{80,240},{96,192},{112... | collective-permute-start | bytes 196616 | tf_op jit(solution)/shard_map/ppermute | solution.py:61
  139.3 2.8 %collective-permute-done.27 = f32[128,128]{1,0:T(8,128)S(1)} collective-permute-done((f32[128,128]{1,0:T(8,128)S(1)}, f32[128,128]{1,0:T(8,128)S(1)}, u32[]{:S(2)}, u32[]{:S(2)}) %collective-permute-start.27) | collective-permute-done | bytes 65568 | tf_op jit(solution)/shard_map/ppermute | solution.py:61
  142.0 3.8 %collective-permute-done.26 = f32[128,128]{1,0:T(8,128)S(1)} collective-permute-done((f32[128,128]{1,0:T(8,128)S(1)}, f32[128,128]{1,0:T(8,128)S(1)}, u32[]{:S(2)}, u32[]{:S(2)}) %collective-permute-start.26) | collective-permute-done | bytes 65568 | tf_op jit(solution)/shard_map/ppermute | solution.py:61
  146.5 6.9 %all-to-all-done.3 = f32[16,128,128]{2,1,0:T(8,128)S(1)} async-done(((f32[16,128,128]{2,1,0:T(8,128)}), f32[16,128,128]{2,1,0:T(8,128)S(1)}, u32[]{:S(2)}, u32[]{:S(2)}) %all-to-all-start.3) | async-done | bytes 1048608 | tf_op jit(solution)/shard_map/all_to_all | solution.py:56
  (83 shorter events, 18.1 us)
Async XLA Ops:
  3.3 40.8 %all-to-all-start = ((f32[16,136,128]{2,1,0:T(8,128)}), f32[16,136,128]{2,1,0:T(8,128)S(1)}, u32[]{:S(2)}, u32[]{:S(2)}) async-start(f32[16,136,128]{2,1,0:T(8,128)} %get-tuple-element.14), calls=%async_computation | async-start | bytes 2228224 | tf_op jit(solution)/shard_map/all_to_all | solution.py:56
  15.1 11.1 %collective-permute-start.7 = (f32[2,136,128]{2,1,0:T(8,128)S(1)}, f32[2,136,128]{2,1,0:T(8,128)S(1)}, u32[]{:S(2)}, u32[]{:S(2)}) collective-permute-start(f32[2,136,128]{2,1,0:T(8,128)S(1)} %pad_maximum_fusion.refs_1_), channel_id=1, source_target_pairs={{0,224},{16,240},{32,192},{48,208},{64,160},{80,176},{96,128},{112... | collective-permute-start | bytes 417800 | tf_op jit(solution)/shard_map/ppermute | solution.py:61
  18.7 10.4 %collective-permute-start.6 = (f32[2,136,128]{2,1,0:T(8,128)S(1)}, f32[2,136,128]{2,1,0:T(8,128)S(1)}, u32[]{:S(2)}, u32[]{:S(2)}) collective-permute-start(f32[2,136,128]{2,1,0:T(8,128)S(1)} %pad_maximum_fusion.refs_1_), channel_id=1, source_target_pairs={{0,192},{16,208},{32,224},{48,240},{64,128},{80,144},{96,160},{112... | collective-permute-start | bytes 417800 | tf_op jit(solution)/shard_map/ppermute | solution.py:61
  19.6 13.1 %collective-permute-start.5 = (f32[2,136,128]{2,1,0:T(8,128)S(1)}, f32[2,136,128]{2,1,0:T(8,128)S(1)}, u32[]{:S(2)}, u32[]{:S(2)}) collective-permute-start(f32[2,136,128]{2,1,0:T(8,128)S(1)} %pad_maximum_fusion.refs_1_), channel_id=1, source_target_pairs={{0,160},{16,176},{32,128},{48,144},{64,224},{80,240},{96,192},{112... | collective-permute-start | bytes 417800 | tf_op jit(solution)/shard_map/ppermute | solution.py:61
  21.0 16.3 %collective-permute-start.4 = (f32[2,136,128]{2,1,0:T(8,128)S(1)}, f32[2,136,128]{2,1,0:T(8,128)S(1)}, u32[]{:S(2)}, u32[]{:S(2)}) collective-permute-start(f32[2,136,128]{2,1,0:T(8,128)S(1)} %pad_maximum_fusion.refs_1_), channel_id=1, source_target_pairs={{0,128},{16,144},{32,160},{48,176},{64,192},{80,208},{96,224},{112... | collective-permute-start | bytes 417800 | tf_op jit(solution)/shard_map/ppermute | solution.py:61
  21.6 15.6 %collective-permute-start.3 = (f32[2,136,128]{2,1,0:T(8,128)S(1)}, f32[2,136,128]{2,1,0:T(8,128)S(1)}, u32[]{:S(2)}, u32[]{:S(2)}) collective-permute-start(f32[2,136,128]{2,1,0:T(8,128)S(1)} %pad_maximum_fusion.refs_1_), channel_id=1, source_target_pairs={{0,96},{16,112},{32,64},{48,80},{64,32},{80,48},{96,0},{112,16},{1... | collective-permute-start | bytes 417800 | tf_op jit(solution)/shard_map/ppermute | solution.py:61
  26.2 11.1 %collective-permute-start.2 = (f32[2,136,128]{2,1,0:T(8,128)S(1)}, f32[2,136,128]{2,1,0:T(8,128)S(1)}, u32[]{:S(2)}, u32[]{:S(2)}) collective-permute-start(f32[2,136,128]{2,1,0:T(8,128)S(1)} %pad_maximum_fusion.refs_1_), channel_id=1, source_target_pairs={{0,64},{16,80},{32,96},{48,112},{64,0},{80,16},{96,32},{112,48},{1... | collective-permute-start | bytes 417800 | tf_op jit(solution)/shard_map/ppermute | solution.py:61
  29.1 8.2 %collective-permute-start.1 = (f32[2,136,128]{2,1,0:T(8,128)S(1)}, f32[2,136,128]{2,1,0:T(8,128)S(1)}, u32[]{:S(2)}, u32[]{:S(2)}) collective-permute-start(f32[2,136,128]{2,1,0:T(8,128)S(1)} %pad_maximum_fusion.refs_1_), channel_id=1, source_target_pairs={{0,32},{16,48},{32,0},{48,16},{64,96},{80,112},{96,64},{112,80},{1... | collective-permute-start | bytes 417800 | tf_op jit(solution)/shard_map/ppermute | solution.py:61
  50.0 29.1 %all-to-all-start.1 = ((f32[16,6,8,128]{3,2,1,0:T(8,128)}), f32[16,6,8,128]{3,2,1,0:T(8,128)S(1)}, u32[]{:S(2)}, u32[]{:S(2)}) async-start(f32[16,6,8,128]{3,2,1,0:T(8,128)} %get-tuple-element.16), calls=%async_computation.1 | async-start | bytes 786432 | tf_op jit(solution)/shard_map/all_to_all | solution.py:56
  60.8 6.4 %collective-permute-start.9 = (f32[2,6,8,128]{3,2,1,0:T(8,128)S(1)}, f32[2,6,8,128]{3,2,1,0:T(8,128)S(1)}, u32[]{:S(2)}, u32[]{:S(2)}) collective-permute-start(f32[2,6,8,128]{3,2,1,0:T(8,128)S(1)} %pad_maximum_fusion.10), channel_id=1, source_target_pairs={{0,32},{16,48},{32,0},{48,16},{64,96},{80,112},{96,64},{112,80},{1... | collective-permute-start | bytes 147464 | tf_op jit(solution)/shard_map/ppermute | solution.py:61
  60.9 11.9 %collective-permute-start.10 = (f32[2,6,8,128]{3,2,1,0:T(8,128)S(1)}, f32[2,6,8,128]{3,2,1,0:T(8,128)S(1)}, u32[]{:S(2)}, u32[]{:S(2)}) collective-permute-start(f32[2,6,8,128]{3,2,1,0:T(8,128)S(1)} %pad_maximum_fusion.11), channel_id=1, source_target_pairs={{0,64},{16,80},{32,96},{48,112},{64,0},{80,16},{96,32},{112,48},{1... | collective-permute-start | bytes 147464 | tf_op jit(solution)/shard_map/ppermute | solution.py:61
  65.0 7.8 %collective-permute-start.11 = (f32[2,6,8,128]{3,2,1,0:T(8,128)S(1)}, f32[2,6,8,128]{3,2,1,0:T(8,128)S(1)}, u32[]{:S(2)}, u32[]{:S(2)}) collective-permute-start(f32[2,6,8,128]{3,2,1,0:T(8,128)S(1)} %pad_maximum_fusion.12), channel_id=1, source_target_pairs={{0,96},{16,112},{32,64},{48,80},{64,32},{80,48},{96,0},{112,16},{1... | collective-permute-start | bytes 147464 | tf_op jit(solution)/shard_map/ppermute | solution.py:61
  65.6 7.2 %collective-permute-start.12 = (f32[2,6,8,128]{3,2,1,0:T(8,128)S(1)}, f32[2,6,8,128]{3,2,1,0:T(8,128)S(1)}, u32[]{:S(2)}, u32[]{:S(2)}) collective-permute-start(f32[2,6,8,128]{3,2,1,0:T(8,128)S(1)} %pad_maximum_fusion.13), channel_id=1, source_target_pairs={{0,128},{16,144},{32,160},{48,176},{64,192},{80,208},{96,224},{112... | collective-permute-start | bytes 147464 | tf_op jit(solution)/shard_map/ppermute | solution.py:61
  67.2 5.7 %collective-permute-start.13 = (f32[2,6,8,128]{3,2,1,0:T(8,128)S(1)}, f32[2,6,8,128]{3,2,1,0:T(8,128)S(1)}, u32[]{:S(2)}, u32[]{:S(2)}) collective-permute-start(f32[2,6,8,128]{3,2,1,0:T(8,128)S(1)} %pad_maximum_fusion.14), channel_id=1, source_target_pairs={{0,160},{16,176},{32,128},{48,144},{64,224},{80,240},{96,192},{112... | collective-permute-start | bytes 147464 | tf_op jit(solution)/shard_map/ppermute | solution.py:61
  67.3 8.1 %collective-permute-start.14 = (f32[2,6,8,128]{3,2,1,0:T(8,128)S(1)}, f32[2,6,8,128]{3,2,1,0:T(8,128)S(1)}, u32[]{:S(2)}, u32[]{:S(2)}) collective-permute-start(f32[2,6,8,128]{3,2,1,0:T(8,128)S(1)} %pad_maximum_fusion.15), channel_id=1, source_target_pairs={{0,192},{16,208},{32,224},{48,240},{64,128},{80,144},{96,160},{112... | collective-permute-start | bytes 147464 | tf_op jit(solution)/shard_map/ppermute | solution.py:61
  72.8 6.2 %collective-permute-start.15 = (f32[2,6,8,128]{3,2,1,0:T(8,128)S(1)}, f32[2,6,8,128]{3,2,1,0:T(8,128)S(1)}, u32[]{:S(2)}, u32[]{:S(2)}) collective-permute-start(f32[2,6,8,128]{3,2,1,0:T(8,128)S(1)} %pad_maximum_fusion.16), channel_id=1, source_target_pairs={{0,224},{16,240},{32,192},{48,208},{64,160},{80,176},{96,128},{112... | collective-permute-start | bytes 147464 | tf_op jit(solution)/shard_map/ppermute | solution.py:61
  82.4 26.0 %all-to-all-start.2 = ((f32[16,7,8,128]{3,2,1,0:T(8,128)}), f32[16,7,8,128]{3,2,1,0:T(8,128)S(1)}, u32[]{:S(2)}, u32[]{:S(2)}) async-start(f32[16,7,8,128]{3,2,1,0:T(8,128)} %get-tuple-element.19), calls=%async_computation.2 | async-start | bytes 917504 | tf_op jit(solution)/shard_map/all_to_all | solution.py:56
  93.3 6.0 %collective-permute-start.17 = (f32[2,7,8,128]{3,2,1,0:T(8,128)S(1)}, f32[2,7,8,128]{3,2,1,0:T(8,128)S(1)}, u32[]{:S(2)}, u32[]{:S(2)}) collective-permute-start(f32[2,7,8,128]{3,2,1,0:T(8,128)S(1)} %pad_maximum_fusion.2), channel_id=1, source_target_pairs={{0,32},{16,48},{32,0},{48,16},{64,96},{80,112},{96,64},{112,80},{1... | collective-permute-start | bytes 172040 | tf_op jit(solution)/shard_map/ppermute | solution.py:61
  93.4 8.6 %collective-permute-start.18 = (f32[2,7,8,128]{3,2,1,0:T(8,128)S(1)}, f32[2,7,8,128]{3,2,1,0:T(8,128)S(1)}, u32[]{:S(2)}, u32[]{:S(2)}) collective-permute-start(f32[2,7,8,128]{3,2,1,0:T(8,128)S(1)} %pad_maximum_fusion.3), channel_id=1, source_target_pairs={{0,64},{16,80},{32,96},{48,112},{64,0},{80,16},{96,32},{112,48},{1... | collective-permute-start | bytes 172040 | tf_op jit(solution)/shard_map/ppermute | solution.py:61
  95.0 10.3 %collective-permute-start.19 = (f32[2,7,8,128]{3,2,1,0:T(8,128)S(1)}, f32[2,7,8,128]{3,2,1,0:T(8,128)S(1)}, u32[]{:S(2)}, u32[]{:S(2)}) collective-permute-start(f32[2,7,8,128]{3,2,1,0:T(8,128)S(1)} %pad_maximum_fusion.4), channel_id=1, source_target_pairs={{0,96},{16,112},{32,64},{48,80},{64,32},{80,48},{96,0},{112,16},{1... | collective-permute-start | bytes 172040 | tf_op jit(solution)/shard_map/ppermute | solution.py:61
  98.1 7.2 %collective-permute-start.20 = (f32[2,7,8,128]{3,2,1,0:T(8,128)S(1)}, f32[2,7,8,128]{3,2,1,0:T(8,128)S(1)}, u32[]{:S(2)}, u32[]{:S(2)}) collective-permute-start(f32[2,7,8,128]{3,2,1,0:T(8,128)S(1)} %pad_maximum_fusion.5), channel_id=1, source_target_pairs={{0,128},{16,144},{32,160},{48,176},{64,192},{80,208},{96,224},{112... | collective-permute-start | bytes 172040 | tf_op jit(solution)/shard_map/ppermute | solution.py:61
  99.3 6.1 %collective-permute-start.21 = (f32[2,7,8,128]{3,2,1,0:T(8,128)S(1)}, f32[2,7,8,128]{3,2,1,0:T(8,128)S(1)}, u32[]{:S(2)}, u32[]{:S(2)}) collective-permute-start(f32[2,7,8,128]{3,2,1,0:T(8,128)S(1)} %pad_maximum_fusion.6), channel_id=1, source_target_pairs={{0,160},{16,176},{32,128},{48,144},{64,224},{80,240},{96,192},{112... | collective-permute-start | bytes 172040 | tf_op jit(solution)/shard_map/ppermute | solution.py:61
  99.3 6.8 %collective-permute-start.22 = (f32[2,7,8,128]{3,2,1,0:T(8,128)S(1)}, f32[2,7,8,128]{3,2,1,0:T(8,128)S(1)}, u32[]{:S(2)}, u32[]{:S(2)}) collective-permute-start(f32[2,7,8,128]{3,2,1,0:T(8,128)S(1)} %pad_maximum_fusion.7), channel_id=1, source_target_pairs={{0,192},{16,208},{32,224},{48,240},{64,128},{80,144},{96,160},{112... | collective-permute-start | bytes 172040 | tf_op jit(solution)/shard_map/ppermute | solution.py:61
  102.1 6.3 %collective-permute-start.23 = (f32[2,7,8,128]{3,2,1,0:T(8,128)S(1)}, f32[2,7,8,128]{3,2,1,0:T(8,128)S(1)}, u32[]{:S(2)}, u32[]{:S(2)}) collective-permute-start(f32[2,7,8,128]{3,2,1,0:T(8,128)S(1)} %pad_maximum_fusion.8), channel_id=1, source_target_pairs={{0,224},{16,240},{32,192},{48,208},{64,160},{80,176},{96,128},{112... | collective-permute-start | bytes 172040 | tf_op jit(solution)/shard_map/ppermute | solution.py:61
  114.7 38.6 %all-to-all-start.3 = ((f32[16,128,128]{2,1,0:T(8,128)}), f32[16,128,128]{2,1,0:T(8,128)S(1)}, u32[]{:S(2)}, u32[]{:S(2)}) async-start(f32[16,128,128]{2,1,0:T(8,128)} %get-tuple-element.22), calls=%async_computation.3 | async-start | bytes 2097152 | tf_op jit(solution)/shard_map/all_to_all | solution.py:56
  124.8 10.1 %collective-permute-start.25 = (f32[128,128]{1,0:T(8,128)S(1)}, f32[128,128]{1,0:T(8,128)S(1)}, u32[]{:S(2)}, u32[]{:S(2)}) collective-permute-start(f32[128,128]{1,0:T(8,128)S(1)} %get-tuple-element.26), channel_id=1, source_target_pairs={{0,192},{16,208},{32,224},{48,240},{64,128},{80,144},{96,160},{112... | collective-permute-start | bytes 196616 | tf_op jit(solution)/shard_map/ppermute | solution.py:61
  127.4 11.0 %collective-permute-start.31 = (f32[128,128]{1,0:T(8,128)S(1)}, f32[128,128]{1,0:T(8,128)S(1)}, u32[]{:S(2)}, u32[]{:S(2)}) collective-permute-start(f32[128,128]{1,0:T(8,128)S(1)} %get-tuple-element.27), channel_id=1, source_target_pairs={{0,32},{16,48},{32,0},{48,16},{64,96},{80,112},{96,64},{112,80},{1... | collective-permute-start | bytes 196616 | tf_op jit(solution)/shard_map/ppermute | solution.py:61
  132.8 6.4 %collective-permute-start.30 = (f32[128,128]{1,0:T(8,128)S(1)}, f32[128,128]{1,0:T(8,128)S(1)}, u32[]{:S(2)}, u32[]{:S(2)}) collective-permute-start(f32[128,128]{1,0:T(8,128)S(1)} %get-tuple-element.28), channel_id=1, source_target_pairs={{0,96},{16,112},{32,64},{48,80},{64,32},{80,48},{96,0},{112,16},{1... | collective-permute-start | bytes 196616 | tf_op jit(solution)/shard_map/ppermute | solution.py:61
  132.8 6.4 %collective-permute-start.29 = (f32[128,128]{1,0:T(8,128)S(1)}, f32[128,128]{1,0:T(8,128)S(1)}, u32[]{:S(2)}, u32[]{:S(2)}) collective-permute-start(f32[128,128]{1,0:T(8,128)S(1)} %get-tuple-element.29), channel_id=1, source_target_pairs={{0,128},{16,144},{32,160},{48,176},{64,192},{80,208},{96,224},{112... | collective-permute-start | bytes 196616 | tf_op jit(solution)/shard_map/ppermute | solution.py:61
  132.8 6.4 %collective-permute-start.28 = (f32[128,128]{1,0:T(8,128)S(1)}, f32[128,128]{1,0:T(8,128)S(1)}, u32[]{:S(2)}, u32[]{:S(2)}) collective-permute-start(f32[128,128]{1,0:T(8,128)S(1)} %get-tuple-element.30), channel_id=1, source_target_pairs={{0,64},{16,80},{32,96},{48,112},{64,0},{80,16},{96,32},{112,48},{1... | collective-permute-start | bytes 196616 | tf_op jit(solution)/shard_map/ppermute | solution.py:61
  134.9 7.1 %collective-permute-start.27 = (f32[128,128]{1,0:T(8,128)S(1)}, f32[128,128]{1,0:T(8,128)S(1)}, u32[]{:S(2)}, u32[]{:S(2)}) collective-permute-start(f32[128,128]{1,0:T(8,128)S(1)} %get-tuple-element.31), channel_id=1, source_target_pairs={{0,160},{16,176},{32,128},{48,144},{64,224},{80,240},{96,192},{112... | collective-permute-start | bytes 196616 | tf_op jit(solution)/shard_map/ppermute | solution.py:61
  138.4 7.4 %collective-permute-start.26 = (f32[128,128]{1,0:T(8,128)S(1)}, f32[128,128]{1,0:T(8,128)S(1)}, u32[]{:S(2)}, u32[]{:S(2)}) collective-permute-start(f32[128,128]{1,0:T(8,128)S(1)} %get-tuple-element.32), channel_id=1, source_target_pairs={{0,224},{16,240},{32,192},{48,208},{64,160},{80,176},{96,128},{112... | collective-permute-start | bytes 196616 | tf_op jit(solution)/shard_map/ppermute | solution.py:61
  (10 other events, 93.1 us)
